TPU v7x, 256 devices: a whole 4x4x8 slice. The times are simulated.
256 devices in a mesh: dp: 16 (over z_hi, x, core), fsdp: 16 (over y, z_lo).
Axes of the slice: x: 4, y: 4, z: 8 (z_hi: 2, z_lo: 4; z = z_hi * 4 + z_lo), core: 2. Of those that a mesh axis runs over, the one named last changes fastest.
Arguments:
- token_ids: int32 [32768], P('dp'), may hold values from 0 to 30527, as said below
- embed_table: bfloat16 [30528, 768], P('fsdp'), may hold values from -16 to 16, as said below
- w_qkv: bfloat16 [768, 2304], P('fsdp'), may hold values from -2 to 2
- w_out: bfloat16 [768, 768], P('fsdp'), may hold values from -0.21875 to 0.21875
- ln_gain: float32 [768], replicated, may hold values from 0.5 to 1.5
- ln_bias: float32 [768], replicated, may hold values from -1 to 1
- centroids_t: bfloat16 [768, 32768], P('fsdp', 'dp'), may hold values from -24 to 24
- assignments: int32 [32768], replicated, may hold values from 0 to 32767, as said below
Outputs:
- token_loss: float32 [32768], P(('dp', 'fsdp'))
- new_centroids: float32 [32768, 768], P(('dp', 'fsdp'))
Inputs may be any that keep to these rules, and one draw needn't show every extreme that they name: `token_ids`: id 0 is padding; a passage may end in a run of padding. `embed_table`: token embeddings of order one. `assignments`: cluster sizes are skewed.
All inputs are finite; a program needn't handle non-finite values.
Results may differ from a plain program's by a relative error of at most 0.0055.
Values may be sent and summed in bfloat16 or wider, within the bound.
No kernel may reach another device: no remote copies, remote signals or barrier semaphores. Data moves between devices by JAX's collectives and lax.ppermute only.
A program may use at most 64 MiB of HBM per device.

v0:
```python
import jax
import jax.numpy as jnp
from jax import lax
from jax.experimental import pallas as pl
from jax.experimental.pallas import tpu as pltpu
from jax.sharding import Mesh
from jax.sharding import PartitionSpec as P

HEADS = 12
HEAD = 64
SEQ = 128
DP = ("zh", "x", "core")
FS = ("y", "zl")
ALL = DP + FS
LIST = 47
SLOTS = 39
BLOCK = SLOTS + 1
ROOM = 48
F32 = jnp.float32
BF16 = jnp.bfloat16


RING = ((0, 0, 2), (1, 0, 2), (2, 0, 1), (2, 1, 1), (3, 0, 2))


def iota(shape, dim):
    return lax.broadcasted_iota(jnp.int32, shape, dim)


def dot(a, b, dims=((1,), (0,))):
    return lax.dot_general(a, b, (dims, ((), ())), preferred_element_type=F32)


def ranked(present, groups):
    rows = present.shape[0]
    per = rows // groups
    upper = jnp.where(iota((128, 128), 0) < iota((128, 128), 1), 1.0, 0.0).astype(BF16)
    at, of = iota((rows, rows), 0), iota((rows, rows), 1)
    above = jnp.where((at // per == of // per) & (of < at), 1.0, 0.0).astype(BF16)
    ones = present.astype(BF16)
    return dot(ones, upper) + jnp.sum(dot(above, ones), axis=1, keepdims=True)


def tokens_of(ids_refs, dest):
    dests = ids_refs[0].shape[0] // 2
    return jnp.concatenate(
        [ref[pl.ds(z * dests + dest, 1), :] for ref in ids_refs for z in range(2)], axis=1
    )


def lists_kernel(info_ref, *refs):
    ids_refs, table_ref, rows_ref, present_ref, rank_ref, hits_ref = refs[0:4], *refs[4:]
    vocab = table_ref.shape[0]
    dests, tokens = rows_ref.shape[0], 8 * SEQ
    base = info_ref[0] * vocab
    first_slot = info_ref[1] * LIST
    high = 16

    def find(p, _):
        local = tokens_of(ids_refs, p) - base
        inside = (local >= 0) & (local < vocab)
        block = jnp.where((iota((high, tokens), 0) == (local >> 7)) & inside, 1.0, 0.0).astype(BF16)
        lane = jnp.where(iota((128, tokens), 0) == (local & 127), 1.0, 0.0).astype(BF16)
        seen = dot(block, lane, ((1,), (1,)))
        present_ref[pl.ds(pl.multiple_of(p * high, high), high), :] = jnp.where(seen > 0.5, 1.0, 0.0)
        return 0

    lax.fori_loop(0, dests, find, 0, unroll=2)
    present = present_ref[...]
    rank_ref[...] = jnp.where(present > 0.5, ranked(present, dests) - first_slot.astype(F32), -1.0)
    blocks = -(-vocab // 128)

    def choose(p, most):
        ranks = rank_ref[pl.ds(pl.multiple_of(p * high, high), high), :]
        slot = iota((ROOM, 128), 0)
        for h in range(blocks):
            chosen = (slot == ranks[h : h + 1, :].astype(jnp.int32)) & (slot < LIST)
            hits_ref[pl.ds(pl.multiple_of(p * ROOM, ROOM), ROOM), h * 128 : (h + 1) * 128] = jnp.where(
                chosen, 1.0, 0.0
            ).astype(BF16)
        return jnp.maximum(most, jnp.max(ranks))

    most = lax.fori_loop(0, dests, choose, jnp.float32(-1.0)) + first_slot.astype(F32)
    whole = vocab // 16 * 16
    rounds = jnp.floor(most * (1.0 / LIST) + 1e-3) + 1.0
    some = 4

    def fetch(i, _):
        hits = hits_ref[pl.ds(pl.multiple_of(i * some * ROOM, some * ROOM), some * ROOM), :]
        rows = dot(hits[:, 0:whole], table_ref[0:whole, :])
        if whole < vocab:
            tail = table_ref[whole:vocab, :].astype(F32)
            for k in range(vocab - whole):
                rows = rows + hits[:, whole + k : whole + k + 1].astype(F32) * tail[k : k + 1, :]
        rows = rows.reshape(some, ROOM, rows.shape[1])
        rows_ref[pl.ds(i * some, some)] = jnp.where(iota(rows.shape, 1) == LIST, rounds, rows).astype(BF16)
        return 0

    lax.fori_loop(0, dests // some, fetch, 0)


def listed_rows(info, ids, table):
    dests = ids[0].shape[0] // 2
    width = table.shape[1]
    return pl.pallas_call(
        lists_kernel,
        out_shape=jax.ShapeDtypeStruct((dests, ROOM, width), BF16),
        in_specs=[pl.BlockSpec(memory_space=pltpu.SMEM)]
        + [pl.BlockSpec(memory_space=pltpu.VMEM)] * (len(ids) + 1),
        out_specs=pl.BlockSpec(memory_space=pltpu.VMEM),
        scratch_shapes=[
            pltpu.VMEM((dests * 16, 128), F32),
            pltpu.VMEM((dests * 16, 128), F32),
            pltpu.VMEM((dests * ROOM, 16 * 128), BF16),
        ],
        compiler_params=pltpu.CompilerParams(vmem_limit_bytes=40 << 20),
    )(info, *ids, table)


def place_kernel(info_ref, *refs):
    ids_refs, out_ref = refs[0:4], refs[4]
    tokens = 8 * SEQ
    owners = out_ref.shape[1] // ROOM
    first_slot = info_ref[1] * LIST
    vocab = info_ref[2]
    row = tokens_of(ids_refs, info_ref[0])
    owner = jnp.zeros(row.shape, jnp.int32)
    for k in range(1, owners):
        owner = owner + jnp.where(row >= k * vocab, 1, 0)
    local = row - owner * vocab
    group = owner * 16 + (local >> 7)
    block = jnp.where(iota((owners * 16, tokens), 0) == group, 1.0, 0.0).astype(BF16)
    lane = jnp.where(iota((128, tokens), 0) == (local & 127), 1.0, 0.0).astype(BF16)
    present = jnp.where(dot(block, lane, ((1,), (1,))) > 0.5, 1.0, 0.0)
    rank = ranked(present, owners) - first_slot.astype(F32)
    rank = jnp.where((rank >= 0) & (rank < LIST), rank, 255.0).astype(BF16)
    owner = owner.astype(F32)
    low = (local & 127).astype(F32)
    for t in range(tokens // 128):
        cols = slice(t * 128, (t + 1) * 128)
        found = lax.dot_general(
            block[:, cols], rank, (((0,), (0,)), ((), ())), preferred_element_type=F32
        )
        down = jnp.broadcast_to(low[:, cols], (128, 128)).T
        slot = jnp.sum(jnp.where(iota((128, 128), 1).astype(F32) == down, found, 0.0), axis=1, keepdims=True)
        of = jnp.broadcast_to(owner[:, cols], (128, 128)).T[:, 0:1]
        place = jnp.where(slot < LIST, of * ROOM + slot, -1.0).astype(jnp.int32)
        out_ref[cols, :] = jnp.where(place == iota((128, owners * ROOM), 1), 1.0, 0.0).astype(BF16)


def placed_rows(info, ids, owners):
    return pl.pallas_call(
        place_kernel,
        out_shape=jax.ShapeDtypeStruct((8 * SEQ, owners * ROOM), BF16),
        in_specs=[pl.BlockSpec(memory_space=pltpu.SMEM)]
        + [pl.BlockSpec(memory_space=pltpu.VMEM)] * len(ids),
        out_specs=pl.BlockSpec(memory_space=pltpu.VMEM),
        compiler_params=pltpu.CompilerParams(vmem_limit_bytes=40 << 20),
    )(info, *ids)


def expand_kernel(places_ref, got_ref, out_ref, rounds_ref):
    owners, room, width = got_ref.shape
    got = got_ref[...].reshape(owners * room, width)

    def fill(i, _):
        rows = pl.ds(pl.multiple_of(i * 2 * SEQ, 2 * SEQ), 2 * SEQ)
        out_ref[rows, :] = dot(places_ref[rows, :], got).astype(BF16)
        return 0

    lax.fori_loop(0, out_ref.shape[0] // (2 * SEQ), fill, 0)
    most = jnp.max(got_ref[:, LIST, 0:128].astype(F32), axis=0, keepdims=True)
    rounds_ref[...] = jnp.broadcast_to(most, rounds_ref.shape).astype(jnp.int32)


def expanded(places, got):
    return pl.pallas_call(
        expand_kernel,
        out_shape=(
            jax.ShapeDtypeStruct((places.shape[0], got.shape[2]), BF16),
            jax.ShapeDtypeStruct((8, 128), jnp.int32),
        ),
        in_specs=[pl.BlockSpec(memory_space=pltpu.VMEM)] * 2,
        out_specs=(pl.BlockSpec(memory_space=pltpu.VMEM), pl.BlockSpec(memory_space=pltpu.VMEM)),
        compiler_params=pltpu.CompilerParams(vmem_limit_bytes=40 << 20),
    )(places, got)


def join_kernel(*refs):
    parts, out_ref, sems = refs[:-2], refs[-2], refs[-1]
    rows = parts[0].shape[0]
    put(parts, [out_ref.at[pl.ds(k * rows, rows), :] for k in range(len(parts))], sems)


def joined(parts):
    rows, cols = parts[0].shape
    return pl.pallas_call(
        join_kernel,
        out_shape=jax.ShapeDtypeStruct((len(parts) * rows, cols), parts[0].dtype),
        in_specs=[pl.BlockSpec(memory_space=pltpu.HBM)] * len(parts),
        out_specs=pl.BlockSpec(memory_space=pltpu.HBM),
        scratch_shapes=[pltpu.SemaphoreType.DMA((len(parts),))],
    )(*parts)


def put(sources, targets, sems):
    copies = [
        pltpu.make_async_copy(src, dst, sems.at[k])
        for k, (src, dst) in enumerate(zip(sources, targets, strict=True))
    ]
    for c in copies:
        c.start()
    for c in copies:
        c.wait()


def encode_kernel(info_ref, *refs):
    rings = refs[0:10]
    slab_ref, gain_ref, bias_ref, out_ref, w_ref, packed_ref, scores_ref, probs_ref, context_ref, sems = (
        refs[10:]
    )
    x_size = 4
    core, at_x = info_ref[0], info_ref[1]
    depth, part = w_ref.shape[1:]
    targets = []
    for core_at in (core, 1 - core):
        for back, first, count in RING:
            place = core_at * x_size + lax.rem(at_x - back + x_size, x_size)
            targets.append(w_ref.at[place, pl.ds(first * (depth // 2), count * (depth // 2)), :])
    put(rings, targets, sems)
    tokens, width = packed_ref.shape[0], slab_ref.shape[1]
    left = iota((SEQ, 2 * HEAD), 1) < HEAD
    zero = jnp.zeros((SEQ, 2 * HEAD), BF16)
    pairs = HEADS // 2
    passages = tokens // SEQ

    def stacked(values):
        return jnp.concatenate([jnp.where(left, values, zero), jnp.where(left, zero, values)], axis=0)

    def step(i, _):
        x = slab_ref[pl.ds(i * tokens, tokens), :]
        for j in range(6):
            packed_ref[:, j * part : (j + 1) * part] = dot(x, w_ref[j]).astype(BF16)
        for b in range(passages):
            rows = slice(b * SEQ, (b + 1) * SEQ)
            for pair in range(pairs):
                at = pair * 2 * HEAD
                q = packed_ref[rows, at : at + 2 * HEAD] * jnp.asarray(HEAD**-0.5, BF16)
                k = packed_ref[rows, width + at : width + at + 2 * HEAD]
                scores_ref[b * pairs + pair] = dot(q, stacked(k), ((1,), (1,)))
        for n in range(passages * pairs):
            for h in range(2):
                s = scores_ref[n, :, h * SEQ : (h + 1) * SEQ]
                e = jnp.exp(s - jnp.max(s, axis=1, keepdims=True))
                probs = e * (1.0 / jnp.sum(e, axis=1, keepdims=True))
                probs_ref[n, :, h * SEQ : (h + 1) * SEQ] = probs.astype(BF16)
        for b in range(passages):
            rows = slice(b * SEQ, (b + 1) * SEQ)
            for pair in range(pairs):
                at = pair * 2 * HEAD
                v = packed_ref[rows, 2 * width + at : 2 * width + at + 2 * HEAD]
                context_ref[rows, at : at + 2 * HEAD] = dot(
                    probs_ref[b * pairs + pair], stacked(v)
                ).astype(BF16)
        context = context_ref[...]
        half = width // 2
        mixed = [
            dot(context, w_ref[6 + k]) + x[:, k * half : (k + 1) * half].astype(F32) for k in range(2)
        ]
        mean = sum(jnp.sum(m, axis=1, keepdims=True) for m in mixed) * (1.0 / width)
        center = [m - mean for m in mixed]
        spread = sum(jnp.sum(c * c, axis=1, keepdims=True) for c in center) * (1.0 / width)
        scale = lax.rsqrt(spread + 1e-05)
        for k in range(2):
            cols = slice(k * half, (k + 1) * half)
            out_ref[pl.ds(i * tokens, tokens), cols] = (
                center[k] * scale * gain_ref[:, cols] + bias_ref[:, cols]
            ).astype(BF16)
        return 0

    lax.fori_loop(0, slab_ref.shape[0] // tokens, step, 0)


def encoded(info, rings, slab, gain, bias):
    part = rings[0].shape[1]
    tokens, width = 2 * SEQ, slab.shape[1]
    pairs = tokens // SEQ * HEADS // 2
    return pl.pallas_call(
        encode_kernel,
        out_shape=jax.ShapeDtypeStruct(slab.shape, BF16),
        in_specs=[pl.BlockSpec(memory_space=pltpu.SMEM)]
        + [pl.BlockSpec(memory_space=pltpu.HBM)] * len(rings)
        + [pl.BlockSpec(memory_space=pltpu.VMEM)] * 3,
        out_specs=pl.BlockSpec(memory_space=pltpu.VMEM),
        scratch_shapes=[
            pltpu.VMEM((8, width, part), BF16),
            pltpu.VMEM((tokens, 3 * width), BF16),
            pltpu.VMEM((pairs, SEQ, 2 * SEQ), F32),
            pltpu.VMEM((pairs, SEQ, 2 * SEQ), BF16),
            pltpu.VMEM((tokens, width), BF16),
            pltpu.SemaphoreType.DMA((len(rings),)),
        ],
        compiler_params=pltpu.CompilerParams(vmem_limit_bytes=40 << 20),
    )(info, *rings, slab, gain.reshape(1, width), bias.reshape(1, width))


def score_kernel(info_ref, mine_ref, other_ref, local_ref, *refs):
    parts = refs[0:5]
    out_ref, old_ref, cent_ref, sems = refs[5:]
    step = pl.program_id(0)
    half = pl.num_programs(0) // 2

    @pl.when(step == 0)
    def _():
        shard = parts[0].shape[0] // 4
        sources, targets = [], []
        for ref, (back, first, count) in zip(parts, RING, strict=True):
            owner = lax.rem(info_ref[0] - back + 4, 4) * 4
            for k in range(2 * count):
                start = (owner + lax.rem(info_ref[6] - 2 * first - k + 4, 4)) * shard
                sources.append(ref.at[pl.ds(k * shard, shard), :])
                targets.append(cent_ref.at[pl.ds(pl.multiple_of(start, shard), shard), :])
        put(sources, targets, sems)

    block = cent_ref.shape[1]
    span = 2 * SEQ
    for n in range(mine_ref.shape[0] // span):
        rows = slice(n * span, (n + 1) * span)
        s = dot(jnp.where(step < half, mine_ref[rows, :], other_ref[rows, :]), cent_ref[...])
        peak = jnp.max(s, axis=1, keepdims=True)
        mass = jnp.sum(jnp.exp(s - peak), axis=1, keepdims=True)
        local = jnp.concatenate(
            [jnp.broadcast_to(local_ref[2 * n + z], (SEQ, SEQ)).T[:, 0:1] for z in range(2)], axis=0
        )
        picked = jnp.sum(jnp.where(local == iota((span, block), 1), s, 0.0), axis=1, keepdims=True)
        both = jnp.where(iota((span, 128), 1) == 0, peak + jnp.log(mass), picked)
        x_size = info_ref[5]
        per_step = mine_ref.shape[0] // span
        back = lax.rem(step, half) * per_step + n
        x = lax.rem(info_ref[3] - back + x_size, x_size)
        core = jnp.where(step < half, info_ref[2], 1 - info_ref[2])
        for z in range(2):
            zh = info_ref[4] if z == 0 else 1 - info_ref[4]
            out_ref[zh * (2 * x_size) + x * 2 + core] = both[z * SEQ : (z + 1) * SEQ, :].T[0:8, :]

    @pl.when(step == pl.num_programs(0) - 1)
    def _():
        per = old_ref.shape[0]
        old = cent_ref[:, pl.ds(pl.multiple_of(info_ref[1] * per, per), per)]
        old_ref[...] = old.astype(F32).T


def scored(info, mine, other, local, parts):
    tokens, width = mine.shape
    block = parts[0].shape[1]
    step = 4 * SEQ
    per = step // SEQ
    half = tokens // step
    return pl.pallas_call(
        score_kernel,
        grid=(2 * half,),
        out_shape=(
            jax.ShapeDtypeStruct((2 * tokens // SEQ, 8, SEQ), F32),
            jax.ShapeDtypeStruct((SEQ, width), F32),
        ),
        in_specs=[
            pl.BlockSpec(memory_space=pltpu.SMEM),
            pl.BlockSpec((step, width), lambda i: (jnp.minimum(i, half - 1), 0)),
            pl.BlockSpec((step, width), lambda i: (jnp.maximum(i - half, 0), 0)),
            pl.BlockSpec((per, 1, SEQ), lambda i: (i, 0, 0)),
        ]
        + [pl.BlockSpec(memory_space=pltpu.HBM)] * len(parts),
        out_specs=(
            pl.BlockSpec((2 * tokens // SEQ, 8, SEQ), lambda i: (0, 0, 0)),
            pl.BlockSpec((SEQ, width), lambda i: (0, 0)),
        ),
        scratch_shapes=[
            pltpu.VMEM((width, block), BF16),
            pltpu.SemaphoreType.DMA((16,)),
        ],
        compiler_params=pltpu.CompilerParams(vmem_limit_bytes=48 << 20),
    )(info, mine, other, local.reshape(2 * tokens // SEQ, 1, SEQ), *parts)


def choose_kernel(info_ref, local_ref, out_ref, most_ref):
    tokens = local_ref.shape[1]
    per = 128
    dests = out_ref.shape[0] // ROOM
    first_slot = info_ref[1] * SLOTS
    local = local_ref[...]
    upper = iota((per, per), 0) < iota((per, per), 1)
    diagonal = iota((per, per), 0) == iota((per, per), 1)

    def group(g, most):
        match = jnp.where(local - g * per == iota((per, tokens), 0), 1.0, 0.0)
        hits = match.astype(BF16)
        present = jnp.broadcast_to(jnp.max(match, axis=1, keepdims=True), (per, per))
        rank = jnp.sum(jnp.where(upper, present, 0.0), axis=0, keepdims=True).astype(jnp.int32)
        here = jnp.sum(jnp.where(diagonal, present, 0.0), axis=0, keepdims=True)
        slot = iota((ROOM, per), 0)
        chosen = (slot < SLOTS) & (slot == rank - first_slot) & (here > 0.5)
        packing = jnp.where(chosen, 1.0, 0.0).astype(BF16)
        out_ref[pl.ds(pl.multiple_of(g * ROOM, ROOM), ROOM), :] = dot(packing, hits).astype(BF16)
        return jnp.maximum(most, jnp.sum(here, axis=1, keepdims=True))

    most = lax.fori_loop(0, dests, group, jnp.zeros((1, 1), F32), unroll=2)
    most_ref[...] = jnp.broadcast_to(most, most_ref.shape)


def choices(info, local, dests):
    return pl.pallas_call(
        choose_kernel,
        out_shape=(
            jax.ShapeDtypeStruct((dests * ROOM, local.shape[1]), BF16),
            jax.ShapeDtypeStruct((8, 128), F32),
        ),
        in_specs=[pl.BlockSpec(memory_space=pltpu.SMEM), pl.BlockSpec(memory_space=pltpu.VMEM)],
        out_specs=(pl.BlockSpec(memory_space=pltpu.VMEM), pl.BlockSpec(memory_space=pltpu.VMEM)),
        compiler_params=pltpu.CompilerParams(vmem_limit_bytes=40 << 20),
    )(info, local)


def pack_kernel(hits_ref, most_ref, mine_ref, other_ref, out_ref):
    dests, _, width = out_ref.shape
    half = mine_ref.shape[0]
    some = dests // 2

    def pack(i, _):
        hits = hits_ref[pl.ds(pl.multiple_of(i * some * ROOM, some * ROOM), some * ROOM), :]
        sums = dot(hits[:, 0:half], mine_ref[...]) + dot(hits[:, half:], other_ref[...])
        sums = sums.reshape(some, ROOM, width)[:, 0:BLOCK, :]
        last = iota(sums.shape, 1) == SLOTS
        out_ref[pl.ds(i * some, some)] = jnp.where(
            last, most_ref[0:1, 0:1].reshape(1, 1, 1), sums
        ).astype(BF16)
        return 0

    lax.fori_loop(0, 2, pack, 0)


def packed_sums(chosen, mine, other):
    hits, most = chosen
    width = mine.shape[1]
    return pl.pallas_call(
        pack_kernel,
        out_shape=jax.ShapeDtypeStruct((hits.shape[0] // ROOM, BLOCK, width), BF16),
        in_specs=[pl.BlockSpec(memory_space=pltpu.VMEM)] * 4,
        out_specs=pl.BlockSpec(memory_space=pltpu.VMEM),
        compiler_params=pltpu.CompilerParams(vmem_limit_bytes=40 << 20),
    )(hits, most, mine, other)


def count_kernel(info_ref, assign_ref, out_ref):
    dp, slabs, _ = assign_ref.shape
    targets = iota((128, SEQ), 0) + info_ref[0]
    lane = iota(out_ref.shape, 1)

    def slab(f, out):
        acc = jnp.zeros((128, SEQ), F32)
        for d in range(dp):
            acc = acc + jnp.where(assign_ref[d, pl.ds(f, 1), :] == targets, 1.0, 0.0)
        return jnp.where(lane == f, jnp.sum(acc, axis=1, keepdims=True), out)

    out_ref[...] = lax.fori_loop(0, slabs, slab, jnp.zeros(out_ref.shape, F32))


def counted(info, assign):
    return pl.pallas_call(
        count_kernel,
        out_shape=jax.ShapeDtypeStruct((128, 128), F32),
        in_specs=[pl.BlockSpec(memory_space=pltpu.SMEM), pl.BlockSpec(memory_space=pltpu.VMEM)],
        out_specs=pl.BlockSpec(memory_space=pltpu.VMEM),
    )(info, assign)


def unpack_kernel(info_ref, counts_ref, got_ref, out_ref, most_ref):
    slabs, _, width = got_ref.shape
    counts = counts_ref[...]
    present = jnp.where(counts > 0.5, 1.0, 0.0).astype(BF16)
    lower = jnp.where(iota((128, 128), 1) < iota((128, 128), 0), 1.0, 0.0).astype(BF16)
    rank = dot(lower, present).astype(jnp.int32) - info_ref[1] * SLOTS
    slot = iota((128, BLOCK), 1)
    parts = []
    for f in range(slabs):
        chosen = (slot == rank[:, f : f + 1]) & (slot < SLOTS) & (counts[:, f : f + 1] > 0.5)
        parts.append(jnp.where(chosen, 1.0, 0.0))
    hits = jnp.concatenate(parts, axis=1).astype(BF16)
    out_ref[...] = dot(hits, got_ref[...].reshape(slabs * BLOCK, width))
    most = jnp.max(got_ref[:, SLOTS, 0:128].astype(F32), axis=0, keepdims=True)
    most_ref[...] = jnp.broadcast_to(most, most_ref.shape).astype(jnp.int32)


def unpacked_sums(info, counts, got):
    return pl.pallas_call(
        unpack_kernel,
        out_shape=(
            jax.ShapeDtypeStruct((128, got.shape[2]), F32),
            jax.ShapeDtypeStruct((8, 128), jnp.int32),
        ),
        in_specs=[pl.BlockSpec(memory_space=pltpu.SMEM)]
        + [pl.BlockSpec(memory_space=pltpu.VMEM)] * 2,
        out_specs=(pl.BlockSpec(memory_space=pltpu.VMEM), pl.BlockSpec(memory_space=pltpu.VMEM)),
    )(info, counts, got)


def exchanged(blocks, axis):
    return lax.all_to_all(blocks, axis, 0, 0, tiled=True)


def gathered(shard, axis):
    devices = lax.axis_size(axis)
    return exchanged(jnp.broadcast_to(shard[None], (devices,) + shard.shape), axis)


def swapped(shard, axis):
    return lax.ppermute(shard, axis, [(0, 1), (1, 0)])


def turned(shard, axis, by):
    devices = lax.axis_size(axis)
    return lax.ppermute(shard, axis, [(i, (i + by) % devices) for i in range(devices)])


def neighbours(block, axis):
    return turned(block, axis, 1), turned(block, axis, lax.axis_size(axis) - 1)


def far_halves(back, ahead, axis):
    half = back.shape[0] // 2
    return turned(back[:half], axis, 1), turned(ahead[half:], axis, lax.axis_size(axis) - 1)


def backwards(values, here):
    for dim, at in enumerate(here):
        size = values.shape[dim]
        values = jnp.take(values, (at - jnp.arange(size)) % size, axis=dim)
    return values


def shards(token_ids, embed_table, w_qkv, w_out, ln_gain, ln_bias, centroids_t, assignments):
    core = lax.axis_index("core")
    dp_rank = lax.axis_index(DP)
    fs_rank = lax.axis_index(FS)
    fs_size = lax.axis_size(FS)
    dp_size = lax.axis_size(DP)
    x_size = lax.axis_size("x")
    vocab, width = embed_table.shape
    zero = jnp.int32(0)
    ids = token_ids.reshape(fs_size, SEQ)

    at_x = lax.axis_index("x")

    def info_of(*values):
        return jnp.stack([jnp.asarray(v, jnp.int32) for v in values])

    by_dev = assignments.reshape(2, x_size, 2, fs_size, SEQ)
    of_slab = lax.dynamic_index_in_dim(by_dev, fs_rank, 3, keepdims=False)
    of_slab = jnp.transpose(of_slab, (2, 1, 0, 3))
    here = (core, at_x, lax.axis_index("zh"))
    of_slab = backwards(of_slab, here)
    block = centroids_t.shape[1]
    local = of_slab.reshape(1, -1) - dp_rank * block
    chosen = choices(info_of(zero, zero), local, fs_size)
    counts = counted(
        info_of(dp_rank * block + fs_rank * (block // fs_size)),
        assignments.reshape(dp_size, fs_size, SEQ),
    )

    part = (w_qkv.shape[1] + w_out.shape[1]) // (2 * x_size)
    both = jnp.concatenate([w_qkv, w_out], axis=1)
    piece = lax.dynamic_slice_in_dim(both, (core * x_size + at_x) * part, part, 1)
    column = gathered(piece, FS).reshape(width, part)

    two = jnp.concatenate([ids, swapped(ids, "zh")], axis=0)
    ids = [two] + [turned(two, "x", k) for k in range(1, x_size)]

    sent = listed_rows(info_of(fs_rank, zero), ids, embed_table)
    sent, column, local, shard = lax.optimization_barrier((sent, column, local, centroids_t))
    w_back, w_ahead = neighbours(column, "x")
    near = joined([shard] + [turned(shard, "zl", k) for k in range(1, 4)])
    places = placed_rows(info_of(fs_rank, zero, vocab), ids, fs_size)
    w_back, w_ahead, chosen, places = lax.optimization_barrier((w_back, w_ahead, chosen, places))
    rings = [column, w_back, *far_halves(w_back, w_ahead, "x"), w_ahead]
    rings += [swapped(w, "core") for w in rings]
    got = exchanged(sent, FS)
    got, near, *rings = lax.optimization_barrier((got, near, *rings))
    slab, rounds = expanded(places, got)

    def more_rows(state):
        turn, acc = state
        again = exchanged(listed_rows(info_of(fs_rank, turn), ids, embed_table), FS)
        extra, _ = expanded(placed_rows(info_of(fs_rank, turn, vocab), ids, fs_size), again)
        return turn + 1, acc + extra

    rounds = rounds[0, 0]
    _, slab = lax.while_loop(lambda state: state[0] < rounds, more_rows, (jnp.int32(1), slab))

    back, ahead = neighbours(near, "y")

    mine = encoded(info_of(core, at_x), rings, slab, ln_gain, ln_bias)
    mine, back, ahead = lax.optimization_barrier((mine, back, ahead))
    far_low, far_high = far_halves(back, ahead, "y")
    other = swapped(mine, "core")

    def one_turn(turn):
        info = info_of(zero, turn)
        got = exchanged(packed_sums(choices(info, local, fs_size), mine, other), FS)
        return unpacked_sums(info, counts, got)[0]

    packed = packed_sums(chosen, mine, other)
    packed, mine, other, far_low, far_high = lax.optimization_barrier(
        (packed, mine, other, far_low, far_high)
    )
    got = exchanged(packed, FS)

    stats, previous = scored(
        info_of(lax.axis_index("y"), fs_rank, *here, x_size, lax.axis_index("zl")),
        mine,
        other,
        local,
        [near, back, far_low, far_high, ahead],
    )
    stats, got = lax.optimization_barrier((stats, got))
    sums, widest = unpacked_sums(info_of(zero, zero), counts, got)
    widest = widest[0, 0]
    _, sums = lax.while_loop(
        lambda state: state[0] * SLOTS < widest,
        lambda state: (state[0] + 1, state[1] + one_turn(state[0])),
        (jnp.int32(1), sums),
    )

    home = exchanged(stats, DP)
    lse = home[:, 0, :]
    peak = jnp.max(lse, axis=0)
    token_loss = (
        jnp.log(jnp.sum(jnp.exp(lse - peak[None, :]), axis=0)) + peak - jnp.sum(home[:, 1, :], axis=0)
    )

    total = jnp.sum(counts[:, 0:fs_size], axis=1, keepdims=True)
    new_centroids = jnp.where(total > 0, sums / jnp.maximum(total, 1.0), previous)
    return token_loss, new_centroids


def solution(mesh):
    finer = Mesh(mesh.devices.reshape(2, 4, 2, 4, 4), ALL)
    placed = (P(DP), P(FS, None), P(FS, None), P(FS, None), P(), P(), P(FS, DP), P())
    return jax.shard_map(
        shards, mesh=finer, in_specs=placed, out_specs=(P(ALL), P(ALL, None)), check_vma=False
    )
```

profile of v0, /device:TPU:1, one launch (start us, length us, event | category | flops | bytes accessed | tf_op | source)
XLA Modules:
  0.0 209.6 jit_solution(968778865527157051)
XLA Ops:
  0.6 7.8 %collective-permute-start = (s32[16,128]{1,0:T(8,128)}, s32[16,128]{1,0:T(8,128)S(1)}, u32[]{:S(2)}, u32[]{:S(2)}) collective-permute-start(s32[16,128]{1,0:T(8,128)} %bitcast.51), channel_id=1, source_target_pairs={{0,128},{128,0},{1,129},{129,1},{2,130},{130,2},{3,131},{131,3},{4... | collective-permute-start | bytes 24584 | tf_op jit(solution)/shard_map/ppermute | solution.py:516
  8.5 0.9 constant_dynamic-slice_fusion
  9.4 0.6 gather_fusion
  10.0 0.8 fusion
  10.8 0.9 broadcast_in_dim.42
  11.7 5.7 %all-to-all-start.2 = ((bf16[16,48,384]{2,1,0:T(8,128)(2,1)}), bf16[16,48,384]{2,1,0:T(8,128)(2,1)S(1)}, u32[]{:S(2)}, u32[]{:S(2)}) async-start(bf16[16,48,384]{2,1,0:T(8,128)(2,1)} %broadcast_in_dim.42), calls=%async_computation.2 | async-start | bytes 1179648 | tf_op jit(solution)/shard_map/all_to_all | solution.py:507
  17.4 0.6 gather_fusion.1
  18.0 0.1 select_bitcast_fusion
  18.1 0.6 gather_fusion.2
  18.7 0.1 subtract_bitcast_fusion
  18.8 1.3 collective-permute-start.1
  20.1 2.5 %collective-permute-start.2 = (s32[32,128]{1,0:T(8,128)S(1)}, s32[32,128]{1,0:T(8,128)S(1)}, u32[]{:S(2)}, u32[]{:S(2)}) collective-permute-start(s32[32,128]{1,0:T(8,128)S(1)} %pad_add_fusion.3.refs_0_), channel_id=1, source_target_pairs={{0,64},{32,96},{64,0},{96,32},{1,65},{33,97},{65,1},{97,33},{2,66}... | collective-permute-start | bytes 49160 | tf_op jit(solution)/shard_map/ppermute | solution.py:521
  22.5 1.2 collective-permute-start.3
  23.8 0.7 collective-permute-done.2.refs_2_
  24.4 1.0 collective-permute-done.3.refs_3_
  25.5 10.5 %shard_map.95 = bf16[16,48,768]{2,1,0:T(8,128)(2,1)} custom-call(s32[2]{0:T(128)S(1)} %pad_add_fusion.4.info_ref, s32[32,128]{1,0:T(8,128)S(1)} %pad_add_fusion.3.refs_0_, s32[32,128]{1,0:T(8,128)S(1)} %collective-permute-done.1.refs_1_, s32[32,128]{1,0:T(8,128)S(1)} %collective-permute-done.2.refs_2_, s32[32,128]{1,0:T(8,128)S(1)} %collective-permute-done.3.refs_3_, ...), custom_call_target="tpu_custom_call" | custom-call | tf_op jit(solution)/shard_map/pallas_call | solution.py:105
  36.0 6.9 %all-to-all-start.3 = ((bf16[16,48,768]{2,1,0:T(8,128)(2,1)}), bf16[16,48,768]{2,1,0:T(8,128)(2,1)S(1)}, u32[]{:S(2)}, u32[]{:S(2)}) async-start(bf16[16,48,768]{2,1,0:T(8,128)(2,1)} %shard_map.95), calls=%async_computation.3 | async-start | bytes 2359296 | tf_op jit(solution)/shard_map/all_to_all | solution.py:507
  42.9 0.3 collective-permute-start.4
  43.2 2.4 %collective-permute-start.5 = (bf16[768,384]{1,0:T(8,128)(2,1)S(1)}, bf16[768,384]{1,0:T(8,128)(2,1)}, u32[]{:S(2)}, u32[]{:S(2)}) collective-permute-start(bf16[768,384]{1,0:T(8,128)(2,1)S(1)} %bitcast.41), channel_id=1, source_target_pairs={{0,96},{32,0},{64,32},{96,64},{1,97},{33,1},{65,33},{97,65},{2,98}... | collective-permute-start | bytes 1769480 | tf_op jit(solution)/shard_map/ppermute | solution.py:521
  45.6 1.4 collective-permute-start.6
  47.0 2.1 collective-permute-start.7
  49.1 1.2 collective-permute-start.8
  50.2 6.2 %shard_map.96 = (bf16[768,2048]{1,0:T(8,128)(2,1)S(1)}, f32[8,128]{1,0:T(8,128)S(1)}) custom-call(s32[2]{0:T(128)S(1)} %broadcast.308.info_ref, s32[1,2048]{1,0:T(1,128)S(1)} %bitcast.44), custom_call_target="tpu_custom_call" | custom-call | tf_op jit(solution)/shard_map/pallas_call | solution.py:411
  56.4 1.6 copy-done.1
  58.1 2.1 shard_map.97.places_ref
  60.2 5.0 %collective-permute-start.11 = (bf16[768,384]{1,0:T(8,128)(2,1)S(1)}, bf16[768,384]{1,0:T(8,128)(2,1)}, u32[]{:S(2)}, u32[]{:S(2)}) collective-permute-start(bf16[768,384]{1,0:T(8,128)(2,1)S(1)} %bitcast.42), channel_id=1, source_target_pairs={{0,16},{16,0},{1,17},{17,1},{2,18},{18,2},{3,19},{19,3},{4,20},{20... | collective-permute-start | bytes 1769480 | tf_op jit(solution)/shard_map/ppermute | solution.py:516
  65.2 1.0 slice.27
  66.2 0.1 collective-permute-start.9
  66.3 1.0 slice.28
  67.3 2.9 %collective-permute-start.10 = (bf16[384,384]{1,0:T(8,128)(2,1)S(1)}, bf16[384,384]{1,0:T(8,128)(2,1)}, u32[]{:S(2)}, u32[]{:S(2)}) collective-permute-start(bf16[384,384]{1,0:T(8,128)(2,1)S(1)} %slice.28), channel_id=1, source_target_pairs={{0,96},{32,0},{64,32},{96,64},{1,97},{33,1},{65,33},{97,65},{2,98}... | collective-permute-start | bytes 884744 | tf_op jit(solution)/shard_map/ppermute | solution.py:521
  70.2 13.2 %collective-permute-done.7.refs_2_ = bf16[48,2048]{1,0:T(8,128)(2,1)S(1)} collective-permute-done((bf16[48,2048]{1,0:T(8,128)(2,1)}, bf16[48,2048]{1,0:T(8,128)(2,1)S(1)}, u32[]{:S(2)}, u32[]{:S(2)}) %collective-permute-start.7) | collective-permute-done | bytes 196640 | tf_op jit(solution)/shard_map/ppermute | solution.py:521
  83.5 2.5 %collective-permute-start.12 = (bf16[768,384]{1,0:T(8,128)(2,1)}, bf16[768,384]{1,0:T(8,128)(2,1)}, u32[]{:S(2)}, u32[]{:S(2)}) collective-permute-start(bf16[768,384]{1,0:T(8,128)(2,1)} %collective-permute-done.4.refs_1_), channel_id=1, source_target_pairs={{0,16},{16,0},{1,17},{17,1},{2,18},{18,2},{3,19},{19,3},{4,20},{20... | collective-permute-start | bytes 1769480 | tf_op jit(solution)/shard_map/ppermute | solution.py:516
  86.0 0.1 collective-permute-start.15
  86.1 0.4 collective-permute-start.13
  86.5 0.2 copy-done.13
  86.8 0.1 pad_add_fusion.6.info_ref
  86.8 25.0 %shard_map.98.refs_0_ = bf16[192,2048]{1,0:T(8,128)(2,1)} custom-call(bf16[48,2048]{1,0:T(8,128)(2,1)} %refs_0_, bf16[48,2048]{1,0:T(8,128)(2,1)} %copy-done.11, bf16[48,2048]{1,0:T(8,128)(2,1)} %copy-done.12, bf16[48,2048]{1,0:T(8,128)(2,1)} %copy-done.13), custom_call_target="tpu_custom_call" | custom-call | tf_op jit(solution)/shard_map/pallas_call | solution.py:197
  111.9 1.3 collective-permute-start.16
  113.1 1.5 collective-permute-start.17
  114.6 3.2 %shard_map.99 = (bf16[1024,768]{1,0:T(8,128)(2,1)}, s32[8,128]{1,0:T(8,128)S(1)}) custom-call(bf16[1024,768]{1,0:T(8,128)(2,1)S(1)} %shard_map.97.places_ref, bf16[16,48,768]{2,1,0:T(8,128)(2,1)S(1)} %all-to-all-done.3.got_ref), custom_call_target="tpu_custom_call" | custom-call | tf_op jit(solution)/shard_map/pallas_call | solution.py:177
  117.8 0.5 slice.29
  118.3 0.6 while.20
  118.9 16.7 %shard_map.100.mine_ref = bf16[1024,768]{1,0:T(8,128)(2,1)S(1)} custom-call(s32[2]{0:T(128)S(1)} %pad_add_fusion.6.info_ref, bf16[768,384]{1,0:T(8,128)(2,1)S(1)} %bitcast.43, bf16[768,384]{1,0:T(8,128)(2,1)} %collective-permute-done.4.refs_1_, bf16[384,384]{1,0:T(8,128)(2,1)} %collective-permute-done.9.refs_2_, ...), custom_call_target="tpu_custom_call" | custom-call | tf_op jit(solution)/shard_map/pallas_call | solution.py:288
  135.6 1.3 collective-permute-start.18
  136.9 1.0 slice.30
  137.9 0.1 collective-permute-start.19
  138.0 1.0 slice.31
  139.1 2.7 %collective-permute-start.20 = (bf16[96,2048]{1,0:T(8,128)(2,1)S(1)}, bf16[96,2048]{1,0:T(8,128)(2,1)S(1)}, u32[]{:S(2)}, u32[]{:S(2)}) collective-permute-start(bf16[96,2048]{1,0:T(8,128)(2,1)S(1)} %slice.31), channel_id=1, source_target_pairs={{0,12},{4,0},{8,4},{12,8},{1,13},{5,1},{9,5},{13,9},{2,14},{6,2},{... | collective-permute-start | bytes 1179656 | tf_op jit(solution)/shard_map/ppermute | solution.py:521
  141.8 3.7 %shard_map.101 = bf16[16,40,768]{2,1,0:T(8,128)(2,1)} custom-call(bf16[768,2048]{1,0:T(8,128)(2,1)S(1)} %copy-done.2, f32[8,128]{1,0:T(8,128)S(1)} %get-tuple-element.135.most_ref, bf16[1024,768]{1,0:T(8,128)(2,1)S(1)} %shard_map.100.mine_ref, bf16[1024,768]{1,0:T(8,128)(2,1)S(1)} %collective-permute-done.18.other_ref), custom_call_target="tpu_custom_call" | custom-call | tf_op jit(solution)/shard_map/pallas_call | solution.py:444
  145.6 4.2 %collective-permute-done.19.refs_2_ = bf16[96,2048]{1,0:T(8,128)(2,1)S(1)} collective-permute-done((bf16[96,2048]{1,0:T(8,128)(2,1)S(1)}, bf16[96,2048]{1,0:T(8,128)(2,1)S(1)}, u32[]{:S(2)}, u32[]{:S(2)}) %collective-permute-start.19) | collective-permute-done | bytes 393248 | tf_op jit(solution)/shard_map/ppermute | solution.py:521
  149.8 10.6 %all-to-all-start.4 = ((bf16[16,40,768]{2,1,0:T(8,128)(2,1)}), bf16[16,40,768]{2,1,0:T(8,128)(2,1)S(1)}, u32[]{:S(2)}, u32[]{:S(2)}) async-start(bf16[16,40,768]{2,1,0:T(8,128)(2,1)} %shard_map.101), calls=%async_computation.4 | async-start | bytes 1966080 | tf_op jit(solution)/shard_map/all_to_all | solution.py:507
  160.4 3.9 %shard_map.103.counts_ref = f32[128,128]{1,0:T(8,128)S(1)} custom-call(s32[1]{0:T(128)} %bitcast.23.info_ref, s32[16,16,128]{2,1,0:T(8,128)} %bitcast.48), custom_call_target="tpu_custom_call" | custom-call | tf_op jit(solution)/shard_map/pallas_call | solution.py:468
  164.2 0.1 stack.63.info_ref
  164.3 0.1 slice_reduce_fusion
  164.5 16.4 %shard_map.102 = (f32[16,8,128]{2,1,0:T(8,128)}, f32[128,768]{1,0:T(8,128)S(1)}) custom-call(s32[7]{0:T(128)S(1)} %stack.63.info_ref, bf16[1024,768]{1,0:T(8,128)(2,1)} %copy-done.5, bf16[1024,768]{1,0:T(8,128)(2,1)} %copy-done.7, s32[16,1,128]{2,1,0:T(1,128)S(1)} %bitcast.45, bf16[192,2048]{1,0:T(8,128)(2,1)S(1)} %copy-done, ...), custom_call_target="tpu_custom_call" | custom-call | tf_op jit(solution)/shard_map/pallas_call | solution.py:359
  180.8 5.1 %all-to-all-done.4.got_ref = bf16[16,40,768]{2,1,0:T(8,128)(2,1)S(1)} async-done(((bf16[16,40,768]{2,1,0:T(8,128)(2,1)}), bf16[16,40,768]{2,1,0:T(8,128)(2,1)S(1)}, u32[]{:S(2)}, u32[]{:S(2)}) %all-to-all-start.4) | async-done | bytes 983072 | tf_op jit(solution)/shard_map/all_to_all | solution.py:507
  185.9 0.9 copy-done.10
  186.8 2.8 %shard_map.104 = (f32[128,768]{1,0:T(8,128)S(1)}, s32[8,128]{1,0:T(8,128)}) custom-call(s32[2]{0:T(128)} %copy-done.4, f32[128,128]{1,0:T(8,128)S(1)} %shard_map.103.counts_ref, bf16[16,40,768]{2,1,0:T(8,128)(2,1)} %copy-done.10), custom_call_target="tpu_custom_call" | custom-call | tf_op jit(solution)/shard_map/pallas_call | solution.py:494
  189.6 1.2 slice.35
  190.8 0.7 while.21
  191.5 7.8 %all-to-all-start.5 = ((f32[16,8,128]{2,1,0:T(8,128)}), f32[16,8,128]{2,1,0:T(8,128)S(1)}, u32[]{:S(2)}, u32[]{:S(2)}) async-start(f32[16,8,128]{2,1,0:T(8,128)} %get-tuple-element.166), calls=%async_computation.5 | async-start | bytes 131072 | tf_op jit(solution)/shard_map/all_to_all | solution.py:507
  199.3 0.9 divide_select_fusion
  200.1 8.9 %all-to-all-done.5 = f32[16,8,128]{2,1,0:T(8,128)S(1)} async-done(((f32[16,8,128]{2,1,0:T(8,128)}), f32[16,8,128]{2,1,0:T(8,128)S(1)}, u32[]{:S(2)}, u32[]{:S(2)}) %all-to-all-start.5) | async-done | bytes 65568 | tf_op jit(solution)/shard_map/all_to_all | solution.py:507
  209.0 0.5 add_subtract_fusion
  (65 shorter events, 0.6 us)
Async XLA Ops:
  0.6 18.1 %copy-start.14 = (s32[2048]{0:T(1024)S(1)}, s32[2048]{0:T(1024)}, u32[]{:S(2)}) copy-start(s32[2048]{0:T(1024)} %param.12) | copy-start | bytes 24580
  0.6 18.1 %collective-permute-start = (s32[16,128]{1,0:T(8,128)}, s32[16,128]{1,0:T(8,128)S(1)}, u32[]{:S(2)}, u32[]{:S(2)}) collective-permute-start(s32[16,128]{1,0:T(8,128)} %bitcast.51), channel_id=1, source_target_pairs={{0,128},{128,0},{1,129},{129,1},{2,130},{130,2},{3,131},{131,3},{4... | collective-permute-start | bytes 24584 | tf_op jit(solution)/shard_map/ppermute | solution.py:516
  11.7 24.2 %all-to-all-start.2 = ((bf16[16,48,384]{2,1,0:T(8,128)(2,1)}), bf16[16,48,384]{2,1,0:T(8,128)(2,1)S(1)}, u32[]{:S(2)}, u32[]{:S(2)}) async-start(bf16[16,48,384]{2,1,0:T(8,128)(2,1)} %broadcast_in_dim.42), calls=%async_computation.2 | async-start | bytes 1179648 | tf_op jit(solution)/shard_map/all_to_all | solution.py:507
  18.8 5.0 %collective-permute-start.1 = (s32[32,128]{1,0:T(8,128)S(1)}, s32[32,128]{1,0:T(8,128)S(1)}, u32[]{:S(2)}, u32[]{:S(2)}) collective-permute-start(s32[32,128]{1,0:T(8,128)S(1)} %pad_add_fusion.3.refs_0_), channel_id=1, source_target_pairs={{0,32},{32,64},{64,96},{96,0},{1,33},{33,65},{65,97},{97,1},{2,34}... | collective-permute-start | bytes 49160 | tf_op jit(solution)/shard_map/ppermute | solution.py:521
  20.1 4.4 %collective-permute-start.2 = (s32[32,128]{1,0:T(8,128)S(1)}, s32[32,128]{1,0:T(8,128)S(1)}, u32[]{:S(2)}, u32[]{:S(2)}) collective-permute-start(s32[32,128]{1,0:T(8,128)S(1)} %pad_add_fusion.3.refs_0_), channel_id=1, source_target_pairs={{0,64},{32,96},{64,0},{96,32},{1,65},{33,97},{65,1},{97,33},{2,66}... | collective-permute-start | bytes 49160 | tf_op jit(solution)/shard_map/ppermute | solution.py:521
  22.5 3.0 %collective-permute-start.3 = (s32[32,128]{1,0:T(8,128)S(1)}, s32[32,128]{1,0:T(8,128)S(1)}, u32[]{:S(2)}, u32[]{:S(2)}) collective-permute-start(s32[32,128]{1,0:T(8,128)S(1)} %pad_add_fusion.3.refs_0_), channel_id=1, source_target_pairs={{0,96},{32,0},{64,32},{96,64},{1,97},{33,1},{65,33},{97,65},{2,98}... | collective-permute-start | bytes 49160 | tf_op jit(solution)/shard_map/ppermute | solution.py:521
  36.0 75.9 %all-to-all-start.3 = ((bf16[16,48,768]{2,1,0:T(8,128)(2,1)}), bf16[16,48,768]{2,1,0:T(8,128)(2,1)S(1)}, u32[]{:S(2)}, u32[]{:S(2)}) async-start(bf16[16,48,768]{2,1,0:T(8,128)(2,1)} %shard_map.95), calls=%async_computation.3 | async-start | bytes 2359296 | tf_op jit(solution)/shard_map/all_to_all | solution.py:507
  42.8 43.9 %copy-start.15 = (f32[768]{0:T(1024)S(1)}, f32[768]{0:T(1024)}, u32[]{:S(2)}) copy-start(f32[768]{0:T(1024)} %param.16) | copy-start | bytes 9220
  42.8 43.9 %copy-start.16 = (f32[768]{0:T(1024)S(1)}, f32[768]{0:T(1024)}, u32[]{:S(2)}) copy-start(f32[768]{0:T(1024)} %param.17) | copy-start | bytes 9220
  42.9 17.3 %collective-permute-start.4 = (bf16[768,384]{1,0:T(8,128)(2,1)S(1)}, bf16[768,384]{1,0:T(8,128)(2,1)}, u32[]{:S(2)}, u32[]{:S(2)}) collective-permute-start(bf16[768,384]{1,0:T(8,128)(2,1)S(1)} %bitcast.40), channel_id=1, source_target_pairs={{0,32},{32,64},{64,96},{96,0},{1,33},{33,65},{65,97},{97,1},{2,34}... | collective-permute-start | bytes 1769480 | tf_op jit(solution)/shard_map/ppermute | solution.py:521
  43.2 22.0 %collective-permute-start.5 = (bf16[768,384]{1,0:T(8,128)(2,1)S(1)}, bf16[768,384]{1,0:T(8,128)(2,1)}, u32[]{:S(2)}, u32[]{:S(2)}) collective-permute-start(bf16[768,384]{1,0:T(8,128)(2,1)S(1)} %bitcast.41), channel_id=1, source_target_pairs={{0,96},{32,0},{64,32},{96,64},{1,97},{33,1},{65,33},{97,65},{2,98}... | collective-permute-start | bytes 1769480 | tf_op jit(solution)/shard_map/ppermute | solution.py:521
  45.6 21.6 %collective-permute-start.6 = (bf16[48,2048]{1,0:T(8,128)(2,1)}, bf16[48,2048]{1,0:T(8,128)(2,1)S(1)}, u32[]{:S(2)}, u32[]{:S(2)}) collective-permute-start(bf16[48,2048]{1,0:T(8,128)(2,1)} %refs_0_), channel_id=1, source_target_pairs={{0,1},{1,2},{2,3},{3,0},{4,5},{5,6},{6,7},{7,4},{8,9},{9,10},{10,1... | collective-permute-start | bytes 589832 | tf_op jit(solution)/shard_map/ppermute | solution.py:521
  47.0 36.5 %collective-permute-start.7 = (bf16[48,2048]{1,0:T(8,128)(2,1)}, bf16[48,2048]{1,0:T(8,128)(2,1)S(1)}, u32[]{:S(2)}, u32[]{:S(2)}) collective-permute-start(bf16[48,2048]{1,0:T(8,128)(2,1)} %refs_0_), channel_id=1, source_target_pairs={{0,2},{1,3},{2,0},{3,1},{4,6},{5,7},{6,4},{7,5},{8,10},{9,11},{10,... | collective-permute-start | bytes 589832 | tf_op jit(solution)/shard_map/ppermute | solution.py:521
  49.1 36.9 %collective-permute-start.8 = (bf16[48,2048]{1,0:T(8,128)(2,1)}, bf16[48,2048]{1,0:T(8,128)(2,1)S(1)}, u32[]{:S(2)}, u32[]{:S(2)}) collective-permute-start(bf16[48,2048]{1,0:T(8,128)(2,1)} %refs_0_), channel_id=1, source_target_pairs={{0,3},{1,0},{2,1},{3,2},{4,7},{5,4},{6,5},{7,6},{8,11},{9,8},{10,9... | collective-permute-start | bytes 589832 | tf_op jit(solution)/shard_map/ppermute | solution.py:521
  50.2 61.6 %copy-start.4 = (s32[2]{0:T(128)}, s32[2]{0:T(128)S(1)}, u32[]{:S(2)}) copy-start(s32[2]{0:T(128)S(1)} %broadcast.308.info_ref) | copy-start | bytes 28
  56.4 1.6 copy-start.1
  60.2 51.6 %collective-permute-start.11 = (bf16[768,384]{1,0:T(8,128)(2,1)S(1)}, bf16[768,384]{1,0:T(8,128)(2,1)}, u32[]{:S(2)}, u32[]{:S(2)}) collective-permute-start(bf16[768,384]{1,0:T(8,128)(2,1)S(1)} %bitcast.42), channel_id=1, source_target_pairs={{0,16},{16,0},{1,17},{17,1},{2,18},{18,2},{3,19},{19,3},{4,20},{20... | collective-permute-start | bytes 1769480 | tf_op jit(solution)/shard_map/ppermute | solution.py:516
  66.2 19.9 %collective-permute-start.9 = (bf16[384,384]{1,0:T(8,128)(2,1)S(1)}, bf16[384,384]{1,0:T(8,128)(2,1)}, u32[]{:S(2)}, u32[]{:S(2)}) collective-permute-start(bf16[384,384]{1,0:T(8,128)(2,1)S(1)} %slice.27), channel_id=1, source_target_pairs={{0,32},{32,64},{64,96},{96,0},{1,33},{33,65},{65,97},{97,1},{2,34}... | collective-permute-start | bytes 884744 | tf_op jit(solution)/shard_map/ppermute | solution.py:521
  67.3 19.2 %copy-start.11 = (bf16[48,2048]{1,0:T(8,128)(2,1)}, bf16[48,2048]{1,0:T(8,128)(2,1)S(1)}, u32[]{:S(2)}) copy-start(bf16[48,2048]{1,0:T(8,128)(2,1)S(1)} %collective-permute-done.6.refs_1_) | copy-start | bytes 589828
  67.3 19.2 %collective-permute-start.10 = (bf16[384,384]{1,0:T(8,128)(2,1)S(1)}, bf16[384,384]{1,0:T(8,128)(2,1)}, u32[]{:S(2)}, u32[]{:S(2)}) collective-permute-start(bf16[384,384]{1,0:T(8,128)(2,1)S(1)} %slice.28), channel_id=1, source_target_pairs={{0,96},{32,0},{64,32},{96,64},{1,97},{33,1},{65,33},{97,65},{2,98}... | collective-permute-start | bytes 884744 | tf_op jit(solution)/shard_map/ppermute | solution.py:521
  83.4 3.0 %copy-start.12 = (bf16[48,2048]{1,0:T(8,128)(2,1)}, bf16[48,2048]{1,0:T(8,128)(2,1)S(1)}, u32[]{:S(2)}) copy-start(bf16[48,2048]{1,0:T(8,128)(2,1)S(1)} %collective-permute-done.7.refs_2_) | copy-start | bytes 589828
  83.5 28.4 %collective-permute-start.12 = (bf16[768,384]{1,0:T(8,128)(2,1)}, bf16[768,384]{1,0:T(8,128)(2,1)}, u32[]{:S(2)}, u32[]{:S(2)}) collective-permute-start(bf16[768,384]{1,0:T(8,128)(2,1)} %collective-permute-done.4.refs_1_), channel_id=1, source_target_pairs={{0,16},{16,0},{1,17},{17,1},{2,18},{18,2},{3,19},{19,3},{4,20},{20... | collective-permute-start | bytes 1769480 | tf_op jit(solution)/shard_map/ppermute | solution.py:516
  86.0 0.7 copy-start.13
  86.0 25.9 %collective-permute-start.15 = (bf16[768,384]{1,0:T(8,128)(2,1)}, bf16[768,384]{1,0:T(8,128)(2,1)}, u32[]{:S(2)}, u32[]{:S(2)}) collective-permute-start(bf16[768,384]{1,0:T(8,128)(2,1)} %collective-permute-done.5.refs_4_), channel_id=1, source_target_pairs={{0,16},{16,0},{1,17},{17,1},{2,18},{18,2},{3,19},{19,3},{4,20},{20... | collective-permute-start | bytes 1769480 | tf_op jit(solution)/shard_map/ppermute | solution.py:516
  86.1 25.7 %collective-permute-start.13 = (bf16[384,384]{1,0:T(8,128)(2,1)}, bf16[384,384]{1,0:T(8,128)(2,1)}, u32[]{:S(2)}, u32[]{:S(2)}) collective-permute-start(bf16[384,384]{1,0:T(8,128)(2,1)} %collective-permute-done.9.refs_2_), channel_id=1, source_target_pairs={{0,16},{16,0},{1,17},{17,1},{2,18},{18,2},{3,19},{19,3},{4,20},{20... | collective-permute-start | bytes 884744 | tf_op jit(solution)/shard_map/ppermute | solution.py:516
  86.7 25.2 %collective-permute-start.14 = (bf16[384,384]{1,0:T(8,128)(2,1)}, bf16[384,384]{1,0:T(8,128)(2,1)}, u32[]{:S(2)}, u32[]{:S(2)}) collective-permute-start(bf16[384,384]{1,0:T(8,128)(2,1)} %collective-permute-done.10.refs_3_), channel_id=1, source_target_pairs={{0,16},{16,0},{1,17},{17,1},{2,18},{18,2},{3,19},{19,3},{4,20},{20... | collective-permute-start | bytes 884744 | tf_op jit(solution)/shard_map/ppermute | solution.py:516
  111.9 23.7 %collective-permute-start.16 = (bf16[192,2048]{1,0:T(8,128)(2,1)}, bf16[192,2048]{1,0:T(8,128)(2,1)}, u32[]{:S(2)}, u32[]{:S(2)}) collective-permute-start(bf16[192,2048]{1,0:T(8,128)(2,1)} %shard_map.98.refs_0_), channel_id=1, source_target_pairs={{0,4},{4,8},{8,12},{12,0},{1,5},{5,9},{9,13},{13,1},{2,6},{6,10},{... | collective-permute-start | bytes 2359304 | tf_op jit(solution)/shard_map/ppermute | solution.py:521
  113.1 22.5 %collective-permute-start.17 = (bf16[192,2048]{1,0:T(8,128)(2,1)}, bf16[192,2048]{1,0:T(8,128)(2,1)}, u32[]{:S(2)}, u32[]{:S(2)}) collective-permute-start(bf16[192,2048]{1,0:T(8,128)(2,1)} %shard_map.98.refs_0_), channel_id=1, source_target_pairs={{0,12},{4,0},{8,4},{12,8},{1,13},{5,1},{9,5},{13,9},{2,14},{6,2},{... | collective-permute-start | bytes 2359304 | tf_op jit(solution)/shard_map/ppermute | solution.py:521
  118.9 22.9 %copy-start.2 = (bf16[768,2048]{1,0:T(8,128)(2,1)S(1)}, bf16[768,2048]{1,0:T(8,128)(2,1)}, u32[]{:S(2)}) copy-start(bf16[768,2048]{1,0:T(8,128)(2,1)} %copy-done.1) | copy-start | bytes 9437188
  135.6 10.0 %copy-start.5 = (bf16[1024,768]{1,0:T(8,128)(2,1)}, bf16[1024,768]{1,0:T(8,128)(2,1)S(1)}, u32[]{:S(2)}) copy-start(bf16[1024,768]{1,0:T(8,128)(2,1)S(1)} %shard_map.100.mine_ref) | copy-start | bytes 4718596
  135.6 6.2 %collective-permute-start.18 = (bf16[1024,768]{1,0:T(8,128)(2,1)S(1)}, bf16[1024,768]{1,0:T(8,128)(2,1)S(1)}, u32[]{:S(2)}, u32[]{:S(2)}) collective-permute-start(bf16[1024,768]{1,0:T(8,128)(2,1)S(1)} %shard_map.100.mine_ref), channel_id=1, source_target_pairs={{0,16},{16,0},{1,17},{17,1},{2,18},{18,2},{3,19},{19,3},{4,20},{20... | collective-permute-start | bytes 4718600 | tf_op jit(solution)/shard_map/ppermute | solution.py:516
  137.9 11.8 %collective-permute-start.19 = (bf16[96,2048]{1,0:T(8,128)(2,1)S(1)}, bf16[96,2048]{1,0:T(8,128)(2,1)S(1)}, u32[]{:S(2)}, u32[]{:S(2)}) collective-permute-start(bf16[96,2048]{1,0:T(8,128)(2,1)S(1)} %slice.30), channel_id=1, source_target_pairs={{0,4},{4,8},{8,12},{12,0},{1,5},{5,9},{9,13},{13,1},{2,6},{6,10},{... | collective-permute-start | bytes 1179656 | tf_op jit(solution)/shard_map/ppermute | solution.py:521
  139.1 10.7 %collective-permute-start.20 = (bf16[96,2048]{1,0:T(8,128)(2,1)S(1)}, bf16[96,2048]{1,0:T(8,128)(2,1)S(1)}, u32[]{:S(2)}, u32[]{:S(2)}) collective-permute-start(bf16[96,2048]{1,0:T(8,128)(2,1)S(1)} %slice.31), channel_id=1, source_target_pairs={{0,12},{4,0},{8,4},{12,8},{1,13},{5,1},{9,5},{13,9},{2,14},{6,2},{... | collective-permute-start | bytes 1179656 | tf_op jit(solution)/shard_map/ppermute | solution.py:521
  141.8 3.7 %copy-start.7 = (bf16[1024,768]{1,0:T(8,128)(2,1)}, bf16[1024,768]{1,0:T(8,128)(2,1)S(1)}, u32[]{:S(2)}) copy-start(bf16[1024,768]{1,0:T(8,128)(2,1)S(1)} %collective-permute-done.18.other_ref) | copy-start | bytes 4718596
  145.6 18.9 %copy-start = (bf16[192,2048]{1,0:T(8,128)(2,1)S(1)}, bf16[192,2048]{1,0:T(8,128)(2,1)}, u32[]{:S(2)}) copy-start(bf16[192,2048]{1,0:T(8,128)(2,1)} %shard_map.98.refs_0_) | copy-start | bytes 2359300
  149.8 36.1 %all-to-all-start.4 = ((bf16[16,40,768]{2,1,0:T(8,128)(2,1)}), bf16[16,40,768]{2,1,0:T(8,128)(2,1)S(1)}, u32[]{:S(2)}, u32[]{:S(2)}) async-start(bf16[16,40,768]{2,1,0:T(8,128)(2,1)} %shard_map.101), calls=%async_computation.4 | async-start | bytes 1966080 | tf_op jit(solution)/shard_map/all_to_all | solution.py:507
  185.9 0.9 copy-start.10
  191.5 17.5 %all-to-all-start.5 = ((f32[16,8,128]{2,1,0:T(8,128)}), f32[16,8,128]{2,1,0:T(8,128)S(1)}, u32[]{:S(2)}, u32[]{:S(2)}) async-start(f32[16,8,128]{2,1,0:T(8,128)} %get-tuple-element.166), calls=%async_computation.5 | async-start | bytes 131072 | tf_op jit(solution)/shard_map/all_to_all | solution.py:507
where the time goes:
time: 210 us
  Pallas kernels  90.3 us (43%)
  starting transfers between devices  68.9 us (33%)
  waiting for transfers between devices  33.2 us (16%)
  local copies, waits for them, and re-layouts  12.1 us (6%)
  other arithmetic  2.89 us (1%)
    all_to_all x4, starting transfers between devices, exchanged(): return lax.all_to_all(blocks, axis, 0, 0, tiled=True)  30.9 us
    pallas_call x1, Pallas kernels, joined(): pl.pallas_call(join_kernel, out_shape=jax.ShapeDtypeStruct((len(parts) *...  25 us
    ppermute x14, starting transfers between devices, turned(): lax.ppermute(shard, axis, [(i, (i + by) % devices) for i in range(devices)])  20.9 us
    ppermute x14, waiting for transfers between devices, turned(): lax.ppermute(shard, axis, [(i, (i + by) % devices) for i in range(devices)])  19.2 us
    ppermute x7, starting transfers between devices, swapped(): return lax.ppermute(shard, axis, [(0, 1), (1, 0)])  17.2 us
    pallas_call x1, Pallas kernels, encoded(): pl.pallas_call(encode_kernel, out_shape=jax.ShapeDtypeStruct(slab.shape,...  16.7 us
    pallas_call x1, Pallas kernels, scored(): pl.pallas_call(score_kernel, grid=(2 * half,), out_shape=(jax.ShapeDtypeS...  16.4 us
    all_to_all x4, waiting for transfers between devices, exchanged(): return lax.all_to_all(blocks, axis, 0, 0, tiled=True)  13.9 us
  transfers between devices with their start and end apart: 25, of which 6 were waited for; matrix products, arithmetic and copies ran while one was open for 5% of the time, Pallas kernels for 42%

commit v1 on v0

--- a/solution.py
+++ b/solution.py
@@ -65,7 +65,7 @@
         present_ref[pl.ds(pl.multiple_of(p * high, high), high), :] = jnp.where(seen > 0.5, 1.0, 0.0)
         return 0
 
-    lax.fori_loop(0, dests, find, 0, unroll=2)
+    lax.fori_loop(0, dests, find, 0, unroll=4)
     present = present_ref[...]
     rank_ref[...] = jnp.where(present > 0.5, ranked(present, dests) - first_slot.astype(F32), -1.0)
     blocks = -(-vocab // 128)
@@ -80,7 +80,7 @@
             ).astype(BF16)
         return jnp.maximum(most, jnp.max(ranks))
 
-    most = lax.fori_loop(0, dests, choose, jnp.float32(-1.0)) + first_slot.astype(F32)
+    most = lax.fori_loop(0, dests, choose, jnp.float32(-1.0), unroll=2) + first_slot.astype(F32)
     whole = vocab // 16 * 16
     rounds = jnp.floor(most * (1.0 / LIST) + 1e-3) + 1.0
     some = 4
@@ -187,9 +187,10 @@
 
 
 def join_kernel(*refs):
-    parts, out_ref, sems = refs[:-2], refs[-2], refs[-1]
+    parts, out_ref = refs[:-1], refs[-1]
     rows = parts[0].shape[0]
-    put(parts, [out_ref.at[pl.ds(k * rows, rows), :] for k in range(len(parts))], sems)
+    for k, ref in enumerate(parts):
+        out_ref[k * rows : (k + 1) * rows, :] = ref[...]
 
 
 def joined(parts):
@@ -197,9 +198,8 @@
     return pl.pallas_call(
         join_kernel,
         out_shape=jax.ShapeDtypeStruct((len(parts) * rows, cols), parts[0].dtype),
-        in_specs=[pl.BlockSpec(memory_space=pltpu.HBM)] * len(parts),
-        out_specs=pl.BlockSpec(memory_space=pltpu.HBM),
-        scratch_shapes=[pltpu.SemaphoreType.DMA((len(parts),))],
+        in_specs=[pl.BlockSpec(memory_space=pltpu.VMEM)] * len(parts),
+        out_specs=pl.BlockSpec(memory_space=pltpu.VMEM),
     )(*parts)
 
 
@@ -579,7 +579,9 @@
     w_back, w_ahead = neighbours(column, "x")
     near = joined([shard] + [turned(shard, "zl", k) for k in range(1, 4)])
     places = placed_rows(info_of(fs_rank, zero, vocab), ids, fs_size)
-    w_back, w_ahead, chosen, places = lax.optimization_barrier((w_back, w_ahead, chosen, places))
+    w_back, w_ahead, chosen, places, counts = lax.optimization_barrier(
+        (w_back, w_ahead, chosen, places, counts)
+    )
     rings = [column, w_back, *far_halves(w_back, w_ahead, "x"), w_ahead]
     rings += [swapped(w, "core") for w in rings]
     got = exchanged(sent, FS)

time: 210 us -> 186 us (0.89)
  Pallas kernels: 90.3 us -> 66.1 us
    pallas_call x1, Pallas kernels: 25 us -> 2.16 us  [joined(): pl.pallas_call(join_kernel, out_shape=jax.ShapeDtypeStruct((len(parts) *...]
    all_to_all x4, waiting for transfers between devices: 13.9 us -> 17.8 us  [exchanged(): return lax.all_to_all(blocks, axis, 0, 0, tiled=True)]
    ppermute x14, waiting for transfers between devices: 19.2 us -> 15.5 us  [turned(): lax.ppermute(shard, axis, [(i, (i + by) % devices) for i in range(devices)])]
  transfers between devices with their start and end apart: 25 -> 25, of which waited for: 6 -> 8; matrix products, arithmetic and copies ran while one was open for 5% -> 6% of each run, Pallas kernels for 42% -> 34%
where the time goes in v1:
time: 186 us; the launch traced here: 185 us
  starting transfers between devices  68.2 us (37%)
  Pallas kernels  66.1 us (36%)
  waiting for transfers between devices  34.1 us (18%)
  local copies, waits for them, and re-layouts  11.9 us (6%)
  other arithmetic  2.89 us (2%)
    all_to_all x4, starting transfers between devices, exchanged(): return lax.all_to_all(blocks, axis, 0, 0, tiled=True)  30.2 us
    ppermute x14, starting transfers between devices, turned(): lax.ppermute(shard, axis, [(i, (i + by) % devices) for i in range(devices)])  20.9 us
    all_to_all x4, waiting for transfers between devices, exchanged(): return lax.all_to_all(blocks, axis, 0, 0, tiled=True)  17.8 us
    ppermute x7, starting transfers between devices, swapped(): return lax.ppermute(shard, axis, [(0, 1), (1, 0)])  17.2 us
    pallas_call x1, Pallas kernels, encoded(): pl.pallas_call(encode_kernel, out_shape=jax.ShapeDtypeStruct(slab.shape,...  16.7 us
    pallas_call x1, Pallas kernels, scored(): pl.pallas_call(score_kernel, grid=(2 * half,), out_shape=(jax.ShapeDtypeS...  16.4 us
    ppermute x14, waiting for transfers between devices, turned(): lax.ppermute(shard, axis, [(i, (i + by) % devices) for i in range(devices)])  15.5 us
    pallas_call x1, Pallas kernels, listed_rows(): pl.pallas_call(lists_kernel, out_shape=jax.ShapeDtypeStruct((dests, ROOM,...  9.08 us
  transfers between devices with their start and end apart: 25, of which 8 were waited for; matrix products, arithmetic and copies ran while one was open for 6% of the time, Pallas kernels for 34%

profile of v1, /device:TPU:1, one launch (start us, length us, event | category | flops | bytes accessed | tf_op | source)
XLA Modules:
  0.0 185.4 jit_solution(13906501634393135683)
XLA Ops:
  0.6 7.8 %collective-permute-start = (s32[16,128]{1,0:T(8,128)}, s32[16,128]{1,0:T(8,128)S(1)}, u32[]{:S(2)}, u32[]{:S(2)}) collective-permute-start(s32[16,128]{1,0:T(8,128)} %bitcast.51), channel_id=1, source_target_pairs={{0,128},{128,0},{1,129},{129,1},{2,130},{130,2},{3,131},{131,3},{4... | collective-permute-start | bytes 24584 | tf_op jit(solution)/shard_map/ppermute | solution.py:516
  8.5 0.9 constant_dynamic-slice_fusion
  9.4 0.6 gather_fusion
  10.0 0.8 fusion
  10.8 0.9 broadcast_in_dim.42
  11.7 5.7 %all-to-all-start.2 = ((bf16[16,48,384]{2,1,0:T(8,128)(2,1)}), bf16[16,48,384]{2,1,0:T(8,128)(2,1)S(1)}, u32[]{:S(2)}, u32[]{:S(2)}) async-start(bf16[16,48,384]{2,1,0:T(8,128)(2,1)} %broadcast_in_dim.42), calls=%async_computation.2 | async-start | bytes 1179648 | tf_op jit(solution)/shard_map/all_to_all | solution.py:507
  17.4 0.6 gather_fusion.1
  18.1 0.6 gather_fusion.2
  18.7 0.1 subtract_bitcast_fusion
  18.8 1.3 collective-permute-start.1
  20.0 2.5 %collective-permute-start.2 = (s32[32,128]{1,0:T(8,128)S(1)}, s32[32,128]{1,0:T(8,128)S(1)}, u32[]{:S(2)}, u32[]{:S(2)}) collective-permute-start(s32[32,128]{1,0:T(8,128)S(1)} %pad_add_fusion.3.refs_0_), channel_id=1, source_target_pairs={{0,64},{32,96},{64,0},{96,32},{1,65},{33,97},{65,1},{97,33},{2,66}... | collective-permute-start | bytes 49160 | tf_op jit(solution)/shard_map/ppermute | solution.py:521
  22.5 1.2 collective-permute-start.3
  23.7 0.7 collective-permute-done.2.refs_2_
  24.4 1.0 collective-permute-done.3.refs_3_
  25.5 9.1 %shard_map.95 = bf16[16,48,768]{2,1,0:T(8,128)(2,1)} custom-call(s32[2]{0:T(128)S(1)} %pad_add_fusion.4.info_ref, s32[32,128]{1,0:T(8,128)S(1)} %pad_add_fusion.3.refs_0_, s32[32,128]{1,0:T(8,128)S(1)} %collective-permute-done.1.refs_1_, s32[32,128]{1,0:T(8,128)S(1)} %collective-permute-done.2.refs_2_, s32[32,128]{1,0:T(8,128)S(1)} %collective-permute-done.3.refs_3_, ...), custom_call_target="tpu_custom_call" | custom-call | tf_op jit(solution)/shard_map/pallas_call | solution.py:105
  34.5 6.9 %all-to-all-start.3 = ((bf16[16,48,768]{2,1,0:T(8,128)(2,1)}), bf16[16,48,768]{2,1,0:T(8,128)(2,1)S(1)}, u32[]{:S(2)}, u32[]{:S(2)}) async-start(bf16[16,48,768]{2,1,0:T(8,128)(2,1)} %shard_map.95), calls=%async_computation.3 | async-start | bytes 2359296 | tf_op jit(solution)/shard_map/all_to_all | solution.py:507
  41.4 0.3 collective-permute-start.4
  41.8 2.4 %collective-permute-start.5 = (bf16[768,384]{1,0:T(8,128)(2,1)S(1)}, bf16[768,384]{1,0:T(8,128)(2,1)}, u32[]{:S(2)}, u32[]{:S(2)}) collective-permute-start(bf16[768,384]{1,0:T(8,128)(2,1)S(1)} %bitcast.41), channel_id=1, source_target_pairs={{0,96},{32,0},{64,32},{96,64},{1,97},{33,1},{65,33},{97,65},{2,98}... | collective-permute-start | bytes 1769480 | tf_op jit(solution)/shard_map/ppermute | solution.py:521
  44.2 1.4 collective-permute-start.6
  45.6 2.1 %collective-permute-start.7 = (bf16[48,2048]{1,0:T(8,128)(2,1)}, bf16[48,2048]{1,0:T(8,128)(2,1)}, u32[]{:S(2)}, u32[]{:S(2)}) collective-permute-start(bf16[48,2048]{1,0:T(8,128)(2,1)} %refs_0_), channel_id=1, source_target_pairs={{0,2},{1,3},{2,0},{3,1},{4,6},{5,7},{6,4},{7,5},{8,10},{9,11},{10,... | collective-permute-start | bytes 589832 | tf_op jit(solution)/shard_map/ppermute | solution.py:521
  47.6 1.2 collective-permute-start.8
  48.8 6.2 %shard_map.96 = (bf16[768,2048]{1,0:T(8,128)(2,1)S(1)}, f32[8,128]{1,0:T(8,128)S(1)}) custom-call(s32[2]{0:T(128)S(1)} %broadcast.308.info_ref, s32[1,2048]{1,0:T(1,128)S(1)} %bitcast.44), custom_call_target="tpu_custom_call" | custom-call | tf_op jit(solution)/shard_map/pallas_call | solution.py:411
  55.0 1.6 copy-done.1
  56.6 3.9 %shard_map.98.counts_ref = f32[128,128]{1,0:T(8,128)S(1)} custom-call(s32[1]{0:T(128)} %bitcast.20.info_ref, s32[16,16,128]{2,1,0:T(8,128)} %bitcast.48), custom_call_target="tpu_custom_call" | custom-call | tf_op jit(solution)/shard_map/pallas_call | solution.py:468
  60.6 2.1 %shard_map.97.places_ref = bf16[1024,768]{1,0:T(8,128)(2,1)S(1)} custom-call(s32[3]{0:T(128)S(1)} %pad_add_fusion.5.info_ref, s32[32,128]{1,0:T(8,128)S(1)} %pad_add_fusion.3.refs_0_, s32[32,128]{1,0:T(8,128)S(1)} %collective-permute-done.1.refs_1_, s32[32,128]{1,0:T(8,128)S(1)} %collective-permute-done.2.refs_2_, s32[32,128]{1,0:T(8,128)S(1)} %collective-permute-done.3.refs_3_), custom_call_target="tpu_custom_call" | custom-call | tf_op jit(solution)/shard_map/pallas_call | solution.py:152
  62.6 5.0 %collective-permute-start.11 = (bf16[768,384]{1,0:T(8,128)(2,1)S(1)}, bf16[768,384]{1,0:T(8,128)(2,1)}, u32[]{:S(2)}, u32[]{:S(2)}) collective-permute-start(bf16[768,384]{1,0:T(8,128)(2,1)S(1)} %bitcast.42), channel_id=1, source_target_pairs={{0,16},{16,0},{1,17},{17,1},{2,18},{18,2},{3,19},{19,3},{4,20},{20... | collective-permute-start | bytes 1769480 | tf_op jit(solution)/shard_map/ppermute | solution.py:516
  67.6 1.0 slice.27
  68.6 0.1 collective-permute-start.9
  68.7 1.0 slice.28
  69.7 2.9 %collective-permute-start.10 = (bf16[384,384]{1,0:T(8,128)(2,1)S(1)}, bf16[384,384]{1,0:T(8,128)(2,1)}, u32[]{:S(2)}, u32[]{:S(2)}) collective-permute-start(bf16[384,384]{1,0:T(8,128)(2,1)S(1)} %slice.28), channel_id=1, source_target_pairs={{0,96},{32,0},{64,32},{96,64},{1,97},{33,1},{65,33},{97,65},{2,98}... | collective-permute-start | bytes 884744 | tf_op jit(solution)/shard_map/ppermute | solution.py:521
  72.6 9.5 %collective-permute-done.7.refs_2_ = bf16[48,2048]{1,0:T(8,128)(2,1)} collective-permute-done((bf16[48,2048]{1,0:T(8,128)(2,1)}, bf16[48,2048]{1,0:T(8,128)(2,1)}, u32[]{:S(2)}, u32[]{:S(2)}) %collective-permute-start.7) | collective-permute-done | bytes 196640 | tf_op jit(solution)/shard_map/ppermute | solution.py:521
  82.1 2.5 %collective-permute-start.12 = (bf16[768,384]{1,0:T(8,128)(2,1)}, bf16[768,384]{1,0:T(8,128)(2,1)}, u32[]{:S(2)}, u32[]{:S(2)}) collective-permute-start(bf16[768,384]{1,0:T(8,128)(2,1)} %collective-permute-done.4.refs_1_), channel_id=1, source_target_pairs={{0,16},{16,0},{1,17},{17,1},{2,18},{18,2},{3,19},{19,3},{4,20},{20... | collective-permute-start | bytes 1769480 | tf_op jit(solution)/shard_map/ppermute | solution.py:516
  84.7 0.5 collective-permute-start.13
  85.2 0.1 collective-permute-start.14
  85.3 0.1 pad_add_fusion.6.info_ref
  85.4 2.2 %shard_map.99.refs_0_ = bf16[192,2048]{1,0:T(8,128)(2,1)} custom-call(bf16[48,2048]{1,0:T(8,128)(2,1)} %refs_0_, bf16[48,2048]{1,0:T(8,128)(2,1)} %collective-permute-done.6.refs_1_, bf16[48,2048]{1,0:T(8,128)(2,1)} %collective-permute-done.7.refs_2_, bf16[48,2048]{1,0:T(8,128)(2,1)} %collective-permute-done.8.refs_3_), custom_call_target="tpu_custom_call" | custom-call | tf_op jit(solution)/shard_map/pallas_call | solution.py:198
  87.5 0.4 collective-permute-done.13.refs_7_
  87.9 0.4 collective-permute-done.14.refs_8_
  88.3 1.3 collective-permute-start.16
  89.6 1.5 collective-permute-start.17
  91.1 3.2 %shard_map.100 = (bf16[1024,768]{1,0:T(8,128)(2,1)}, s32[8,128]{1,0:T(8,128)S(1)}) custom-call(bf16[1024,768]{1,0:T(8,128)(2,1)S(1)} %shard_map.97.places_ref, bf16[16,48,768]{2,1,0:T(8,128)(2,1)S(1)} %all-to-all-done.3.got_ref), custom_call_target="tpu_custom_call" | custom-call | tf_op jit(solution)/shard_map/pallas_call | solution.py:177
  94.3 0.5 slice.29
  94.8 0.6 while.20
  95.4 16.7 %shard_map.101.mine_ref = bf16[1024,768]{1,0:T(8,128)(2,1)S(1)} custom-call(s32[2]{0:T(128)S(1)} %pad_add_fusion.6.info_ref, bf16[768,384]{1,0:T(8,128)(2,1)S(1)} %bitcast.43, bf16[768,384]{1,0:T(8,128)(2,1)} %collective-permute-done.4.refs_1_, bf16[384,384]{1,0:T(8,128)(2,1)} %collective-permute-done.9.refs_2_, ...), custom_call_target="tpu_custom_call" | custom-call | tf_op jit(solution)/shard_map/pallas_call | solution.py:288
  112.1 1.2 collective-permute-start.18
  113.4 1.0 slice.30
  114.4 0.1 collective-permute-start.19
  114.5 1.0 slice.31
  115.5 2.7 %collective-permute-start.20 = (bf16[96,2048]{1,0:T(8,128)(2,1)S(1)}, bf16[96,2048]{1,0:T(8,128)(2,1)S(1)}, u32[]{:S(2)}, u32[]{:S(2)}) collective-permute-start(bf16[96,2048]{1,0:T(8,128)(2,1)S(1)} %slice.31), channel_id=1, source_target_pairs={{0,12},{4,0},{8,4},{12,8},{1,13},{5,1},{9,5},{13,9},{2,14},{6,2},{... | collective-permute-start | bytes 1179656 | tf_op jit(solution)/shard_map/ppermute | solution.py:521
  118.3 3.7 %shard_map.102 = bf16[16,40,768]{2,1,0:T(8,128)(2,1)} custom-call(bf16[768,2048]{1,0:T(8,128)(2,1)S(1)} %copy-done.2, f32[8,128]{1,0:T(8,128)S(1)} %get-tuple-element.136.most_ref, bf16[1024,768]{1,0:T(8,128)(2,1)S(1)} %shard_map.101.mine_ref, bf16[1024,768]{1,0:T(8,128)(2,1)S(1)} %collective-permute-done.18.other_ref), custom_call_target="tpu_custom_call" | custom-call | tf_op jit(solution)/shard_map/pallas_call | solution.py:444
  122.0 4.2 %collective-permute-done.19.refs_2_ = bf16[96,2048]{1,0:T(8,128)(2,1)S(1)} collective-permute-done((bf16[96,2048]{1,0:T(8,128)(2,1)S(1)}, bf16[96,2048]{1,0:T(8,128)(2,1)S(1)}, u32[]{:S(2)}, u32[]{:S(2)}) %collective-permute-start.19) | collective-permute-done | bytes 393248 | tf_op jit(solution)/shard_map/ppermute | solution.py:521
  126.2 9.9 %all-to-all-start.4 = ((bf16[16,40,768]{2,1,0:T(8,128)(2,1)}), bf16[16,40,768]{2,1,0:T(8,128)(2,1)S(1)}, u32[]{:S(2)}, u32[]{:S(2)}) async-start(bf16[16,40,768]{2,1,0:T(8,128)(2,1)} %shard_map.102), calls=%async_computation.4 | async-start | bytes 1966080 | tf_op jit(solution)/shard_map/all_to_all | solution.py:507
  136.2 0.1 stack.63.info_ref
  136.3 0.1 slice_reduce_fusion
  136.4 16.4 %shard_map.103 = (f32[16,8,128]{2,1,0:T(8,128)}, f32[128,768]{1,0:T(8,128)S(1)}) custom-call(s32[7]{0:T(128)S(1)} %stack.63.info_ref, bf16[1024,768]{1,0:T(8,128)(2,1)} %copy-done.5, bf16[1024,768]{1,0:T(8,128)(2,1)} %copy-done.7, s32[16,1,128]{2,1,0:T(1,128)S(1)} %bitcast.45, bf16[192,2048]{1,0:T(8,128)(2,1)S(1)} %copy-done, ...), custom_call_target="tpu_custom_call" | custom-call | tf_op jit(solution)/shard_map/pallas_call | solution.py:359
  152.8 8.9 %all-to-all-done.4.got_ref = bf16[16,40,768]{2,1,0:T(8,128)(2,1)S(1)} async-done(((bf16[16,40,768]{2,1,0:T(8,128)(2,1)}), bf16[16,40,768]{2,1,0:T(8,128)(2,1)S(1)}, u32[]{:S(2)}, u32[]{:S(2)}) %all-to-all-start.4) | async-done | bytes 983072 | tf_op jit(solution)/shard_map/all_to_all | solution.py:507
  161.7 0.9 copy-done.10
  162.7 2.8 %shard_map.104 = (f32[128,768]{1,0:T(8,128)S(1)}, s32[8,128]{1,0:T(8,128)}) custom-call(s32[2]{0:T(128)} %copy-done.4, f32[128,128]{1,0:T(8,128)S(1)} %shard_map.98.counts_ref, bf16[16,40,768]{2,1,0:T(8,128)(2,1)} %copy-done.10), custom_call_target="tpu_custom_call" | custom-call | tf_op jit(solution)/shard_map/pallas_call | solution.py:494
  165.5 1.2 slice.35
  166.7 0.7 while.21
  167.3 7.7 %all-to-all-start.5 = ((f32[16,8,128]{2,1,0:T(8,128)}), f32[16,8,128]{2,1,0:T(8,128)S(1)}, u32[]{:S(2)}, u32[]{:S(2)}) async-start(f32[16,8,128]{2,1,0:T(8,128)} %get-tuple-element.167), calls=%async_computation.5 | async-start | bytes 131072 | tf_op jit(solution)/shard_map/all_to_all | solution.py:507
  175.1 0.9 divide_select_fusion
  175.9 8.9 %all-to-all-done.5 = f32[16,8,128]{2,1,0:T(8,128)S(1)} async-done(((f32[16,8,128]{2,1,0:T(8,128)}), f32[16,8,128]{2,1,0:T(8,128)S(1)}, u32[]{:S(2)}, u32[]{:S(2)}) %all-to-all-start.5) | async-done | bytes 65568 | tf_op jit(solution)/shard_map/all_to_all | solution.py:507
  184.8 0.5 add_subtract_fusion
  (59 shorter events, 0.6 us)
Async XLA Ops:
  0.6 18.1 %copy-start.11 = (s32[2048]{0:T(1024)S(1)}, s32[2048]{0:T(1024)}, u32[]{:S(2)}) copy-start(s32[2048]{0:T(1024)} %param.12) | copy-start | bytes 24580
  0.6 18.1 %collective-permute-start = (s32[16,128]{1,0:T(8,128)}, s32[16,128]{1,0:T(8,128)S(1)}, u32[]{:S(2)}, u32[]{:S(2)}) collective-permute-start(s32[16,128]{1,0:T(8,128)} %bitcast.51), channel_id=1, source_target_pairs={{0,128},{128,0},{1,129},{129,1},{2,130},{130,2},{3,131},{131,3},{4... | collective-permute-start | bytes 24584 | tf_op jit(solution)/shard_map/ppermute | solution.py:516
  11.7 22.8 %all-to-all-start.2 = ((bf16[16,48,384]{2,1,0:T(8,128)(2,1)}), bf16[16,48,384]{2,1,0:T(8,128)(2,1)S(1)}, u32[]{:S(2)}, u32[]{:S(2)}) async-start(bf16[16,48,384]{2,1,0:T(8,128)(2,1)} %broadcast_in_dim.42), calls=%async_computation.2 | async-start | bytes 1179648 | tf_op jit(solution)/shard_map/all_to_all | solution.py:507
  18.8 5.0 %collective-permute-start.1 = (s32[32,128]{1,0:T(8,128)S(1)}, s32[32,128]{1,0:T(8,128)S(1)}, u32[]{:S(2)}, u32[]{:S(2)}) collective-permute-start(s32[32,128]{1,0:T(8,128)S(1)} %pad_add_fusion.3.refs_0_), channel_id=1, source_target_pairs={{0,32},{32,64},{64,96},{96,0},{1,33},{33,65},{65,97},{97,1},{2,34}... | collective-permute-start | bytes 49160 | tf_op jit(solution)/shard_map/ppermute | solution.py:521
  20.0 4.4 %collective-permute-start.2 = (s32[32,128]{1,0:T(8,128)S(1)}, s32[32,128]{1,0:T(8,128)S(1)}, u32[]{:S(2)}, u32[]{:S(2)}) collective-permute-start(s32[32,128]{1,0:T(8,128)S(1)} %pad_add_fusion.3.refs_0_), channel_id=1, source_target_pairs={{0,64},{32,96},{64,0},{96,32},{1,65},{33,97},{65,1},{97,33},{2,66}... | collective-permute-start | bytes 49160 | tf_op jit(solution)/shard_map/ppermute | solution.py:521
  22.5 3.0 %collective-permute-start.3 = (s32[32,128]{1,0:T(8,128)S(1)}, s32[32,128]{1,0:T(8,128)S(1)}, u32[]{:S(2)}, u32[]{:S(2)}) collective-permute-start(s32[32,128]{1,0:T(8,128)S(1)} %pad_add_fusion.3.refs_0_), channel_id=1, source_target_pairs={{0,96},{32,0},{64,32},{96,64},{1,97},{33,1},{65,33},{97,65},{2,98}... | collective-permute-start | bytes 49160 | tf_op jit(solution)/shard_map/ppermute | solution.py:521
  34.5 53.8 %all-to-all-start.3 = ((bf16[16,48,768]{2,1,0:T(8,128)(2,1)}), bf16[16,48,768]{2,1,0:T(8,128)(2,1)S(1)}, u32[]{:S(2)}, u32[]{:S(2)}) async-start(bf16[16,48,768]{2,1,0:T(8,128)(2,1)} %shard_map.95), calls=%async_computation.3 | async-start | bytes 2359296 | tf_op jit(solution)/shard_map/all_to_all | solution.py:507
  41.4 43.9 %copy-start.12 = (f32[768]{0:T(1024)S(1)}, f32[768]{0:T(1024)}, u32[]{:S(2)}) copy-start(f32[768]{0:T(1024)} %param.16) | copy-start | bytes 9220
  41.4 43.8 %copy-start.13 = (f32[768]{0:T(1024)S(1)}, f32[768]{0:T(1024)}, u32[]{:S(2)}) copy-start(f32[768]{0:T(1024)} %param.17) | copy-start | bytes 9220
  41.4 21.2 %collective-permute-start.4 = (bf16[768,384]{1,0:T(8,128)(2,1)S(1)}, bf16[768,384]{1,0:T(8,128)(2,1)}, u32[]{:S(2)}, u32[]{:S(2)}) collective-permute-start(bf16[768,384]{1,0:T(8,128)(2,1)S(1)} %bitcast.40), channel_id=1, source_target_pairs={{0,32},{32,64},{64,96},{96,0},{1,33},{33,65},{65,97},{97,1},{2,34}... | collective-permute-start | bytes 1769480 | tf_op jit(solution)/shard_map/ppermute | solution.py:521
  41.8 25.8 %collective-permute-start.5 = (bf16[768,384]{1,0:T(8,128)(2,1)S(1)}, bf16[768,384]{1,0:T(8,128)(2,1)}, u32[]{:S(2)}, u32[]{:S(2)}) collective-permute-start(bf16[768,384]{1,0:T(8,128)(2,1)S(1)} %bitcast.41), channel_id=1, source_target_pairs={{0,96},{32,0},{64,32},{96,64},{1,97},{33,1},{65,33},{97,65},{2,98}... | collective-permute-start | bytes 1769480 | tf_op jit(solution)/shard_map/ppermute | solution.py:521
  44.2 25.5 %collective-permute-start.6 = (bf16[48,2048]{1,0:T(8,128)(2,1)}, bf16[48,2048]{1,0:T(8,128)(2,1)}, u32[]{:S(2)}, u32[]{:S(2)}) collective-permute-start(bf16[48,2048]{1,0:T(8,128)(2,1)} %refs_0_), channel_id=1, source_target_pairs={{0,1},{1,2},{2,3},{3,0},{4,5},{5,6},{6,7},{7,4},{8,9},{9,10},{10,1... | collective-permute-start | bytes 589832 | tf_op jit(solution)/shard_map/ppermute | solution.py:521
  45.6 36.6 %collective-permute-start.7 = (bf16[48,2048]{1,0:T(8,128)(2,1)}, bf16[48,2048]{1,0:T(8,128)(2,1)}, u32[]{:S(2)}, u32[]{:S(2)}) collective-permute-start(bf16[48,2048]{1,0:T(8,128)(2,1)} %refs_0_), channel_id=1, source_target_pairs={{0,2},{1,3},{2,0},{3,1},{4,6},{5,7},{6,4},{7,5},{8,10},{9,11},{10,... | collective-permute-start | bytes 589832 | tf_op jit(solution)/shard_map/ppermute | solution.py:521
  47.6 37.0 %collective-permute-start.8 = (bf16[48,2048]{1,0:T(8,128)(2,1)}, bf16[48,2048]{1,0:T(8,128)(2,1)}, u32[]{:S(2)}, u32[]{:S(2)}) collective-permute-start(bf16[48,2048]{1,0:T(8,128)(2,1)} %refs_0_), channel_id=1, source_target_pairs={{0,3},{1,0},{2,1},{3,2},{4,7},{5,4},{6,5},{7,6},{8,11},{9,8},{10,9... | collective-permute-start | bytes 589832 | tf_op jit(solution)/shard_map/ppermute | solution.py:521
  48.8 38.7 %copy-start.4 = (s32[2]{0:T(128)}, s32[2]{0:T(128)S(1)}, u32[]{:S(2)}) copy-start(s32[2]{0:T(128)S(1)} %broadcast.308.info_ref) | copy-start | bytes 28
  55.0 1.6 copy-start.1
  62.6 24.9 %collective-permute-start.11 = (bf16[768,384]{1,0:T(8,128)(2,1)S(1)}, bf16[768,384]{1,0:T(8,128)(2,1)}, u32[]{:S(2)}, u32[]{:S(2)}) collective-permute-start(bf16[768,384]{1,0:T(8,128)(2,1)S(1)} %bitcast.42), channel_id=1, source_target_pairs={{0,16},{16,0},{1,17},{17,1},{2,18},{18,2},{3,19},{19,3},{4,20},{20... | collective-permute-start | bytes 1769480 | tf_op jit(solution)/shard_map/ppermute | solution.py:516
  68.6 16.0 %collective-permute-start.9 = (bf16[384,384]{1,0:T(8,128)(2,1)S(1)}, bf16[384,384]{1,0:T(8,128)(2,1)}, u32[]{:S(2)}, u32[]{:S(2)}) collective-permute-start(bf16[384,384]{1,0:T(8,128)(2,1)S(1)} %slice.27), channel_id=1, source_target_pairs={{0,32},{32,64},{64,96},{96,0},{1,33},{33,65},{65,97},{97,1},{2,34}... | collective-permute-start | bytes 884744 | tf_op jit(solution)/shard_map/ppermute | solution.py:521
  69.7 15.5 %collective-permute-start.10 = (bf16[384,384]{1,0:T(8,128)(2,1)S(1)}, bf16[384,384]{1,0:T(8,128)(2,1)}, u32[]{:S(2)}, u32[]{:S(2)}) collective-permute-start(bf16[384,384]{1,0:T(8,128)(2,1)S(1)} %slice.28), channel_id=1, source_target_pairs={{0,96},{32,0},{64,32},{96,64},{1,97},{33,1},{65,33},{97,65},{2,98}... | collective-permute-start | bytes 884744 | tf_op jit(solution)/shard_map/ppermute | solution.py:521
  82.1 6.2 %collective-permute-start.12 = (bf16[768,384]{1,0:T(8,128)(2,1)}, bf16[768,384]{1,0:T(8,128)(2,1)}, u32[]{:S(2)}, u32[]{:S(2)}) collective-permute-start(bf16[768,384]{1,0:T(8,128)(2,1)} %collective-permute-done.4.refs_1_), channel_id=1, source_target_pairs={{0,16},{16,0},{1,17},{17,1},{2,18},{18,2},{3,19},{19,3},{4,20},{20... | collective-permute-start | bytes 1769480 | tf_op jit(solution)/shard_map/ppermute | solution.py:516
  84.7 3.7 %collective-permute-start.15 = (bf16[768,384]{1,0:T(8,128)(2,1)}, bf16[768,384]{1,0:T(8,128)(2,1)}, u32[]{:S(2)}, u32[]{:S(2)}) collective-permute-start(bf16[768,384]{1,0:T(8,128)(2,1)} %collective-permute-done.5.refs_4_), channel_id=1, source_target_pairs={{0,16},{16,0},{1,17},{17,1},{2,18},{18,2},{3,19},{19,3},{4,20},{20... | collective-permute-start | bytes 1769480 | tf_op jit(solution)/shard_map/ppermute | solution.py:516
  84.7 3.2 %collective-permute-start.13 = (bf16[384,384]{1,0:T(8,128)(2,1)}, bf16[384,384]{1,0:T(8,128)(2,1)}, u32[]{:S(2)}, u32[]{:S(2)}) collective-permute-start(bf16[384,384]{1,0:T(8,128)(2,1)} %collective-permute-done.9.refs_2_), channel_id=1, source_target_pairs={{0,16},{16,0},{1,17},{17,1},{2,18},{18,2},{3,19},{19,3},{4,20},{20... | collective-permute-start | bytes 884744 | tf_op jit(solution)/shard_map/ppermute | solution.py:516
  85.2 3.1 %collective-permute-start.14 = (bf16[384,384]{1,0:T(8,128)(2,1)}, bf16[384,384]{1,0:T(8,128)(2,1)}, u32[]{:S(2)}, u32[]{:S(2)}) collective-permute-start(bf16[384,384]{1,0:T(8,128)(2,1)} %collective-permute-done.10.refs_3_), channel_id=1, source_target_pairs={{0,16},{16,0},{1,17},{17,1},{2,18},{18,2},{3,19},{19,3},{4,20},{20... | collective-permute-start | bytes 884744 | tf_op jit(solution)/shard_map/ppermute | solution.py:516
  88.3 23.8 %collective-permute-start.16 = (bf16[192,2048]{1,0:T(8,128)(2,1)}, bf16[192,2048]{1,0:T(8,128)(2,1)}, u32[]{:S(2)}, u32[]{:S(2)}) collective-permute-start(bf16[192,2048]{1,0:T(8,128)(2,1)} %shard_map.99.refs_0_), channel_id=1, source_target_pairs={{0,4},{4,8},{8,12},{12,0},{1,5},{5,9},{9,13},{13,1},{2,6},{6,10},{... | collective-permute-start | bytes 2359304 | tf_op jit(solution)/shard_map/ppermute | solution.py:521
  89.6 22.5 %collective-permute-start.17 = (bf16[192,2048]{1,0:T(8,128)(2,1)}, bf16[192,2048]{1,0:T(8,128)(2,1)}, u32[]{:S(2)}, u32[]{:S(2)}) collective-permute-start(bf16[192,2048]{1,0:T(8,128)(2,1)} %shard_map.99.refs_0_), channel_id=1, source_target_pairs={{0,12},{4,0},{8,4},{12,8},{1,13},{5,1},{9,5},{13,9},{2,14},{6,2},{... | collective-permute-start | bytes 2359304 | tf_op jit(solution)/shard_map/ppermute | solution.py:521
  95.4 22.8 %copy-start.2 = (bf16[768,2048]{1,0:T(8,128)(2,1)S(1)}, bf16[768,2048]{1,0:T(8,128)(2,1)}, u32[]{:S(2)}) copy-start(bf16[768,2048]{1,0:T(8,128)(2,1)} %copy-done.1) | copy-start | bytes 9437188
  112.1 9.9 %copy-start.5 = (bf16[1024,768]{1,0:T(8,128)(2,1)}, bf16[1024,768]{1,0:T(8,128)(2,1)S(1)}, u32[]{:S(2)}) copy-start(bf16[1024,768]{1,0:T(8,128)(2,1)S(1)} %shard_map.101.mine_ref) | copy-start | bytes 4718596
  112.1 6.1 %collective-permute-start.18 = (bf16[1024,768]{1,0:T(8,128)(2,1)S(1)}, bf16[1024,768]{1,0:T(8,128)(2,1)S(1)}, u32[]{:S(2)}, u32[]{:S(2)}) collective-permute-start(bf16[1024,768]{1,0:T(8,128)(2,1)S(1)} %shard_map.101.mine_ref), channel_id=1, source_target_pairs={{0,16},{16,0},{1,17},{17,1},{2,18},{18,2},{3,19},{19,3},{4,20},{20... | collective-permute-start | bytes 4718600 | tf_op jit(solution)/shard_map/ppermute | solution.py:516
  114.4 11.8 %collective-permute-start.19 = (bf16[96,2048]{1,0:T(8,128)(2,1)S(1)}, bf16[96,2048]{1,0:T(8,128)(2,1)S(1)}, u32[]{:S(2)}, u32[]{:S(2)}) collective-permute-start(bf16[96,2048]{1,0:T(8,128)(2,1)S(1)} %slice.30), channel_id=1, source_target_pairs={{0,4},{4,8},{8,12},{12,0},{1,5},{5,9},{9,13},{13,1},{2,6},{6,10},{... | collective-permute-start | bytes 1179656 | tf_op jit(solution)/shard_map/ppermute | solution.py:521
  115.5 10.7 %collective-permute-start.20 = (bf16[96,2048]{1,0:T(8,128)(2,1)S(1)}, bf16[96,2048]{1,0:T(8,128)(2,1)S(1)}, u32[]{:S(2)}, u32[]{:S(2)}) collective-permute-start(bf16[96,2048]{1,0:T(8,128)(2,1)S(1)} %slice.31), channel_id=1, source_target_pairs={{0,12},{4,0},{8,4},{12,8},{1,13},{5,1},{9,5},{13,9},{2,14},{6,2},{... | collective-permute-start | bytes 1179656 | tf_op jit(solution)/shard_map/ppermute | solution.py:521
  118.3 3.7 %copy-start.7 = (bf16[1024,768]{1,0:T(8,128)(2,1)}, bf16[1024,768]{1,0:T(8,128)(2,1)S(1)}, u32[]{:S(2)}) copy-start(bf16[1024,768]{1,0:T(8,128)(2,1)S(1)} %collective-permute-done.18.other_ref) | copy-start | bytes 4718596
  122.0 14.4 %copy-start = (bf16[192,2048]{1,0:T(8,128)(2,1)S(1)}, bf16[192,2048]{1,0:T(8,128)(2,1)}, u32[]{:S(2)}) copy-start(bf16[192,2048]{1,0:T(8,128)(2,1)} %shard_map.99.refs_0_) | copy-start | bytes 2359300
  126.2 35.5 %all-to-all-start.4 = ((bf16[16,40,768]{2,1,0:T(8,128)(2,1)}), bf16[16,40,768]{2,1,0:T(8,128)(2,1)S(1)}, u32[]{:S(2)}, u32[]{:S(2)}) async-start(bf16[16,40,768]{2,1,0:T(8,128)(2,1)} %shard_map.102), calls=%async_computation.4 | async-start | bytes 1966080 | tf_op jit(solution)/shard_map/all_to_all | solution.py:507
  161.7 1.0 copy-start.10
  167.3 17.5 %all-to-all-start.5 = ((f32[16,8,128]{2,1,0:T(8,128)}), f32[16,8,128]{2,1,0:T(8,128)S(1)}, u32[]{:S(2)}, u32[]{:S(2)}) async-start(f32[16,8,128]{2,1,0:T(8,128)} %get-tuple-element.167), calls=%async_computation.5 | async-start | bytes 131072 | tf_op jit(solution)/shard_map/all_to_all | solution.py:507

commit v2 on v1

--- a/solution.py
+++ b/solution.py
@@ -12,9 +12,9 @@
 DP = ("zh", "x", "core")
 FS = ("y", "zl")
 ALL = DP + FS
-LIST = 47
-SLOTS = 39
-BLOCK = SLOTS + 1
+LIST = 30
+SLOTS = 25
+BLOCK = 40
 ROOM = 48
 F32 = jnp.float32
 BF16 = jnp.bfloat16

time: 186 us -> 281 us (1.51)
  starting transfers between devices: 68.2 us -> 117 us
  waiting for transfers between devices: 34.1 us -> 61.6 us
  Pallas kernels: 66.1 us -> 80 us
    all_to_all x4 -> x5, starting transfers between devices: 30.2 us -> 78 us  [exchanged(): return lax.all_to_all(blocks, axis, 0, 0, tiled=True)]
    all_to_all x4 -> x5, waiting for transfers between devices: 17.8 us -> 45.5 us  [exchanged(): return lax.all_to_all(blocks, axis, 0, 0, tiled=True)]
    pallas_call x1 -> x2, Pallas kernels: 9.08 us -> 18.2 us  [listed_rows(): pl.pallas_call(lists_kernel, out_shape=jax.ShapeDtypeStruct((dests, ROOM,...]
    pallas_call x1 -> x2, Pallas kernels: 3.19 us -> 5.82 us  [expanded(): pl.pallas_call(expand_kernel, out_shape=(jax.ShapeDtypeStruct((places.sha...]
  transfers between devices with their start and end apart: 25 -> 26, of which waited for: 8 -> 9; matrix products, arithmetic and copies ran while one was open for 6% -> 4% of each run, Pallas kernels for 34% -> 28%
where the time goes in v2:
time: 281 us; the launch traced here: 278 us
  starting transfers between devices  117 us (42%)
  Pallas kernels  80 us (28%)
  waiting for transfers between devices  61.6 us (22%)
  local copies, waits for them, and re-layouts  13.1 us (5%)
  other arithmetic  3.83 us (1%)
    all_to_all x5, starting transfers between devices, exchanged(): return lax.all_to_all(blocks, axis, 0, 0, tiled=True)  78 us
    all_to_all x5, waiting for transfers between devices, exchanged(): return lax.all_to_all(blocks, axis, 0, 0, tiled=True)  45.5 us
    ppermute x14, starting transfers between devices, turned(): lax.ppermute(shard, axis, [(i, (i + by) % devices) for i in range(devices)])  20.9 us
    pallas_call x2, Pallas kernels, listed_rows(): pl.pallas_call(lists_kernel, out_shape=jax.ShapeDtypeStruct((dests, ROOM,...  18.2 us
    ppermute x7, starting transfers between devices, swapped(): return lax.ppermute(shard, axis, [(0, 1), (1, 0)])  18 us
    pallas_call x1, Pallas kernels, encoded(): pl.pallas_call(encode_kernel, out_shape=jax.ShapeDtypeStruct(slab.shape,...  16.7 us
    pallas_call x1, Pallas kernels, scored(): pl.pallas_call(score_kernel, grid=(2 * half,), out_shape=(jax.ShapeDtypeS...  16.4 us
    ppermute x14, waiting for transfers between devices, turned(): lax.ppermute(shard, axis, [(i, (i + by) % devices) for i in range(devices)])  15.3 us
  transfers between devices with their start and end apart: 26, of which 9 were waited for; matrix products, arithmetic and copies ran while one was open for 4% of the time, Pallas kernels for 28%

profile of v2, /device:TPU:1, one launch (start us, length us, event | category | flops | bytes accessed | tf_op | source)
XLA Modules:
  0.0 278.2 jit_solution(12824864346048239179)
XLA Ops:
  0.6 7.8 %collective-permute-start = (s32[16,128]{1,0:T(8,128)}, s32[16,128]{1,0:T(8,128)S(1)}, u32[]{:S(2)}, u32[]{:S(2)}) collective-permute-start(s32[16,128]{1,0:T(8,128)} %bitcast.51), channel_id=1, source_target_pairs={{0,128},{128,0},{1,129},{129,1},{2,130},{130,2},{3,131},{131,3},{4... | collective-permute-start | bytes 24584 | tf_op jit(solution)/shard_map/ppermute | solution.py:516
  8.5 0.9 constant_dynamic-slice_fusion
  9.4 0.6 gather_fusion
  10.0 0.8 fusion
  10.8 0.9 broadcast_in_dim.42
  11.7 5.7 %all-to-all-start.2 = ((bf16[16,48,384]{2,1,0:T(8,128)(2,1)}), bf16[16,48,384]{2,1,0:T(8,128)(2,1)S(1)}, u32[]{:S(2)}, u32[]{:S(2)}) async-start(bf16[16,48,384]{2,1,0:T(8,128)(2,1)} %broadcast_in_dim.42), calls=%async_computation.2 | async-start | bytes 1179648 | tf_op jit(solution)/shard_map/all_to_all | solution.py:507
  17.4 0.6 gather_fusion.1
  18.1 0.6 gather_fusion.2
  18.8 1.3 collective-permute-start.1
  20.0 2.5 collective-permute-start.2
  22.5 1.2 collective-permute-start.3
  23.7 0.7 collective-permute-done.2.refs_2_
  24.4 1.0 collective-permute-done.3.refs_3_
  25.5 9.1 %shard_map.95 = bf16[16,48,768]{2,1,0:T(8,128)(2,1)} custom-call(s32[2]{0:T(128)S(1)} %pad_add_fusion.4.info_ref, s32[32,128]{1,0:T(8,128)S(1)} %pad_add_fusion.3.refs_0_, s32[32,128]{1,0:T(8,128)S(1)} %collective-permute-done.1.refs_1_, s32[32,128]{1,0:T(8,128)S(1)} %collective-permute-done.2.refs_2_, s32[32,128]{1,0:T(8,128)S(1)} %collective-permute-done.3.refs_3_, ...), custom_call_target="tpu_custom_call" | custom-call | tf_op jit(solution)/shard_map/pallas_call | solution.py:105
  34.6 6.9 %all-to-all-start.3 = ((bf16[16,48,768]{2,1,0:T(8,128)(2,1)}), bf16[16,48,768]{2,1,0:T(8,128)(2,1)S(1)}, u32[]{:S(2)}, u32[]{:S(2)}) async-start(bf16[16,48,768]{2,1,0:T(8,128)(2,1)} %shard_map.95), calls=%async_computation.3 | async-start | bytes 2359296 | tf_op jit(solution)/shard_map/all_to_all | solution.py:507
  41.5 0.4 collective-permute-start.4
  41.8 2.4 collective-permute-start.5
  44.2 1.4 collective-permute-start.6
  45.6 2.1 collective-permute-start.7
  47.7 1.2 collective-permute-start.8
  48.8 6.3 %shard_map.96 = (bf16[768,2048]{1,0:T(8,128)(2,1)S(1)}, f32[8,128]{1,0:T(8,128)S(1)}) custom-call(s32[2]{0:T(128)S(1)} %broadcast.308.info_ref, s32[1,2048]{1,0:T(1,128)S(1)} %bitcast.44), custom_call_target="tpu_custom_call" | custom-call | tf_op jit(solution)/shard_map/pallas_call | solution.py:411
  55.1 1.6 copy-done.1
  56.8 3.9 %shard_map.98.counts_ref = f32[128,128]{1,0:T(8,128)S(1)} custom-call(s32[1]{0:T(128)} %bitcast.20.info_ref, s32[16,16,128]{2,1,0:T(8,128)} %bitcast.48), custom_call_target="tpu_custom_call" | custom-call | tf_op jit(solution)/shard_map/pallas_call | solution.py:468
  60.7 2.1 shard_map.97.places_ref
  62.8 5.0 %collective-permute-start.11 = (bf16[768,384]{1,0:T(8,128)(2,1)S(1)}, bf16[768,384]{1,0:T(8,128)(2,1)}, u32[]{:S(2)}, u32[]{:S(2)}) collective-permute-start(bf16[768,384]{1,0:T(8,128)(2,1)S(1)} %bitcast.42), channel_id=1, source_target_pairs={{0,16},{16,0},{1,17},{17,1},{2,18},{18,2},{3,19},{19,3},{4,20},{20... | collective-permute-start | bytes 1769480 | tf_op jit(solution)/shard_map/ppermute | solution.py:516
  67.8 1.0 slice.27
  68.9 1.0 slice.28
  69.9 2.9 %collective-permute-start.10 = (bf16[384,384]{1,0:T(8,128)(2,1)S(1)}, bf16[384,384]{1,0:T(8,128)(2,1)}, u32[]{:S(2)}, u32[]{:S(2)}) collective-permute-start(bf16[384,384]{1,0:T(8,128)(2,1)S(1)} %slice.28), channel_id=1, source_target_pairs={{0,96},{32,0},{64,32},{96,64},{1,97},{33,1},{65,33},{97,65},{2,98}... | collective-permute-start | bytes 884744 | tf_op jit(solution)/shard_map/ppermute | solution.py:521
  72.8 9.4 %collective-permute-done.7.refs_2_ = bf16[48,2048]{1,0:T(8,128)(2,1)} collective-permute-done((bf16[48,2048]{1,0:T(8,128)(2,1)}, bf16[48,2048]{1,0:T(8,128)(2,1)}, u32[]{:S(2)}, u32[]{:S(2)}) %collective-permute-start.7) | collective-permute-done | bytes 196640 | tf_op jit(solution)/shard_map/ppermute | solution.py:521
  82.2 2.5 collective-permute-start.12
  84.7 0.5 collective-permute-start.13
  85.4 2.2 shard_map.99.refs_0_
  87.6 0.4 collective-permute-done.13.refs_7_
  87.9 0.4 collective-permute-done.14.refs_8_
  88.3 1.3 collective-permute-start.16
  89.6 1.5 collective-permute-start.17
  91.1 3.2 %shard_map.100 = (bf16[1024,768]{1,0:T(8,128)(2,1)}, s32[8,128]{1,0:T(8,128)S(1)}) custom-call(bf16[1024,768]{1,0:T(8,128)(2,1)S(1)} %shard_map.97.places_ref, bf16[16,48,768]{2,1,0:T(8,128)(2,1)S(1)} %all-to-all-done.3.got_ref), custom_call_target="tpu_custom_call" | custom-call | tf_op jit(solution)/shard_map/pallas_call | solution.py:177
  94.3 0.5 slice.29
  94.8 53.5 %while.20 = (s32[]{:T(128)}, bf16[1024,768]{1,0:T(8,128)(2,1)}, s32[]{:T(128)}, s32[]{:T(128)}, s32[32,128]{1,0:T(8,128)S(1)}, /*index=5*/s32[32,128]{1,0:T(8,12...) while((s32[]{:T(128)}, bf16[1024,768]{1,0:T(8,128)(2,1)}, ...), condition=%wide.region_1.2_spmd, body=%wide.region_0.1_spmd.sunk | while | flops 786442 | bytes 20840692 | solution.py:598
  95.5 9.1 %body.7 = bf16[16,48,768]{2,1,0:T(8,128)(2,1)} custom-call(s32[2]{0:T(128)S(1)} %pad_add_fusion.11.info_ref, s32[32,128]{1,0:T(8,128)S(1)} %get-tuple-element.347.refs_0_, s32[32,128]{1,0:T(8,128)S(1)} %get-tuple-element.348.refs_1_, s32[32,128]{1,0:T(8,128)S(1)} %get-tuple-element.349.refs_2_, s32[32,128]{1,0:T(8,128)S(1)} %get-tuple-element.350.refs_3_, ...), custom_call_target="tpu_custom_call" | custom-call | tf_op jit(solution)/shard_map/while/body/pallas_call | solution.py:105
  104.6 8.6 %all-to-all-start = ((bf16[16,48,768]{2,1,0:T(8,128)(2,1)}), bf16[16,48,768]{2,1,0:T(8,128)(2,1)S(1)}, u32[]{:S(2)}, u32[]{:S(2)}) async-start(bf16[16,48,768]{2,1,0:T(8,128)(2,1)} %body.7), calls=%async_computation | async-start | bytes 2359296 | tf_op jit(solution)/shard_map/while/body/all_to_all | solution.py:507
  113.4 2.1 body.6.places_ref
  115.4 27.7 %all-to-all-done.got_ref = bf16[16,48,768]{2,1,0:T(8,128)(2,1)S(1)} async-done(((bf16[16,48,768]{2,1,0:T(8,128)(2,1)}), bf16[16,48,768]{2,1,0:T(8,128)(2,1)S(1)}, u32[]{:S(2)}, u32[]{:S(2)}) %all-to-all-start) | async-done | bytes 1179680 | tf_op jit(solution)/shard_map/while/body/all_to_all | solution.py:507
  143.1 2.6 body.8
  145.7 0.8 add.230
  146.5 1.1 copy-done.9
  148.3 16.7 %shard_map.101.mine_ref = bf16[1024,768]{1,0:T(8,128)(2,1)S(1)} custom-call(s32[2]{0:T(128)S(1)} %pad_add_fusion.6.info_ref, bf16[768,384]{1,0:T(8,128)(2,1)S(1)} %bitcast.43, bf16[768,384]{1,0:T(8,128)(2,1)} %collective-permute-done.4.refs_1_, bf16[384,384]{1,0:T(8,128)(2,1)} %collective-permute-done.9.refs_2_, ...), custom_call_target="tpu_custom_call" | custom-call | tf_op jit(solution)/shard_map/pallas_call | solution.py:288
  165.0 2.0 collective-permute-start.18
  167.0 1.0 slice.30
  168.2 1.0 slice.31
  169.2 2.7 collective-permute-start.20
  171.9 3.7 %shard_map.102 = bf16[16,40,768]{2,1,0:T(8,128)(2,1)} custom-call(bf16[768,2048]{1,0:T(8,128)(2,1)S(1)} %copy-done.2, f32[8,128]{1,0:T(8,128)S(1)} %get-tuple-element.136.most_ref, bf16[1024,768]{1,0:T(8,128)(2,1)S(1)} %shard_map.101.mine_ref, bf16[1024,768]{1,0:T(8,128)(2,1)S(1)} %collective-permute-done.18.other_ref), custom_call_target="tpu_custom_call" | custom-call | tf_op jit(solution)/shard_map/pallas_call | solution.py:444
  175.7 4.2 %collective-permute-done.19.refs_2_ = bf16[96,2048]{1,0:T(8,128)(2,1)S(1)} collective-permute-done((bf16[96,2048]{1,0:T(8,128)(2,1)S(1)}, bf16[96,2048]{1,0:T(8,128)(2,1)S(1)}, u32[]{:S(2)}, u32[]{:S(2)}) %collective-permute-start.19) | collective-permute-done | bytes 393248 | tf_op jit(solution)/shard_map/ppermute | solution.py:521
  179.9 4.8 %all-to-all-start.4 = ((bf16[16,40,768]{2,1,0:T(8,128)(2,1)}), bf16[16,40,768]{2,1,0:T(8,128)(2,1)S(1)}, u32[]{:S(2)}, u32[]{:S(2)}) async-start(bf16[16,40,768]{2,1,0:T(8,128)(2,1)} %shard_map.102), calls=%async_computation.4 | async-start | bytes 1966080 | tf_op jit(solution)/shard_map/all_to_all | solution.py:507
  184.9 16.4 %shard_map.103 = (f32[16,8,128]{2,1,0:T(8,128)}, f32[128,768]{1,0:T(8,128)S(1)}) custom-call(s32[7]{0:T(128)S(1)} %stack.63.info_ref, bf16[1024,768]{1,0:T(8,128)(2,1)} %copy-done.5, bf16[1024,768]{1,0:T(8,128)(2,1)} %copy-done.7, s32[16,1,128]{2,1,0:T(1,128)S(1)} %bitcast.45, bf16[192,2048]{1,0:T(8,128)(2,1)S(1)} %copy-done, ...), custom_call_target="tpu_custom_call" | custom-call | tf_op jit(solution)/shard_map/pallas_call | solution.py:359
  201.3 8.9 %all-to-all-done.4.got_ref = bf16[16,40,768]{2,1,0:T(8,128)(2,1)S(1)} async-done(((bf16[16,40,768]{2,1,0:T(8,128)(2,1)}), bf16[16,40,768]{2,1,0:T(8,128)(2,1)S(1)}, u32[]{:S(2)}, u32[]{:S(2)}) %all-to-all-start.4) | async-done | bytes 983072 | tf_op jit(solution)/shard_map/all_to_all | solution.py:507
  210.2 0.9 copy-done.10
  211.2 2.8 %shard_map.104 = (f32[128,768]{1,0:T(8,128)S(1)}, s32[8,128]{1,0:T(8,128)}) custom-call(s32[2]{0:T(128)} %copy-done.4, f32[128,128]{1,0:T(8,128)S(1)} %shard_map.98.counts_ref, bf16[16,40,768]{2,1,0:T(8,128)(2,1)} %copy-done.10), custom_call_target="tpu_custom_call" | custom-call | tf_op jit(solution)/shard_map/pallas_call | solution.py:494
  214.0 1.2 slice.35
  215.2 0.7 while.21
  215.8 52.0 %all-to-all-start.5 = ((f32[16,8,128]{2,1,0:T(8,128)}), f32[16,8,128]{2,1,0:T(8,128)S(1)}, u32[]{:S(2)}, u32[]{:S(2)}) async-start(f32[16,8,128]{2,1,0:T(8,128)} %get-tuple-element.167), calls=%async_computation.5 | async-start | bytes 131072 | tf_op jit(solution)/shard_map/all_to_all | solution.py:507
  267.9 0.9 divide_select_fusion
  268.7 8.9 %all-to-all-done.5 = f32[16,8,128]{2,1,0:T(8,128)S(1)} async-done(((f32[16,8,128]{2,1,0:T(8,128)}), f32[16,8,128]{2,1,0:T(8,128)S(1)}, u32[]{:S(2)}, u32[]{:S(2)}) %all-to-all-start.5) | async-done | bytes 65568 | tf_op jit(solution)/shard_map/all_to_all | solution.py:507
  277.6 0.5 add_subtract_fusion
  (71 shorter events, 1.4 us)
Async XLA Ops:
  0.6 18.1 %copy-start.11 = (s32[2048]{0:T(1024)S(1)}, s32[2048]{0:T(1024)}, u32[]{:S(2)}) copy-start(s32[2048]{0:T(1024)} %param.12) | copy-start | bytes 24580
  0.6 18.1 %collective-permute-start = (s32[16,128]{1,0:T(8,128)}, s32[16,128]{1,0:T(8,128)S(1)}, u32[]{:S(2)}, u32[]{:S(2)}) collective-permute-start(s32[16,128]{1,0:T(8,128)} %bitcast.51), channel_id=1, source_target_pairs={{0,128},{128,0},{1,129},{129,1},{2,130},{130,2},{3,131},{131,3},{4... | collective-permute-start | bytes 24584 | tf_op jit(solution)/shard_map/ppermute | solution.py:516
  11.7 22.8 %all-to-all-start.2 = ((bf16[16,48,384]{2,1,0:T(8,128)(2,1)}), bf16[16,48,384]{2,1,0:T(8,128)(2,1)S(1)}, u32[]{:S(2)}, u32[]{:S(2)}) async-start(bf16[16,48,384]{2,1,0:T(8,128)(2,1)} %broadcast_in_dim.42), calls=%async_computation.2 | async-start | bytes 1179648 | tf_op jit(solution)/shard_map/all_to_all | solution.py:507
  18.8 5.0 %collective-permute-start.1 = (s32[32,128]{1,0:T(8,128)S(1)}, s32[32,128]{1,0:T(8,128)S(1)}, u32[]{:S(2)}, u32[]{:S(2)}) collective-permute-start(s32[32,128]{1,0:T(8,128)S(1)} %pad_add_fusion.3.refs_0_), channel_id=1, source_target_pairs={{0,32},{32,64},{64,96},{96,0},{1,33},{33,65},{65,97},{97,1},{2,34}... | collective-permute-start | bytes 49160 | tf_op jit(solution)/shard_map/ppermute | solution.py:521
  20.0 4.4 %collective-permute-start.2 = (s32[32,128]{1,0:T(8,128)S(1)}, s32[32,128]{1,0:T(8,128)S(1)}, u32[]{:S(2)}, u32[]{:S(2)}) collective-permute-start(s32[32,128]{1,0:T(8,128)S(1)} %pad_add_fusion.3.refs_0_), channel_id=1, source_target_pairs={{0,64},{32,96},{64,0},{96,32},{1,65},{33,97},{65,1},{97,33},{2,66}... | collective-permute-start | bytes 49160 | tf_op jit(solution)/shard_map/ppermute | solution.py:521
  22.5 3.0 %collective-permute-start.3 = (s32[32,128]{1,0:T(8,128)S(1)}, s32[32,128]{1,0:T(8,128)S(1)}, u32[]{:S(2)}, u32[]{:S(2)}) collective-permute-start(s32[32,128]{1,0:T(8,128)S(1)} %pad_add_fusion.3.refs_0_), channel_id=1, source_target_pairs={{0,96},{32,0},{64,32},{96,64},{1,97},{33,1},{65,33},{97,65},{2,98}... | collective-permute-start | bytes 49160 | tf_op jit(solution)/shard_map/ppermute | solution.py:521
  34.6 53.8 %all-to-all-start.3 = ((bf16[16,48,768]{2,1,0:T(8,128)(2,1)}), bf16[16,48,768]{2,1,0:T(8,128)(2,1)S(1)}, u32[]{:S(2)}, u32[]{:S(2)}) async-start(bf16[16,48,768]{2,1,0:T(8,128)(2,1)} %shard_map.95), calls=%async_computation.3 | async-start | bytes 2359296 | tf_op jit(solution)/shard_map/all_to_all | solution.py:507
  41.4 43.9 %copy-start.12 = (f32[768]{0:T(1024)S(1)}, f32[768]{0:T(1024)}, u32[]{:S(2)}) copy-start(f32[768]{0:T(1024)} %param.16) | copy-start | bytes 9220
  41.4 43.8 %copy-start.13 = (f32[768]{0:T(1024)S(1)}, f32[768]{0:T(1024)}, u32[]{:S(2)}) copy-start(f32[768]{0:T(1024)} %param.17) | copy-start | bytes 9220
  41.5 21.3 %collective-permute-start.4 = (bf16[768,384]{1,0:T(8,128)(2,1)S(1)}, bf16[768,384]{1,0:T(8,128)(2,1)}, u32[]{:S(2)}, u32[]{:S(2)}) collective-permute-start(bf16[768,384]{1,0:T(8,128)(2,1)S(1)} %bitcast.40), channel_id=1, source_target_pairs={{0,32},{32,64},{64,96},{96,0},{1,33},{33,65},{65,97},{97,1},{2,34}... | collective-permute-start | bytes 1769480 | tf_op jit(solution)/shard_map/ppermute | solution.py:521
  41.8 26.0 %collective-permute-start.5 = (bf16[768,384]{1,0:T(8,128)(2,1)S(1)}, bf16[768,384]{1,0:T(8,128)(2,1)}, u32[]{:S(2)}, u32[]{:S(2)}) collective-permute-start(bf16[768,384]{1,0:T(8,128)(2,1)S(1)} %bitcast.41), channel_id=1, source_target_pairs={{0,96},{32,0},{64,32},{96,64},{1,97},{33,1},{65,33},{97,65},{2,98}... | collective-permute-start | bytes 1769480 | tf_op jit(solution)/shard_map/ppermute | solution.py:521
  44.2 25.6 %collective-permute-start.6 = (bf16[48,2048]{1,0:T(8,128)(2,1)}, bf16[48,2048]{1,0:T(8,128)(2,1)}, u32[]{:S(2)}, u32[]{:S(2)}) collective-permute-start(bf16[48,2048]{1,0:T(8,128)(2,1)} %refs_0_), channel_id=1, source_target_pairs={{0,1},{1,2},{2,3},{3,0},{4,5},{5,6},{6,7},{7,4},{8,9},{9,10},{10,1... | collective-permute-start | bytes 589832 | tf_op jit(solution)/shard_map/ppermute | solution.py:521
  45.6 36.6 %collective-permute-start.7 = (bf16[48,2048]{1,0:T(8,128)(2,1)}, bf16[48,2048]{1,0:T(8,128)(2,1)}, u32[]{:S(2)}, u32[]{:S(2)}) collective-permute-start(bf16[48,2048]{1,0:T(8,128)(2,1)} %refs_0_), channel_id=1, source_target_pairs={{0,2},{1,3},{2,0},{3,1},{4,6},{5,7},{6,4},{7,5},{8,10},{9,11},{10,... | collective-permute-start | bytes 589832 | tf_op jit(solution)/shard_map/ppermute | solution.py:521
  47.7 37.0 %collective-permute-start.8 = (bf16[48,2048]{1,0:T(8,128)(2,1)}, bf16[48,2048]{1,0:T(8,128)(2,1)}, u32[]{:S(2)}, u32[]{:S(2)}) collective-permute-start(bf16[48,2048]{1,0:T(8,128)(2,1)} %refs_0_), channel_id=1, source_target_pairs={{0,3},{1,0},{2,1},{3,2},{4,7},{5,4},{6,5},{7,6},{8,11},{9,8},{10,9... | collective-permute-start | bytes 589832 | tf_op jit(solution)/shard_map/ppermute | solution.py:521
  48.8 38.7 %copy-start.4 = (s32[2]{0:T(128)}, s32[2]{0:T(128)S(1)}, u32[]{:S(2)}) copy-start(s32[2]{0:T(128)S(1)} %broadcast.308.info_ref) | copy-start | bytes 28
  55.1 1.6 copy-start.1
  62.8 24.8 %collective-permute-start.11 = (bf16[768,384]{1,0:T(8,128)(2,1)S(1)}, bf16[768,384]{1,0:T(8,128)(2,1)}, u32[]{:S(2)}, u32[]{:S(2)}) collective-permute-start(bf16[768,384]{1,0:T(8,128)(2,1)S(1)} %bitcast.42), channel_id=1, source_target_pairs={{0,16},{16,0},{1,17},{17,1},{2,18},{18,2},{3,19},{19,3},{4,20},{20... | collective-permute-start | bytes 1769480 | tf_op jit(solution)/shard_map/ppermute | solution.py:516
  68.8 15.9 %collective-permute-start.9 = (bf16[384,384]{1,0:T(8,128)(2,1)S(1)}, bf16[384,384]{1,0:T(8,128)(2,1)}, u32[]{:S(2)}, u32[]{:S(2)}) collective-permute-start(bf16[384,384]{1,0:T(8,128)(2,1)S(1)} %slice.27), channel_id=1, source_target_pairs={{0,32},{32,64},{64,96},{96,0},{1,33},{33,65},{65,97},{97,1},{2,34}... | collective-permute-start | bytes 884744 | tf_op jit(solution)/shard_map/ppermute | solution.py:521
  69.9 15.3 %collective-permute-start.10 = (bf16[384,384]{1,0:T(8,128)(2,1)S(1)}, bf16[384,384]{1,0:T(8,128)(2,1)}, u32[]{:S(2)}, u32[]{:S(2)}) collective-permute-start(bf16[384,384]{1,0:T(8,128)(2,1)S(1)} %slice.28), channel_id=1, source_target_pairs={{0,96},{32,0},{64,32},{96,64},{1,97},{33,1},{65,33},{97,65},{2,98}... | collective-permute-start | bytes 884744 | tf_op jit(solution)/shard_map/ppermute | solution.py:521
  82.2 6.2 %collective-permute-start.12 = (bf16[768,384]{1,0:T(8,128)(2,1)}, bf16[768,384]{1,0:T(8,128)(2,1)}, u32[]{:S(2)}, u32[]{:S(2)}) collective-permute-start(bf16[768,384]{1,0:T(8,128)(2,1)} %collective-permute-done.4.refs_1_), channel_id=1, source_target_pairs={{0,16},{16,0},{1,17},{17,1},{2,18},{18,2},{3,19},{19,3},{4,20},{20... | collective-permute-start | bytes 1769480 | tf_op jit(solution)/shard_map/ppermute | solution.py:516
  84.7 3.7 %collective-permute-start.15 = (bf16[768,384]{1,0:T(8,128)(2,1)}, bf16[768,384]{1,0:T(8,128)(2,1)}, u32[]{:S(2)}, u32[]{:S(2)}) collective-permute-start(bf16[768,384]{1,0:T(8,128)(2,1)} %collective-permute-done.5.refs_4_), channel_id=1, source_target_pairs={{0,16},{16,0},{1,17},{17,1},{2,18},{18,2},{3,19},{19,3},{4,20},{20... | collective-permute-start | bytes 1769480 | tf_op jit(solution)/shard_map/ppermute | solution.py:516
  84.7 3.2 %collective-permute-start.13 = (bf16[384,384]{1,0:T(8,128)(2,1)}, bf16[384,384]{1,0:T(8,128)(2,1)}, u32[]{:S(2)}, u32[]{:S(2)}) collective-permute-start(bf16[384,384]{1,0:T(8,128)(2,1)} %collective-permute-done.9.refs_2_), channel_id=1, source_target_pairs={{0,16},{16,0},{1,17},{17,1},{2,18},{18,2},{3,19},{19,3},{4,20},{20... | collective-permute-start | bytes 884744 | tf_op jit(solution)/shard_map/ppermute | solution.py:516
  85.2 3.1 %collective-permute-start.14 = (bf16[384,384]{1,0:T(8,128)(2,1)}, bf16[384,384]{1,0:T(8,128)(2,1)}, u32[]{:S(2)}, u32[]{:S(2)}) collective-permute-start(bf16[384,384]{1,0:T(8,128)(2,1)} %collective-permute-done.10.refs_3_), channel_id=1, source_target_pairs={{0,16},{16,0},{1,17},{17,1},{2,18},{18,2},{3,19},{19,3},{4,20},{20... | collective-permute-start | bytes 884744 | tf_op jit(solution)/shard_map/ppermute | solution.py:516
  88.3 76.6 %collective-permute-start.16 = (bf16[192,2048]{1,0:T(8,128)(2,1)}, bf16[192,2048]{1,0:T(8,128)(2,1)}, u32[]{:S(2)}, u32[]{:S(2)}) collective-permute-start(bf16[192,2048]{1,0:T(8,128)(2,1)} %shard_map.99.refs_0_), channel_id=1, source_target_pairs={{0,4},{4,8},{8,12},{12,0},{1,5},{5,9},{9,13},{13,1},{2,6},{6,10},{... | collective-permute-start | bytes 2359304 | tf_op jit(solution)/shard_map/ppermute | solution.py:521
  89.6 75.4 %collective-permute-start.17 = (bf16[192,2048]{1,0:T(8,128)(2,1)}, bf16[192,2048]{1,0:T(8,128)(2,1)}, u32[]{:S(2)}, u32[]{:S(2)}) collective-permute-start(bf16[192,2048]{1,0:T(8,128)(2,1)} %shard_map.99.refs_0_), channel_id=1, source_target_pairs={{0,12},{4,0},{8,4},{12,8},{1,13},{5,1},{9,5},{13,9},{2,14},{6,2},{... | collective-permute-start | bytes 2359304 | tf_op jit(solution)/shard_map/ppermute | solution.py:521
  104.6 38.5 %all-to-all-start = ((bf16[16,48,768]{2,1,0:T(8,128)(2,1)}), bf16[16,48,768]{2,1,0:T(8,128)(2,1)S(1)}, u32[]{:S(2)}, u32[]{:S(2)}) async-start(bf16[16,48,768]{2,1,0:T(8,128)(2,1)} %body.7), calls=%async_computation | async-start | bytes 2359296 | tf_op jit(solution)/shard_map/while/body/all_to_all | solution.py:507
  143.1 2.6 copy-start.8
  146.5 1.2 copy-start.9
  148.3 23.6 %copy-start.2 = (bf16[768,2048]{1,0:T(8,128)(2,1)S(1)}, bf16[768,2048]{1,0:T(8,128)(2,1)}, u32[]{:S(2)}) copy-start(bf16[768,2048]{1,0:T(8,128)(2,1)} %copy-done.1) | copy-start | bytes 9437188
  165.0 10.7 %copy-start.5 = (bf16[1024,768]{1,0:T(8,128)(2,1)}, bf16[1024,768]{1,0:T(8,128)(2,1)S(1)}, u32[]{:S(2)}) copy-start(bf16[1024,768]{1,0:T(8,128)(2,1)S(1)} %shard_map.101.mine_ref) | copy-start | bytes 4718596
  165.0 6.9 %collective-permute-start.18 = (bf16[1024,768]{1,0:T(8,128)(2,1)S(1)}, bf16[1024,768]{1,0:T(8,128)(2,1)S(1)}, u32[]{:S(2)}, u32[]{:S(2)}) collective-permute-start(bf16[1024,768]{1,0:T(8,128)(2,1)S(1)} %shard_map.101.mine_ref), channel_id=1, source_target_pairs={{0,16},{16,0},{1,17},{17,1},{2,18},{18,2},{3,19},{19,3},{4,20},{20... | collective-permute-start | bytes 4718600 | tf_op jit(solution)/shard_map/ppermute | solution.py:516
  168.1 11.8 %collective-permute-start.19 = (bf16[96,2048]{1,0:T(8,128)(2,1)S(1)}, bf16[96,2048]{1,0:T(8,128)(2,1)S(1)}, u32[]{:S(2)}, u32[]{:S(2)}) collective-permute-start(bf16[96,2048]{1,0:T(8,128)(2,1)S(1)} %slice.30), channel_id=1, source_target_pairs={{0,4},{4,8},{8,12},{12,0},{1,5},{5,9},{9,13},{13,1},{2,6},{6,10},{... | collective-permute-start | bytes 1179656 | tf_op jit(solution)/shard_map/ppermute | solution.py:521
  169.2 10.7 %collective-permute-start.20 = (bf16[96,2048]{1,0:T(8,128)(2,1)S(1)}, bf16[96,2048]{1,0:T(8,128)(2,1)S(1)}, u32[]{:S(2)}, u32[]{:S(2)}) collective-permute-start(bf16[96,2048]{1,0:T(8,128)(2,1)S(1)} %slice.31), channel_id=1, source_target_pairs={{0,12},{4,0},{8,4},{12,8},{1,13},{5,1},{9,5},{13,9},{2,14},{6,2},{... | collective-permute-start | bytes 1179656 | tf_op jit(solution)/shard_map/ppermute | solution.py:521
  171.9 3.7 %copy-start.7 = (bf16[1024,768]{1,0:T(8,128)(2,1)}, bf16[1024,768]{1,0:T(8,128)(2,1)S(1)}, u32[]{:S(2)}) copy-start(bf16[1024,768]{1,0:T(8,128)(2,1)S(1)} %collective-permute-done.18.other_ref) | copy-start | bytes 4718596
  175.7 9.3 %copy-start = (bf16[192,2048]{1,0:T(8,128)(2,1)S(1)}, bf16[192,2048]{1,0:T(8,128)(2,1)}, u32[]{:S(2)}) copy-start(bf16[192,2048]{1,0:T(8,128)(2,1)} %shard_map.99.refs_0_) | copy-start | bytes 2359300
  179.9 30.3 %all-to-all-start.4 = ((bf16[16,40,768]{2,1,0:T(8,128)(2,1)}), bf16[16,40,768]{2,1,0:T(8,128)(2,1)S(1)}, u32[]{:S(2)}, u32[]{:S(2)}) async-start(bf16[16,40,768]{2,1,0:T(8,128)(2,1)} %shard_map.102), calls=%async_computation.4 | async-start | bytes 1966080 | tf_op jit(solution)/shard_map/all_to_all | solution.py:507
  210.2 1.0 copy-start.10
  215.8 61.7 %all-to-all-start.5 = ((f32[16,8,128]{2,1,0:T(8,128)}), f32[16,8,128]{2,1,0:T(8,128)S(1)}, u32[]{:S(2)}, u32[]{:S(2)}) async-start(f32[16,8,128]{2,1,0:T(8,128)} %get-tuple-element.167), calls=%async_computation.5 | async-start | bytes 131072 | tf_op jit(solution)/shard_map/all_to_all | solution.py:507

commit v3 on v1

--- a/solution.py
+++ b/solution.py
@@ -575,9 +575,12 @@
     ids = [two] + [turned(two, "x", k) for k in range(1, x_size)]
 
     sent = listed_rows(info_of(fs_rank, zero), ids, embed_table)
-    sent, column, local, shard = lax.optimization_barrier((sent, column, local, centroids_t))
+    first = turned(centroids_t, "zl", 1)
+    sent, column, local, shard, first = lax.optimization_barrier(
+        (sent, column, local, centroids_t, first)
+    )
     w_back, w_ahead = neighbours(column, "x")
-    near = joined([shard] + [turned(shard, "zl", k) for k in range(1, 4)])
+    near = joined([shard, first] + [turned(shard, "zl", k) for k in range(2, 4)])
     places = placed_rows(info_of(fs_rank, zero, vocab), ids, fs_size)
     w_back, w_ahead, chosen, places, counts = lax.optimization_barrier(
         (w_back, w_ahead, chosen, places, counts)

time: 186 us -> 181 us (0.973)
  starting transfers between devices: 68.2 us -> 65.1 us
  waiting for transfers between devices: 34.1 us -> 31 us
    ppermute x14, waiting for transfers between devices: 15.5 us -> 12.4 us  [turned(): lax.ppermute(shard, axis, [(i, (i + by) % devices) for i in range(devices)])]
    all_to_all x4, starting transfers between devices: 30.2 us -> 27.6 us  [exchanged(): return lax.all_to_all(blocks, axis, 0, 0, tiled=True)]
  transfers between devices with their start and end apart: 25 -> 25, of which waited for: 8 -> 8; matrix products, arithmetic and copies ran while one was open for 6% -> 6% of each run, Pallas kernels for 34% -> 35%
where the time goes in v3:
time: 181 us; the launch traced here: 180 us
  Pallas kernels  66.1 us (37%)
  starting transfers between devices  65.1 us (36%)
  waiting for transfers between devices  31 us (17%)
  local copies, waits for them, and re-layouts  12.6 us (7%)
  other arithmetic  2.89 us (2%)
    all_to_all x4, starting transfers between devices, exchanged(): return lax.all_to_all(blocks, axis, 0, 0, tiled=True)  27.6 us
    ppermute x14, starting transfers between devices, turned(): lax.ppermute(shard, axis, [(i, (i + by) % devices) for i in range(devices)])  20.4 us
    all_to_all x4, waiting for transfers between devices, exchanged(): return lax.all_to_all(blocks, axis, 0, 0, tiled=True)  17.8 us
    ppermute x7, starting transfers between devices, swapped(): return lax.ppermute(shard, axis, [(0, 1), (1, 0)])  17.2 us
    pallas_call x1, Pallas kernels, encoded(): pl.pallas_call(encode_kernel, out_shape=jax.ShapeDtypeStruct(slab.shape,...  16.7 us
    pallas_call x1, Pallas kernels, scored(): pl.pallas_call(score_kernel, grid=(2 * half,), out_shape=(jax.ShapeDtypeS...  16.4 us
    ppermute x14, waiting for transfers between devices, turned(): lax.ppermute(shard, axis, [(i, (i + by) % devices) for i in range(devices)])  12.4 us
    pallas_call x1, Pallas kernels, listed_rows(): pl.pallas_call(lists_kernel, out_shape=jax.ShapeDtypeStruct((dests, ROOM,...  9.07 us
  transfers between devices with their start and end apart: 25, of which 8 were waited for; matrix products, arithmetic and copies ran while one was open for 6% of the time, Pallas kernels for 35%

profile of v3, /device:TPU:1, one launch (start us, length us, event | category | flops | bytes accessed | tf_op | source)
XLA Modules:
  0.0 179.9 jit_solution(3584419855223431959)
XLA Ops:
  0.6 7.8 %collective-permute-start = (s32[16,128]{1,0:T(8,128)}, s32[16,128]{1,0:T(8,128)S(1)}, u32[]{:S(2)}, u32[]{:S(2)}) collective-permute-start(s32[16,128]{1,0:T(8,128)} %bitcast.51), channel_id=1, source_target_pairs={{0,128},{128,0},{1,129},{129,1},{2,130},{130,2},{3,131},{131,3},{4... | collective-permute-start | bytes 24584 | tf_op jit(solution)/shard_map/ppermute | solution.py:516
  8.5 0.7 collective-permute-start.4
  9.3 0.9 constant_dynamic-slice_fusion
  10.1 0.6 gather_fusion
  10.8 0.8 fusion
  11.6 0.9 broadcast_in_dim.42
  12.5 6.5 %all-to-all-start.2 = ((bf16[16,48,384]{2,1,0:T(8,128)(2,1)}), bf16[16,48,384]{2,1,0:T(8,128)(2,1)S(1)}, u32[]{:S(2)}, u32[]{:S(2)}) async-start(bf16[16,48,384]{2,1,0:T(8,128)(2,1)} %broadcast_in_dim.42), calls=%async_computation.2 | async-start | bytes 1179648 | tf_op jit(solution)/shard_map/all_to_all | solution.py:507
  19.0 0.6 gather_fusion.1
  19.7 0.6 gather_fusion.2
  20.4 1.3 collective-permute-start.1
  21.7 2.5 %collective-permute-start.2 = (s32[32,128]{1,0:T(8,128)S(1)}, s32[32,128]{1,0:T(8,128)S(1)}, u32[]{:S(2)}, u32[]{:S(2)}) collective-permute-start(s32[32,128]{1,0:T(8,128)S(1)} %pad_add_fusion.3.refs_0_), channel_id=1, source_target_pairs={{0,64},{32,96},{64,0},{96,32},{1,65},{33,97},{65,1},{97,33},{2,66}... | collective-permute-start | bytes 49160 | tf_op jit(solution)/shard_map/ppermute | solution.py:521
  24.1 1.2 collective-permute-start.3
  25.4 0.7 collective-permute-done.2.refs_2_
  26.1 0.9 collective-permute-done.3.refs_3_
  27.0 9.1 %shard_map.95 = bf16[16,48,768]{2,1,0:T(8,128)(2,1)} custom-call(s32[2]{0:T(128)S(1)} %pad_add_fusion.4.info_ref, s32[32,128]{1,0:T(8,128)S(1)} %pad_add_fusion.3.refs_0_, s32[32,128]{1,0:T(8,128)S(1)} %collective-permute-done.1.refs_1_, s32[32,128]{1,0:T(8,128)S(1)} %collective-permute-done.2.refs_2_, s32[32,128]{1,0:T(8,128)S(1)} %collective-permute-done.3.refs_3_, ...), custom_call_target="tpu_custom_call" | custom-call | tf_op jit(solution)/shard_map/pallas_call | solution.py:105
  36.1 0.6 copy-done.11
  36.7 7.0 %all-to-all-start.3 = ((bf16[16,48,768]{2,1,0:T(8,128)(2,1)}), bf16[16,48,768]{2,1,0:T(8,128)(2,1)S(1)}, u32[]{:S(2)}, u32[]{:S(2)}) async-start(bf16[16,48,768]{2,1,0:T(8,128)(2,1)} %shard_map.95), calls=%async_computation.3 | async-start | bytes 2359296 | tf_op jit(solution)/shard_map/all_to_all | solution.py:507
  43.7 0.3 collective-permute-start.5
  44.1 2.4 %collective-permute-start.6 = (bf16[768,384]{1,0:T(8,128)(2,1)S(1)}, bf16[768,384]{1,0:T(8,128)(2,1)}, u32[]{:S(2)}, u32[]{:S(2)}) collective-permute-start(bf16[768,384]{1,0:T(8,128)(2,1)S(1)} %bitcast.41), channel_id=1, source_target_pairs={{0,96},{32,0},{64,32},{96,64},{1,97},{33,1},{65,33},{97,65},{2,98}... | collective-permute-start | bytes 1769480 | tf_op jit(solution)/shard_map/ppermute | solution.py:521
  46.5 2.3 %collective-permute-start.7 = (bf16[48,2048]{1,0:T(8,128)(2,1)}, bf16[48,2048]{1,0:T(8,128)(2,1)}, u32[]{:S(2)}, u32[]{:S(2)}) collective-permute-start(bf16[48,2048]{1,0:T(8,128)(2,1)} %refs_0_), channel_id=1, source_target_pairs={{0,2},{1,3},{2,0},{3,1},{4,6},{5,7},{6,4},{7,5},{8,10},{9,11},{10,... | collective-permute-start | bytes 589832 | tf_op jit(solution)/shard_map/ppermute | solution.py:521
  48.7 1.2 collective-permute-start.8
  49.9 6.2 %shard_map.96 = (bf16[768,2048]{1,0:T(8,128)(2,1)S(1)}, f32[8,128]{1,0:T(8,128)S(1)}) custom-call(s32[2]{0:T(128)S(1)} %broadcast.308.info_ref, s32[1,2048]{1,0:T(1,128)S(1)} %bitcast.44), custom_call_target="tpu_custom_call" | custom-call | tf_op jit(solution)/shard_map/pallas_call | solution.py:411
  56.1 1.6 copy-done.1
  57.7 3.9 %shard_map.98.counts_ref = f32[128,128]{1,0:T(8,128)S(1)} custom-call(s32[1]{0:T(128)} %bitcast.20.info_ref, s32[16,16,128]{2,1,0:T(8,128)} %bitcast.48), custom_call_target="tpu_custom_call" | custom-call | tf_op jit(solution)/shard_map/pallas_call | solution.py:468
  61.7 2.1 %shard_map.97.places_ref = bf16[1024,768]{1,0:T(8,128)(2,1)S(1)} custom-call(s32[3]{0:T(128)S(1)} %pad_add_fusion.5.info_ref, s32[32,128]{1,0:T(8,128)S(1)} %pad_add_fusion.3.refs_0_, s32[32,128]{1,0:T(8,128)S(1)} %collective-permute-done.1.refs_1_, s32[32,128]{1,0:T(8,128)S(1)} %collective-permute-done.2.refs_2_, s32[32,128]{1,0:T(8,128)S(1)} %collective-permute-done.3.refs_3_), custom_call_target="tpu_custom_call" | custom-call | tf_op jit(solution)/shard_map/pallas_call | solution.py:152
  63.7 5.0 %collective-permute-start.11 = (bf16[768,384]{1,0:T(8,128)(2,1)S(1)}, bf16[768,384]{1,0:T(8,128)(2,1)}, u32[]{:S(2)}, u32[]{:S(2)}) collective-permute-start(bf16[768,384]{1,0:T(8,128)(2,1)S(1)} %bitcast.42), channel_id=1, source_target_pairs={{0,16},{16,0},{1,17},{17,1},{2,18},{18,2},{3,19},{19,3},{4,20},{20... | collective-permute-start | bytes 1769480 | tf_op jit(solution)/shard_map/ppermute | solution.py:516
  68.7 1.0 slice.27
  69.7 0.1 collective-permute-start.9
  69.8 1.0 slice.28
  70.8 2.9 %collective-permute-start.10 = (bf16[384,384]{1,0:T(8,128)(2,1)S(1)}, bf16[384,384]{1,0:T(8,128)(2,1)}, u32[]{:S(2)}, u32[]{:S(2)}) collective-permute-start(bf16[384,384]{1,0:T(8,128)(2,1)S(1)} %slice.28), channel_id=1, source_target_pairs={{0,96},{32,0},{64,32},{96,64},{1,97},{33,1},{65,33},{97,65},{2,98}... | collective-permute-start | bytes 884744 | tf_op jit(solution)/shard_map/ppermute | solution.py:521
  73.7 6.5 %collective-permute-done.7.refs_2_ = bf16[48,2048]{1,0:T(8,128)(2,1)} collective-permute-done((bf16[48,2048]{1,0:T(8,128)(2,1)}, bf16[48,2048]{1,0:T(8,128)(2,1)}, u32[]{:S(2)}, u32[]{:S(2)}) %collective-permute-start.7) | collective-permute-done | bytes 196640 | tf_op jit(solution)/shard_map/ppermute | solution.py:521
  80.2 2.5 %collective-permute-start.12 = (bf16[768,384]{1,0:T(8,128)(2,1)}, bf16[768,384]{1,0:T(8,128)(2,1)}, u32[]{:S(2)}, u32[]{:S(2)}) collective-permute-start(bf16[768,384]{1,0:T(8,128)(2,1)} %collective-permute-done.5.refs_1_), channel_id=1, source_target_pairs={{0,16},{16,0},{1,17},{17,1},{2,18},{18,2},{3,19},{19,3},{4,20},{20... | collective-permute-start | bytes 1769480 | tf_op jit(solution)/shard_map/ppermute | solution.py:516
  82.7 0.5 collective-permute-start.13
  83.3 0.1 collective-permute-start.14
  83.4 0.1 pad_add_fusion.6.info_ref
  83.4 2.2 %shard_map.99.refs_0_ = bf16[192,2048]{1,0:T(8,128)(2,1)} custom-call(bf16[48,2048]{1,0:T(8,128)(2,1)} %refs_0_, bf16[48,2048]{1,0:T(8,128)(2,1)} %copy-done.11, bf16[48,2048]{1,0:T(8,128)(2,1)} %collective-permute-done.7.refs_2_, bf16[48,2048]{1,0:T(8,128)(2,1)} %collective-permute-done.8.refs_3_), custom_call_target="tpu_custom_call" | custom-call | tf_op jit(solution)/shard_map/pallas_call | solution.py:198
  85.6 0.3 collective-permute-done.13.refs_7_
  86.0 0.4 collective-permute-done.14.refs_8_
  86.4 1.3 collective-permute-start.16
  87.7 1.5 collective-permute-start.17
  89.2 3.2 %shard_map.100 = (bf16[1024,768]{1,0:T(8,128)(2,1)}, s32[8,128]{1,0:T(8,128)S(1)}) custom-call(bf16[1024,768]{1,0:T(8,128)(2,1)S(1)} %shard_map.97.places_ref, bf16[16,48,768]{2,1,0:T(8,128)(2,1)S(1)} %all-to-all-done.3.got_ref), custom_call_target="tpu_custom_call" | custom-call | tf_op jit(solution)/shard_map/pallas_call | solution.py:177
  92.3 0.5 slice.29
  92.9 0.6 while.20
  93.5 16.7 %shard_map.101.mine_ref = bf16[1024,768]{1,0:T(8,128)(2,1)S(1)} custom-call(s32[2]{0:T(128)S(1)} %pad_add_fusion.6.info_ref, bf16[768,384]{1,0:T(8,128)(2,1)S(1)} %bitcast.43, bf16[768,384]{1,0:T(8,128)(2,1)} %collective-permute-done.5.refs_1_, bf16[384,384]{1,0:T(8,128)(2,1)} %collective-permute-done.9.refs_2_, ...), custom_call_target="tpu_custom_call" | custom-call | tf_op jit(solution)/shard_map/pallas_call | solution.py:288
  110.2 1.2 collective-permute-start.18
  111.4 1.0 slice.30
  112.5 0.1 collective-permute-start.19
  112.6 1.0 slice.31
  113.6 2.7 %collective-permute-start.20 = (bf16[96,2048]{1,0:T(8,128)(2,1)S(1)}, bf16[96,2048]{1,0:T(8,128)(2,1)S(1)}, u32[]{:S(2)}, u32[]{:S(2)}) collective-permute-start(bf16[96,2048]{1,0:T(8,128)(2,1)S(1)} %slice.31), channel_id=1, source_target_pairs={{0,12},{4,0},{8,4},{12,8},{1,13},{5,1},{9,5},{13,9},{2,14},{6,2},{... | collective-permute-start | bytes 1179656 | tf_op jit(solution)/shard_map/ppermute | solution.py:521
  116.3 3.7 %shard_map.102 = bf16[16,40,768]{2,1,0:T(8,128)(2,1)} custom-call(bf16[768,2048]{1,0:T(8,128)(2,1)S(1)} %copy-done.2, f32[8,128]{1,0:T(8,128)S(1)} %get-tuple-element.137.most_ref, bf16[1024,768]{1,0:T(8,128)(2,1)S(1)} %shard_map.101.mine_ref, bf16[1024,768]{1,0:T(8,128)(2,1)S(1)} %collective-permute-done.18.other_ref), custom_call_target="tpu_custom_call" | custom-call | tf_op jit(solution)/shard_map/pallas_call | solution.py:444
  120.1 4.2 %collective-permute-done.19.refs_2_ = bf16[96,2048]{1,0:T(8,128)(2,1)S(1)} collective-permute-done((bf16[96,2048]{1,0:T(8,128)(2,1)S(1)}, bf16[96,2048]{1,0:T(8,128)(2,1)S(1)}, u32[]{:S(2)}, u32[]{:S(2)}) %collective-permute-start.19) | collective-permute-done | bytes 393248 | tf_op jit(solution)/shard_map/ppermute | solution.py:521
  124.3 8.6 %all-to-all-start.4 = ((bf16[16,40,768]{2,1,0:T(8,128)(2,1)}), bf16[16,40,768]{2,1,0:T(8,128)(2,1)S(1)}, u32[]{:S(2)}, u32[]{:S(2)}) async-start(bf16[16,40,768]{2,1,0:T(8,128)(2,1)} %shard_map.102), calls=%async_computation.4 | async-start | bytes 1966080 | tf_op jit(solution)/shard_map/all_to_all | solution.py:507
  132.9 0.1 stack.63.info_ref
  133.0 0.1 slice_reduce_fusion
  133.1 16.4 %shard_map.103 = (f32[16,8,128]{2,1,0:T(8,128)}, f32[128,768]{1,0:T(8,128)S(1)}) custom-call(s32[7]{0:T(128)S(1)} %stack.63.info_ref, bf16[1024,768]{1,0:T(8,128)(2,1)} %copy-done.5, bf16[1024,768]{1,0:T(8,128)(2,1)} %copy-done.7, s32[16,1,128]{2,1,0:T(1,128)S(1)} %bitcast.45, bf16[192,2048]{1,0:T(8,128)(2,1)S(1)} %copy-done, ...), custom_call_target="tpu_custom_call" | custom-call | tf_op jit(solution)/shard_map/pallas_call | solution.py:359
  149.5 8.9 %all-to-all-done.4.got_ref = bf16[16,40,768]{2,1,0:T(8,128)(2,1)S(1)} async-done(((bf16[16,40,768]{2,1,0:T(8,128)(2,1)}), bf16[16,40,768]{2,1,0:T(8,128)(2,1)S(1)}, u32[]{:S(2)}, u32[]{:S(2)}) %all-to-all-start.4) | async-done | bytes 983072 | tf_op jit(solution)/shard_map/all_to_all | solution.py:507
  158.4 0.9 copy-done.10
  159.4 2.8 %shard_map.104 = (f32[128,768]{1,0:T(8,128)S(1)}, s32[8,128]{1,0:T(8,128)}) custom-call(s32[2]{0:T(128)} %copy-done.4, f32[128,128]{1,0:T(8,128)S(1)} %shard_map.98.counts_ref, bf16[16,40,768]{2,1,0:T(8,128)(2,1)} %copy-done.10), custom_call_target="tpu_custom_call" | custom-call | tf_op jit(solution)/shard_map/pallas_call | solution.py:494
  162.2 1.2 slice.35
  163.4 0.7 while.21
  164.0 5.5 %all-to-all-start.5 = ((f32[16,8,128]{2,1,0:T(8,128)}), f32[16,8,128]{2,1,0:T(8,128)S(1)}, u32[]{:S(2)}, u32[]{:S(2)}) async-start(f32[16,8,128]{2,1,0:T(8,128)} %get-tuple-element.169), calls=%async_computation.5 | async-start | bytes 131072 | tf_op jit(solution)/shard_map/all_to_all | solution.py:507
  169.5 0.9 divide_select_fusion
  170.4 8.9 %all-to-all-done.5 = f32[16,8,128]{2,1,0:T(8,128)S(1)} async-done(((f32[16,8,128]{2,1,0:T(8,128)}), f32[16,8,128]{2,1,0:T(8,128)S(1)}, u32[]{:S(2)}, u32[]{:S(2)}) %all-to-all-start.5) | async-done | bytes 65568 | tf_op jit(solution)/shard_map/all_to_all | solution.py:507
  179.3 0.5 add_subtract_fusion
  (61 shorter events, 0.7 us)
Async XLA Ops:
  0.6 19.7 %copy-start.12 = (s32[2048]{0:T(1024)S(1)}, s32[2048]{0:T(1024)}, u32[]{:S(2)}) copy-start(s32[2048]{0:T(1024)} %param.12) | copy-start | bytes 24580
  0.6 19.7 %collective-permute-start = (s32[16,128]{1,0:T(8,128)}, s32[16,128]{1,0:T(8,128)S(1)}, u32[]{:S(2)}, u32[]{:S(2)}) collective-permute-start(s32[16,128]{1,0:T(8,128)} %bitcast.51), channel_id=1, source_target_pairs={{0,128},{128,0},{1,129},{129,1},{2,130},{130,2},{3,131},{131,3},{4... | collective-permute-start | bytes 24584 | tf_op jit(solution)/shard_map/ppermute | solution.py:516
  8.5 27.6 %collective-permute-start.4 = (bf16[48,2048]{1,0:T(8,128)(2,1)}, bf16[48,2048]{1,0:T(8,128)(2,1)S(1)}, u32[]{:S(2)}, u32[]{:S(2)}) collective-permute-start(bf16[48,2048]{1,0:T(8,128)(2,1)} %refs_0_), channel_id=1, source_target_pairs={{0,1},{1,2},{2,3},{3,0},{4,5},{5,6},{6,7},{7,4},{8,9},{9,10},{10,1... | collective-permute-start | bytes 589832 | tf_op jit(solution)/shard_map/ppermute | solution.py:521
  12.5 23.7 %all-to-all-start.2 = ((bf16[16,48,384]{2,1,0:T(8,128)(2,1)}), bf16[16,48,384]{2,1,0:T(8,128)(2,1)S(1)}, u32[]{:S(2)}, u32[]{:S(2)}) async-start(bf16[16,48,384]{2,1,0:T(8,128)(2,1)} %broadcast_in_dim.42), calls=%async_computation.2 | async-start | bytes 1179648 | tf_op jit(solution)/shard_map/all_to_all | solution.py:507
  20.4 5.0 %collective-permute-start.1 = (s32[32,128]{1,0:T(8,128)S(1)}, s32[32,128]{1,0:T(8,128)S(1)}, u32[]{:S(2)}, u32[]{:S(2)}) collective-permute-start(s32[32,128]{1,0:T(8,128)S(1)} %pad_add_fusion.3.refs_0_), channel_id=1, source_target_pairs={{0,32},{32,64},{64,96},{96,0},{1,33},{33,65},{65,97},{97,1},{2,34}... | collective-permute-start | bytes 49160 | tf_op jit(solution)/shard_map/ppermute | solution.py:521
  21.7 4.4 %collective-permute-start.2 = (s32[32,128]{1,0:T(8,128)S(1)}, s32[32,128]{1,0:T(8,128)S(1)}, u32[]{:S(2)}, u32[]{:S(2)}) collective-permute-start(s32[32,128]{1,0:T(8,128)S(1)} %pad_add_fusion.3.refs_0_), channel_id=1, source_target_pairs={{0,64},{32,96},{64,0},{96,32},{1,65},{33,97},{65,1},{97,33},{2,66}... | collective-permute-start | bytes 49160 | tf_op jit(solution)/shard_map/ppermute | solution.py:521
  24.1 2.9 %collective-permute-start.3 = (s32[32,128]{1,0:T(8,128)S(1)}, s32[32,128]{1,0:T(8,128)S(1)}, u32[]{:S(2)}, u32[]{:S(2)}) collective-permute-start(s32[32,128]{1,0:T(8,128)S(1)} %pad_add_fusion.3.refs_0_), channel_id=1, source_target_pairs={{0,96},{32,0},{64,32},{96,64},{1,97},{33,1},{65,33},{97,65},{2,98}... | collective-permute-start | bytes 49160 | tf_op jit(solution)/shard_map/ppermute | solution.py:521
  36.1 0.7 copy-start.11
  36.7 49.7 %all-to-all-start.3 = ((bf16[16,48,768]{2,1,0:T(8,128)(2,1)}), bf16[16,48,768]{2,1,0:T(8,128)(2,1)S(1)}, u32[]{:S(2)}, u32[]{:S(2)}) async-start(bf16[16,48,768]{2,1,0:T(8,128)(2,1)} %shard_map.95), calls=%async_computation.3 | async-start | bytes 2359296 | tf_op jit(solution)/shard_map/all_to_all | solution.py:507
  43.7 39.6 %copy-start.13 = (f32[768]{0:T(1024)S(1)}, f32[768]{0:T(1024)}, u32[]{:S(2)}) copy-start(f32[768]{0:T(1024)} %param.16) | copy-start | bytes 9220
  43.7 39.6 %copy-start.14 = (f32[768]{0:T(1024)S(1)}, f32[768]{0:T(1024)}, u32[]{:S(2)}) copy-start(f32[768]{0:T(1024)} %param.17) | copy-start | bytes 9220
  43.7 25.0 %collective-permute-start.5 = (bf16[768,384]{1,0:T(8,128)(2,1)S(1)}, bf16[768,384]{1,0:T(8,128)(2,1)}, u32[]{:S(2)}, u32[]{:S(2)}) collective-permute-start(bf16[768,384]{1,0:T(8,128)(2,1)S(1)} %bitcast.40), channel_id=1, source_target_pairs={{0,32},{32,64},{64,96},{96,0},{1,33},{33,65},{65,97},{97,1},{2,34}... | collective-permute-start | bytes 1769480 | tf_op jit(solution)/shard_map/ppermute | solution.py:521
  44.1 24.6 %collective-permute-start.6 = (bf16[768,384]{1,0:T(8,128)(2,1)S(1)}, bf16[768,384]{1,0:T(8,128)(2,1)}, u32[]{:S(2)}, u32[]{:S(2)}) collective-permute-start(bf16[768,384]{1,0:T(8,128)(2,1)S(1)} %bitcast.41), channel_id=1, source_target_pairs={{0,96},{32,0},{64,32},{96,64},{1,97},{33,1},{65,33},{97,65},{2,98}... | collective-permute-start | bytes 1769480 | tf_op jit(solution)/shard_map/ppermute | solution.py:521
  46.5 33.7 %collective-permute-start.7 = (bf16[48,2048]{1,0:T(8,128)(2,1)}, bf16[48,2048]{1,0:T(8,128)(2,1)}, u32[]{:S(2)}, u32[]{:S(2)}) collective-permute-start(bf16[48,2048]{1,0:T(8,128)(2,1)} %refs_0_), channel_id=1, source_target_pairs={{0,2},{1,3},{2,0},{3,1},{4,6},{5,7},{6,4},{7,5},{8,10},{9,11},{10,... | collective-permute-start | bytes 589832 | tf_op jit(solution)/shard_map/ppermute | solution.py:521
  48.7 34.0 %collective-permute-start.8 = (bf16[48,2048]{1,0:T(8,128)(2,1)}, bf16[48,2048]{1,0:T(8,128)(2,1)}, u32[]{:S(2)}, u32[]{:S(2)}) collective-permute-start(bf16[48,2048]{1,0:T(8,128)(2,1)} %refs_0_), channel_id=1, source_target_pairs={{0,3},{1,0},{2,1},{3,2},{4,7},{5,4},{6,5},{7,6},{8,11},{9,8},{10,9... | collective-permute-start | bytes 589832 | tf_op jit(solution)/shard_map/ppermute | solution.py:521
  49.9 35.7 %copy-start.4 = (s32[2]{0:T(128)}, s32[2]{0:T(128)S(1)}, u32[]{:S(2)}) copy-start(s32[2]{0:T(128)S(1)} %broadcast.308.info_ref) | copy-start | bytes 28
  56.1 1.6 copy-start.1
  63.7 21.9 %collective-permute-start.11 = (bf16[768,384]{1,0:T(8,128)(2,1)S(1)}, bf16[768,384]{1,0:T(8,128)(2,1)}, u32[]{:S(2)}, u32[]{:S(2)}) collective-permute-start(bf16[768,384]{1,0:T(8,128)(2,1)S(1)} %bitcast.42), channel_id=1, source_target_pairs={{0,16},{16,0},{1,17},{17,1},{2,18},{18,2},{3,19},{19,3},{4,20},{20... | collective-permute-start | bytes 1769480 | tf_op jit(solution)/shard_map/ppermute | solution.py:516
  69.7 13.0 %collective-permute-start.9 = (bf16[384,384]{1,0:T(8,128)(2,1)S(1)}, bf16[384,384]{1,0:T(8,128)(2,1)}, u32[]{:S(2)}, u32[]{:S(2)}) collective-permute-start(bf16[384,384]{1,0:T(8,128)(2,1)S(1)} %slice.27), channel_id=1, source_target_pairs={{0,32},{32,64},{64,96},{96,0},{1,33},{33,65},{65,97},{97,1},{2,34}... | collective-permute-start | bytes 884744 | tf_op jit(solution)/shard_map/ppermute | solution.py:521
  70.8 12.4 %collective-permute-start.10 = (bf16[384,384]{1,0:T(8,128)(2,1)S(1)}, bf16[384,384]{1,0:T(8,128)(2,1)}, u32[]{:S(2)}, u32[]{:S(2)}) collective-permute-start(bf16[384,384]{1,0:T(8,128)(2,1)S(1)} %slice.28), channel_id=1, source_target_pairs={{0,96},{32,0},{64,32},{96,64},{1,97},{33,1},{65,33},{97,65},{2,98}... | collective-permute-start | bytes 884744 | tf_op jit(solution)/shard_map/ppermute | solution.py:521
  80.2 6.2 %collective-permute-start.12 = (bf16[768,384]{1,0:T(8,128)(2,1)}, bf16[768,384]{1,0:T(8,128)(2,1)}, u32[]{:S(2)}, u32[]{:S(2)}) collective-permute-start(bf16[768,384]{1,0:T(8,128)(2,1)} %collective-permute-done.5.refs_1_), channel_id=1, source_target_pairs={{0,16},{16,0},{1,17},{17,1},{2,18},{18,2},{3,19},{19,3},{4,20},{20... | collective-permute-start | bytes 1769480 | tf_op jit(solution)/shard_map/ppermute | solution.py:516
  82.7 3.7 %collective-permute-start.15 = (bf16[768,384]{1,0:T(8,128)(2,1)}, bf16[768,384]{1,0:T(8,128)(2,1)}, u32[]{:S(2)}, u32[]{:S(2)}) collective-permute-start(bf16[768,384]{1,0:T(8,128)(2,1)} %collective-permute-done.6.refs_4_), channel_id=1, source_target_pairs={{0,16},{16,0},{1,17},{17,1},{2,18},{18,2},{3,19},{19,3},{4,20},{20... | collective-permute-start | bytes 1769480 | tf_op jit(solution)/shard_map/ppermute | solution.py:516
  82.7 3.2 %collective-permute-start.13 = (bf16[384,384]{1,0:T(8,128)(2,1)}, bf16[384,384]{1,0:T(8,128)(2,1)}, u32[]{:S(2)}, u32[]{:S(2)}) collective-permute-start(bf16[384,384]{1,0:T(8,128)(2,1)} %collective-permute-done.9.refs_2_), channel_id=1, source_target_pairs={{0,16},{16,0},{1,17},{17,1},{2,18},{18,2},{3,19},{19,3},{4,20},{20... | collective-permute-start | bytes 884744 | tf_op jit(solution)/shard_map/ppermute | solution.py:516
  83.3 3.1 %collective-permute-start.14 = (bf16[384,384]{1,0:T(8,128)(2,1)}, bf16[384,384]{1,0:T(8,128)(2,1)}, u32[]{:S(2)}, u32[]{:S(2)}) collective-permute-start(bf16[384,384]{1,0:T(8,128)(2,1)} %collective-permute-done.10.refs_3_), channel_id=1, source_target_pairs={{0,16},{16,0},{1,17},{17,1},{2,18},{18,2},{3,19},{19,3},{4,20},{20... | collective-permute-start | bytes 884744 | tf_op jit(solution)/shard_map/ppermute | solution.py:516
  86.4 23.8 %collective-permute-start.16 = (bf16[192,2048]{1,0:T(8,128)(2,1)}, bf16[192,2048]{1,0:T(8,128)(2,1)}, u32[]{:S(2)}, u32[]{:S(2)}) collective-permute-start(bf16[192,2048]{1,0:T(8,128)(2,1)} %shard_map.99.refs_0_), channel_id=1, source_target_pairs={{0,4},{4,8},{8,12},{12,0},{1,5},{5,9},{9,13},{13,1},{2,6},{6,10},{... | collective-permute-start | bytes 2359304 | tf_op jit(solution)/shard_map/ppermute | solution.py:521
  87.7 22.5 %collective-permute-start.17 = (bf16[192,2048]{1,0:T(8,128)(2,1)}, bf16[192,2048]{1,0:T(8,128)(2,1)}, u32[]{:S(2)}, u32[]{:S(2)}) collective-permute-start(bf16[192,2048]{1,0:T(8,128)(2,1)} %shard_map.99.refs_0_), channel_id=1, source_target_pairs={{0,12},{4,0},{8,4},{12,8},{1,13},{5,1},{9,5},{13,9},{2,14},{6,2},{... | collective-permute-start | bytes 2359304 | tf_op jit(solution)/shard_map/ppermute | solution.py:521
  93.5 22.8 %copy-start.2 = (bf16[768,2048]{1,0:T(8,128)(2,1)S(1)}, bf16[768,2048]{1,0:T(8,128)(2,1)}, u32[]{:S(2)}) copy-start(bf16[768,2048]{1,0:T(8,128)(2,1)} %copy-done.1) | copy-start | bytes 9437188
  110.2 9.9 %copy-start.5 = (bf16[1024,768]{1,0:T(8,128)(2,1)}, bf16[1024,768]{1,0:T(8,128)(2,1)S(1)}, u32[]{:S(2)}) copy-start(bf16[1024,768]{1,0:T(8,128)(2,1)S(1)} %shard_map.101.mine_ref) | copy-start | bytes 4718596
  110.2 6.1 %collective-permute-start.18 = (bf16[1024,768]{1,0:T(8,128)(2,1)S(1)}, bf16[1024,768]{1,0:T(8,128)(2,1)S(1)}, u32[]{:S(2)}, u32[]{:S(2)}) collective-permute-start(bf16[1024,768]{1,0:T(8,128)(2,1)S(1)} %shard_map.101.mine_ref), channel_id=1, source_target_pairs={{0,16},{16,0},{1,17},{17,1},{2,18},{18,2},{3,19},{19,3},{4,20},{20... | collective-permute-start | bytes 4718600 | tf_op jit(solution)/shard_map/ppermute | solution.py:516
  112.5 11.8 %collective-permute-start.19 = (bf16[96,2048]{1,0:T(8,128)(2,1)S(1)}, bf16[96,2048]{1,0:T(8,128)(2,1)S(1)}, u32[]{:S(2)}, u32[]{:S(2)}) collective-permute-start(bf16[96,2048]{1,0:T(8,128)(2,1)S(1)} %slice.30), channel_id=1, source_target_pairs={{0,4},{4,8},{8,12},{12,0},{1,5},{5,9},{9,13},{13,1},{2,6},{6,10},{... | collective-permute-start | bytes 1179656 | tf_op jit(solution)/shard_map/ppermute | solution.py:521
  113.6 10.7 %collective-permute-start.20 = (bf16[96,2048]{1,0:T(8,128)(2,1)S(1)}, bf16[96,2048]{1,0:T(8,128)(2,1)S(1)}, u32[]{:S(2)}, u32[]{:S(2)}) collective-permute-start(bf16[96,2048]{1,0:T(8,128)(2,1)S(1)} %slice.31), channel_id=1, source_target_pairs={{0,12},{4,0},{8,4},{12,8},{1,13},{5,1},{9,5},{13,9},{2,14},{6,2},{... | collective-permute-start | bytes 1179656 | tf_op jit(solution)/shard_map/ppermute | solution.py:521
  116.3 3.7 %copy-start.7 = (bf16[1024,768]{1,0:T(8,128)(2,1)}, bf16[1024,768]{1,0:T(8,128)(2,1)S(1)}, u32[]{:S(2)}) copy-start(bf16[1024,768]{1,0:T(8,128)(2,1)S(1)} %collective-permute-done.18.other_ref) | copy-start | bytes 4718596
  120.1 13.0 %copy-start = (bf16[192,2048]{1,0:T(8,128)(2,1)S(1)}, bf16[192,2048]{1,0:T(8,128)(2,1)}, u32[]{:S(2)}) copy-start(bf16[192,2048]{1,0:T(8,128)(2,1)} %shard_map.99.refs_0_) | copy-start | bytes 2359300
  124.3 34.1 %all-to-all-start.4 = ((bf16[16,40,768]{2,1,0:T(8,128)(2,1)}), bf16[16,40,768]{2,1,0:T(8,128)(2,1)S(1)}, u32[]{:S(2)}, u32[]{:S(2)}) async-start(bf16[16,40,768]{2,1,0:T(8,128)(2,1)} %shard_map.102), calls=%async_computation.4 | async-start | bytes 1966080 | tf_op jit(solution)/shard_map/all_to_all | solution.py:507
  158.4 0.9 copy-start.10
  164.0 15.3 %all-to-all-start.5 = ((f32[16,8,128]{2,1,0:T(8,128)}), f32[16,8,128]{2,1,0:T(8,128)S(1)}, u32[]{:S(2)}, u32[]{:S(2)}) async-start(f32[16,8,128]{2,1,0:T(8,128)} %get-tuple-element.169), calls=%async_computation.5 | async-start | bytes 131072 | tf_op jit(solution)/shard_map/all_to_all | solution.py:507

commit v4 on v1

--- a/solution.py
+++ b/solution.py
@@ -575,9 +575,12 @@
     ids = [two] + [turned(two, "x", k) for k in range(1, x_size)]
 
     sent = listed_rows(info_of(fs_rank, zero), ids, embed_table)
-    sent, column, local, shard = lax.optimization_barrier((sent, column, local, centroids_t))
+    first, last = turned(centroids_t, "zl", 1), turned(centroids_t, "zl", 3)
+    sent, column, local, shard, first, last = lax.optimization_barrier(
+        (sent, column, local, centroids_t, first, last)
+    )
     w_back, w_ahead = neighbours(column, "x")
-    near = joined([shard] + [turned(shard, "zl", k) for k in range(1, 4)])
+    near = joined([shard, first, turned(shard, "zl", 2), last])
     places = placed_rows(info_of(fs_rank, zero, vocab), ids, fs_size)
     w_back, w_ahead, chosen, places, counts = lax.optimization_barrier(
         (w_back, w_ahead, chosen, places, counts)

time: 186 us -> 177 us (0.952)
  starting transfers between devices: 68.2 us -> 61.2 us
  waiting for transfers between devices: 34.1 us -> 30.8 us
    all_to_all x4, starting transfers between devices: 30.2 us -> 22.8 us  [exchanged(): return lax.all_to_all(blocks, axis, 0, 0, tiled=True)]
    ppermute x14, starting transfers between devices: 20.9 us -> 23.8 us  [turned(): lax.ppermute(shard, axis, [(i, (i + by) % devices) for i in range(devices)])]
    ppermute x7, starting transfers between devices: 17.2 us -> 14.6 us  [swapped(): return lax.ppermute(shard, axis, [(0, 1), (1, 0)])]
    ppermute x14, waiting for transfers between devices: 15.5 us -> 12.9 us  [turned(): lax.ppermute(shard, axis, [(i, (i + by) % devices) for i in range(devices)])]
  transfers between devices with their start and end apart: 25 -> 25, of which waited for: 8 -> 6; matrix products, arithmetic and copies ran while one was open for 6% -> 6% of each run, Pallas kernels for 34% -> 36%
where the time goes in v4:
time: 177 us; the launch traced here: 176 us
  Pallas kernels  66 us (37%)
  starting transfers between devices  61.2 us (35%)
  waiting for transfers between devices  30.8 us (17%)
  local copies, waits for them, and re-layouts  12.6 us (7%)
  other arithmetic  2.89 us (2%)
    ppermute x14, starting transfers between devices, turned(): lax.ppermute(shard, axis, [(i, (i + by) % devices) for i in range(devices)])  23.8 us
    all_to_all x4, starting transfers between devices, exchanged(): return lax.all_to_all(blocks, axis, 0, 0, tiled=True)  22.8 us
    all_to_all x4, waiting for transfers between devices, exchanged(): return lax.all_to_all(blocks, axis, 0, 0, tiled=True)  17.8 us
    pallas_call x1, Pallas kernels, encoded(): pl.pallas_call(encode_kernel, out_shape=jax.ShapeDtypeStruct(slab.shape,...  16.7 us
    pallas_call x1, Pallas kernels, scored(): pl.pallas_call(score_kernel, grid=(2 * half,), out_shape=(jax.ShapeDtypeS...  16.4 us
    ppermute x7, starting transfers between devices, swapped(): return lax.ppermute(shard, axis, [(0, 1), (1, 0)])  14.6 us
    ppermute x14, waiting for transfers between devices, turned(): lax.ppermute(shard, axis, [(i, (i + by) % devices) for i in range(devices)])  12.9 us
    pallas_call x1, Pallas kernels, listed_rows(): pl.pallas_call(lists_kernel, out_shape=jax.ShapeDtypeStruct((dests, ROOM,...  9.06 us
  transfers between devices with their start and end apart: 25, of which 6 were waited for; matrix products, arithmetic and copies ran while one was open for 6% of the time, Pallas kernels for 36%

profile of v4, /device:TPU:1, one launch (start us, length us, event | category | flops | bytes accessed | tf_op | source)
XLA Modules:
  0.0 175.8 jit_solution(14895846587202748215)
XLA Ops:
  0.6 2.5 %collective-permute-start.4 = (bf16[48,2048]{1,0:T(8,128)(2,1)}, bf16[48,2048]{1,0:T(8,128)(2,1)S(1)}, u32[]{:S(2)}, u32[]{:S(2)}) collective-permute-start(bf16[48,2048]{1,0:T(8,128)(2,1)} %refs_0_), channel_id=1, source_target_pairs={{0,1},{1,2},{2,3},{3,0},{4,5},{5,6},{6,7},{7,4},{8,9},{9,10},{10,1... | collective-permute-start | bytes 589832 | tf_op jit(solution)/shard_map/ppermute | solution.py:521
  3.2 2.8 %collective-permute-start.5 = (bf16[48,2048]{1,0:T(8,128)(2,1)}, bf16[48,2048]{1,0:T(8,128)(2,1)S(1)}, u32[]{:S(2)}, u32[]{:S(2)}) collective-permute-start(bf16[48,2048]{1,0:T(8,128)(2,1)} %refs_0_), channel_id=1, source_target_pairs={{0,3},{1,0},{2,1},{3,2},{4,7},{5,4},{6,5},{7,6},{8,11},{9,8},{10,9... | collective-permute-start | bytes 589832 | tf_op jit(solution)/shard_map/ppermute | solution.py:521
  6.0 5.7 %collective-permute-start = (s32[16,128]{1,0:T(8,128)}, s32[16,128]{1,0:T(8,128)S(1)}, u32[]{:S(2)}, u32[]{:S(2)}) collective-permute-start(s32[16,128]{1,0:T(8,128)} %bitcast.51), channel_id=1, source_target_pairs={{0,128},{128,0},{1,129},{129,1},{2,130},{130,2},{3,131},{131,3},{4... | collective-permute-start | bytes 24584 | tf_op jit(solution)/shard_map/ppermute | solution.py:516
  11.8 0.9 constant_dynamic-slice_fusion
  12.6 0.6 gather_fusion
  13.3 0.8 fusion
  14.1 0.9 broadcast_in_dim.42
  15.0 4.3 %all-to-all-start.2 = ((bf16[16,48,384]{2,1,0:T(8,128)(2,1)}), bf16[16,48,384]{2,1,0:T(8,128)(2,1)S(1)}, u32[]{:S(2)}, u32[]{:S(2)}) async-start(bf16[16,48,384]{2,1,0:T(8,128)(2,1)} %broadcast_in_dim.42), calls=%async_computation.2 | async-start | bytes 1179648 | tf_op jit(solution)/shard_map/all_to_all | solution.py:507
  19.3 0.6 gather_fusion.1
  20.0 0.6 gather_fusion.2
  20.5 0.1 subtract_bitcast_fusion
  20.6 1.3 collective-permute-start.1
  21.9 2.5 %collective-permute-start.2 = (s32[32,128]{1,0:T(8,128)S(1)}, s32[32,128]{1,0:T(8,128)S(1)}, u32[]{:S(2)}, u32[]{:S(2)}) collective-permute-start(s32[32,128]{1,0:T(8,128)S(1)} %pad_add_fusion.3.refs_0_), channel_id=1, source_target_pairs={{0,64},{32,96},{64,0},{96,32},{1,65},{33,97},{65,1},{97,33},{2,66}... | collective-permute-start | bytes 49160 | tf_op jit(solution)/shard_map/ppermute | solution.py:521
  24.4 1.2 collective-permute-start.3
  25.6 0.7 collective-permute-done.2.refs_2_
  26.3 0.9 collective-permute-done.3.refs_3_
  27.3 9.1 %shard_map.95 = bf16[16,48,768]{2,1,0:T(8,128)(2,1)} custom-call(s32[2]{0:T(128)S(1)} %pad_add_fusion.4.info_ref, s32[32,128]{1,0:T(8,128)S(1)} %pad_add_fusion.3.refs_0_, s32[32,128]{1,0:T(8,128)S(1)} %collective-permute-done.1.refs_1_, s32[32,128]{1,0:T(8,128)S(1)} %collective-permute-done.2.refs_2_, s32[32,128]{1,0:T(8,128)S(1)} %collective-permute-done.3.refs_3_, ...), custom_call_target="tpu_custom_call" | custom-call | tf_op jit(solution)/shard_map/pallas_call | solution.py:105
  36.4 0.6 copy-done.11
  37.0 0.1 copy-done.12
  37.1 7.0 %all-to-all-start.3 = ((bf16[16,48,768]{2,1,0:T(8,128)(2,1)}), bf16[16,48,768]{2,1,0:T(8,128)(2,1)S(1)}, u32[]{:S(2)}, u32[]{:S(2)}) async-start(bf16[16,48,768]{2,1,0:T(8,128)(2,1)} %shard_map.95), calls=%async_computation.3 | async-start | bytes 2359296 | tf_op jit(solution)/shard_map/all_to_all | solution.py:507
  44.1 0.3 collective-permute-start.6
  44.4 2.4 %collective-permute-start.7 = (bf16[768,384]{1,0:T(8,128)(2,1)S(1)}, bf16[768,384]{1,0:T(8,128)(2,1)}, u32[]{:S(2)}, u32[]{:S(2)}) collective-permute-start(bf16[768,384]{1,0:T(8,128)(2,1)S(1)} %bitcast.41), channel_id=1, source_target_pairs={{0,96},{32,0},{64,32},{96,64},{1,97},{33,1},{65,33},{97,65},{2,98}... | collective-permute-start | bytes 1769480 | tf_op jit(solution)/shard_map/ppermute | solution.py:521
  46.8 2.3 %collective-permute-start.8 = (bf16[48,2048]{1,0:T(8,128)(2,1)}, bf16[48,2048]{1,0:T(8,128)(2,1)}, u32[]{:S(2)}, u32[]{:S(2)}) collective-permute-start(bf16[48,2048]{1,0:T(8,128)(2,1)} %refs_0_), channel_id=1, source_target_pairs={{0,2},{1,3},{2,0},{3,1},{4,6},{5,7},{6,4},{7,5},{8,10},{9,11},{10,... | collective-permute-start | bytes 589832 | tf_op jit(solution)/shard_map/ppermute | solution.py:521
  49.1 6.2 %shard_map.96 = (bf16[768,2048]{1,0:T(8,128)(2,1)S(1)}, f32[8,128]{1,0:T(8,128)S(1)}) custom-call(s32[2]{0:T(128)S(1)} %broadcast.308.info_ref, s32[1,2048]{1,0:T(1,128)S(1)} %bitcast.44), custom_call_target="tpu_custom_call" | custom-call | tf_op jit(solution)/shard_map/pallas_call | solution.py:411
  55.3 1.6 copy-done.1
  56.9 3.9 %shard_map.98.counts_ref = f32[128,128]{1,0:T(8,128)S(1)} custom-call(s32[1]{0:T(128)} %bitcast.20.info_ref, s32[16,16,128]{2,1,0:T(8,128)} %bitcast.48), custom_call_target="tpu_custom_call" | custom-call | tf_op jit(solution)/shard_map/pallas_call | solution.py:468
  60.8 2.1 %shard_map.97.places_ref = bf16[1024,768]{1,0:T(8,128)(2,1)S(1)} custom-call(s32[3]{0:T(128)S(1)} %pad_add_fusion.5.info_ref, s32[32,128]{1,0:T(8,128)S(1)} %pad_add_fusion.3.refs_0_, s32[32,128]{1,0:T(8,128)S(1)} %collective-permute-done.1.refs_1_, s32[32,128]{1,0:T(8,128)S(1)} %collective-permute-done.2.refs_2_, s32[32,128]{1,0:T(8,128)S(1)} %collective-permute-done.3.refs_3_), custom_call_target="tpu_custom_call" | custom-call | tf_op jit(solution)/shard_map/pallas_call | solution.py:152
  62.9 5.0 %collective-permute-start.11 = (bf16[768,384]{1,0:T(8,128)(2,1)S(1)}, bf16[768,384]{1,0:T(8,128)(2,1)}, u32[]{:S(2)}, u32[]{:S(2)}) collective-permute-start(bf16[768,384]{1,0:T(8,128)(2,1)S(1)} %bitcast.42), channel_id=1, source_target_pairs={{0,16},{16,0},{1,17},{17,1},{2,18},{18,2},{3,19},{19,3},{4,20},{20... | collective-permute-start | bytes 1769480 | tf_op jit(solution)/shard_map/ppermute | solution.py:516
  67.9 1.0 slice.27
  68.9 0.1 collective-permute-start.9
  69.0 1.0 slice.28
  70.0 2.9 %collective-permute-start.10 = (bf16[384,384]{1,0:T(8,128)(2,1)S(1)}, bf16[384,384]{1,0:T(8,128)(2,1)}, u32[]{:S(2)}, u32[]{:S(2)}) collective-permute-start(bf16[384,384]{1,0:T(8,128)(2,1)S(1)} %slice.28), channel_id=1, source_target_pairs={{0,96},{32,0},{64,32},{96,64},{1,97},{33,1},{65,33},{97,65},{2,98}... | collective-permute-start | bytes 884744 | tf_op jit(solution)/shard_map/ppermute | solution.py:521
  72.9 0.6 collective-permute-start.12
  73.5 7.0 %collective-permute-done.8.refs_2_ = bf16[48,2048]{1,0:T(8,128)(2,1)} collective-permute-done((bf16[48,2048]{1,0:T(8,128)(2,1)}, bf16[48,2048]{1,0:T(8,128)(2,1)}, u32[]{:S(2)}, u32[]{:S(2)}) %collective-permute-start.8) | collective-permute-done | bytes 196640 | tf_op jit(solution)/shard_map/ppermute | solution.py:521
  80.5 1.5 collective-permute-start.15
  82.0 0.5 collective-permute-start.14
  82.6 0.1 pad_add_fusion.6.info_ref
  82.6 2.2 %shard_map.99.refs_0_ = bf16[192,2048]{1,0:T(8,128)(2,1)} custom-call(bf16[48,2048]{1,0:T(8,128)(2,1)} %refs_0_, bf16[48,2048]{1,0:T(8,128)(2,1)} %copy-done.11, bf16[48,2048]{1,0:T(8,128)(2,1)} %collective-permute-done.8.refs_2_, bf16[48,2048]{1,0:T(8,128)(2,1)} %copy-done.12), custom_call_target="tpu_custom_call" | custom-call | tf_op jit(solution)/shard_map/pallas_call | solution.py:198
  84.9 1.3 collective-permute-start.16
  86.1 1.5 collective-permute-start.17
  87.6 3.2 %shard_map.100 = (bf16[1024,768]{1,0:T(8,128)(2,1)}, s32[8,128]{1,0:T(8,128)S(1)}) custom-call(bf16[1024,768]{1,0:T(8,128)(2,1)S(1)} %shard_map.97.places_ref, bf16[16,48,768]{2,1,0:T(8,128)(2,1)S(1)} %all-to-all-done.3.got_ref), custom_call_target="tpu_custom_call" | custom-call | tf_op jit(solution)/shard_map/pallas_call | solution.py:177
  90.8 0.5 slice.29
  91.3 0.6 while.20
  92.0 16.7 %shard_map.101.mine_ref = bf16[1024,768]{1,0:T(8,128)(2,1)S(1)} custom-call(s32[2]{0:T(128)S(1)} %pad_add_fusion.6.info_ref, bf16[768,384]{1,0:T(8,128)(2,1)S(1)} %bitcast.43, bf16[768,384]{1,0:T(8,128)(2,1)} %collective-permute-done.6.refs_1_, bf16[384,384]{1,0:T(8,128)(2,1)} %collective-permute-done.9.refs_2_, ...), custom_call_target="tpu_custom_call" | custom-call | tf_op jit(solution)/shard_map/pallas_call | solution.py:288
  108.7 1.2 collective-permute-start.18
  109.9 1.0 slice.30
  110.9 0.1 collective-permute-start.19
  111.0 1.0 slice.31
  112.1 2.7 %collective-permute-start.20 = (bf16[96,2048]{1,0:T(8,128)(2,1)S(1)}, bf16[96,2048]{1,0:T(8,128)(2,1)S(1)}, u32[]{:S(2)}, u32[]{:S(2)}) collective-permute-start(bf16[96,2048]{1,0:T(8,128)(2,1)S(1)} %slice.31), channel_id=1, source_target_pairs={{0,12},{4,0},{8,4},{12,8},{1,13},{5,1},{9,5},{13,9},{2,14},{6,2},{... | collective-permute-start | bytes 1179656 | tf_op jit(solution)/shard_map/ppermute | solution.py:521
  114.8 3.7 %shard_map.102 = bf16[16,40,768]{2,1,0:T(8,128)(2,1)} custom-call(bf16[768,2048]{1,0:T(8,128)(2,1)S(1)} %copy-done.2, f32[8,128]{1,0:T(8,128)S(1)} %get-tuple-element.138.most_ref, bf16[1024,768]{1,0:T(8,128)(2,1)S(1)} %shard_map.101.mine_ref, bf16[1024,768]{1,0:T(8,128)(2,1)S(1)} %collective-permute-done.18.other_ref), custom_call_target="tpu_custom_call" | custom-call | tf_op jit(solution)/shard_map/pallas_call | solution.py:444
  118.5 4.2 %collective-permute-done.19.refs_2_ = bf16[96,2048]{1,0:T(8,128)(2,1)S(1)} collective-permute-done((bf16[96,2048]{1,0:T(8,128)(2,1)S(1)}, bf16[96,2048]{1,0:T(8,128)(2,1)S(1)}, u32[]{:S(2)}, u32[]{:S(2)}) %collective-permute-start.19) | collective-permute-done | bytes 393248 | tf_op jit(solution)/shard_map/ppermute | solution.py:521
  122.8 5.4 %all-to-all-start.4 = ((bf16[16,40,768]{2,1,0:T(8,128)(2,1)}), bf16[16,40,768]{2,1,0:T(8,128)(2,1)S(1)}, u32[]{:S(2)}, u32[]{:S(2)}) async-start(bf16[16,40,768]{2,1,0:T(8,128)(2,1)} %shard_map.102), calls=%async_computation.4 | async-start | bytes 1966080 | tf_op jit(solution)/shard_map/all_to_all | solution.py:507
  128.2 0.1 stack.63.info_ref
  128.3 0.1 slice_reduce_fusion
  128.4 16.4 %shard_map.103 = (f32[16,8,128]{2,1,0:T(8,128)}, f32[128,768]{1,0:T(8,128)S(1)}) custom-call(s32[7]{0:T(128)S(1)} %stack.63.info_ref, bf16[1024,768]{1,0:T(8,128)(2,1)} %copy-done.5, bf16[1024,768]{1,0:T(8,128)(2,1)} %copy-done.7, s32[16,1,128]{2,1,0:T(1,128)S(1)} %bitcast.45, bf16[192,2048]{1,0:T(8,128)(2,1)S(1)} %copy-done, ...), custom_call_target="tpu_custom_call" | custom-call | tf_op jit(solution)/shard_map/pallas_call | solution.py:359
  144.8 8.9 %all-to-all-done.4.got_ref = bf16[16,40,768]{2,1,0:T(8,128)(2,1)S(1)} async-done(((bf16[16,40,768]{2,1,0:T(8,128)(2,1)}), bf16[16,40,768]{2,1,0:T(8,128)(2,1)S(1)}, u32[]{:S(2)}, u32[]{:S(2)}) %all-to-all-start.4) | async-done | bytes 983072 | tf_op jit(solution)/shard_map/all_to_all | solution.py:507
  153.7 0.9 copy-done.10
  154.7 2.8 %shard_map.104 = (f32[128,768]{1,0:T(8,128)S(1)}, s32[8,128]{1,0:T(8,128)}) custom-call(s32[2]{0:T(128)} %copy-done.4, f32[128,128]{1,0:T(8,128)S(1)} %shard_map.98.counts_ref, bf16[16,40,768]{2,1,0:T(8,128)(2,1)} %copy-done.10), custom_call_target="tpu_custom_call" | custom-call | tf_op jit(solution)/shard_map/pallas_call | solution.py:494
  157.5 1.2 slice.35
  158.7 0.7 while.21
  159.3 6.1 %all-to-all-start.5 = ((f32[16,8,128]{2,1,0:T(8,128)}), f32[16,8,128]{2,1,0:T(8,128)S(1)}, u32[]{:S(2)}, u32[]{:S(2)}) async-start(f32[16,8,128]{2,1,0:T(8,128)} %get-tuple-element.171), calls=%async_computation.5 | async-start | bytes 131072 | tf_op jit(solution)/shard_map/all_to_all | solution.py:507
  165.5 0.9 divide_select_fusion
  166.3 8.9 %all-to-all-done.5 = f32[16,8,128]{2,1,0:T(8,128)S(1)} async-done(((f32[16,8,128]{2,1,0:T(8,128)}), f32[16,8,128]{2,1,0:T(8,128)S(1)}, u32[]{:S(2)}, u32[]{:S(2)}) %all-to-all-start.5) | async-done | bytes 65568 | tf_op jit(solution)/shard_map/all_to_all | solution.py:507
  175.3 0.5 add_subtract_fusion
  (63 shorter events, 0.7 us)
Async XLA Ops:
  0.6 20.0 %copy-start.13 = (s32[2048]{0:T(1024)S(1)}, s32[2048]{0:T(1024)}, u32[]{:S(2)}) copy-start(s32[2048]{0:T(1024)} %param.12) | copy-start | bytes 24580
  0.6 35.7 %collective-permute-start.4 = (bf16[48,2048]{1,0:T(8,128)(2,1)}, bf16[48,2048]{1,0:T(8,128)(2,1)S(1)}, u32[]{:S(2)}, u32[]{:S(2)}) collective-permute-start(bf16[48,2048]{1,0:T(8,128)(2,1)} %refs_0_), channel_id=1, source_target_pairs={{0,1},{1,2},{2,3},{3,0},{4,5},{5,6},{6,7},{7,4},{8,9},{9,10},{10,1... | collective-permute-start | bytes 589832 | tf_op jit(solution)/shard_map/ppermute | solution.py:521
  3.2 33.2 %collective-permute-start.5 = (bf16[48,2048]{1,0:T(8,128)(2,1)}, bf16[48,2048]{1,0:T(8,128)(2,1)S(1)}, u32[]{:S(2)}, u32[]{:S(2)}) collective-permute-start(bf16[48,2048]{1,0:T(8,128)(2,1)} %refs_0_), channel_id=1, source_target_pairs={{0,3},{1,0},{2,1},{3,2},{4,7},{5,4},{6,5},{7,6},{8,11},{9,8},{10,9... | collective-permute-start | bytes 589832 | tf_op jit(solution)/shard_map/ppermute | solution.py:521
  6.0 14.6 %collective-permute-start = (s32[16,128]{1,0:T(8,128)}, s32[16,128]{1,0:T(8,128)S(1)}, u32[]{:S(2)}, u32[]{:S(2)}) collective-permute-start(s32[16,128]{1,0:T(8,128)} %bitcast.51), channel_id=1, source_target_pairs={{0,128},{128,0},{1,129},{129,1},{2,130},{130,2},{3,131},{131,3},{4... | collective-permute-start | bytes 24584 | tf_op jit(solution)/shard_map/ppermute | solution.py:516
  15.0 21.4 %all-to-all-start.2 = ((bf16[16,48,384]{2,1,0:T(8,128)(2,1)}), bf16[16,48,384]{2,1,0:T(8,128)(2,1)S(1)}, u32[]{:S(2)}, u32[]{:S(2)}) async-start(bf16[16,48,384]{2,1,0:T(8,128)(2,1)} %broadcast_in_dim.42), calls=%async_computation.2 | async-start | bytes 1179648 | tf_op jit(solution)/shard_map/all_to_all | solution.py:507
  20.6 5.0 %collective-permute-start.1 = (s32[32,128]{1,0:T(8,128)S(1)}, s32[32,128]{1,0:T(8,128)S(1)}, u32[]{:S(2)}, u32[]{:S(2)}) collective-permute-start(s32[32,128]{1,0:T(8,128)S(1)} %pad_add_fusion.3.refs_0_), channel_id=1, source_target_pairs={{0,32},{32,64},{64,96},{96,0},{1,33},{33,65},{65,97},{97,1},{2,34}... | collective-permute-start | bytes 49160 | tf_op jit(solution)/shard_map/ppermute | solution.py:521
  21.9 4.4 %collective-permute-start.2 = (s32[32,128]{1,0:T(8,128)S(1)}, s32[32,128]{1,0:T(8,128)S(1)}, u32[]{:S(2)}, u32[]{:S(2)}) collective-permute-start(s32[32,128]{1,0:T(8,128)S(1)} %pad_add_fusion.3.refs_0_), channel_id=1, source_target_pairs={{0,64},{32,96},{64,0},{96,32},{1,65},{33,97},{65,1},{97,33},{2,66}... | collective-permute-start | bytes 49160 | tf_op jit(solution)/shard_map/ppermute | solution.py:521
  24.4 2.9 %collective-permute-start.3 = (s32[32,128]{1,0:T(8,128)S(1)}, s32[32,128]{1,0:T(8,128)S(1)}, u32[]{:S(2)}, u32[]{:S(2)}) collective-permute-start(s32[32,128]{1,0:T(8,128)S(1)} %pad_add_fusion.3.refs_0_), channel_id=1, source_target_pairs={{0,96},{32,0},{64,32},{96,64},{1,97},{33,1},{65,33},{97,65},{2,98}... | collective-permute-start | bytes 49160 | tf_op jit(solution)/shard_map/ppermute | solution.py:521
  36.3 0.7 copy-start.11
  36.3 0.7 copy-start.12
  37.1 47.8 %all-to-all-start.3 = ((bf16[16,48,768]{2,1,0:T(8,128)(2,1)}), bf16[16,48,768]{2,1,0:T(8,128)(2,1)S(1)}, u32[]{:S(2)}, u32[]{:S(2)}) async-start(bf16[16,48,768]{2,1,0:T(8,128)(2,1)} %shard_map.95), calls=%async_computation.3 | async-start | bytes 2359296 | tf_op jit(solution)/shard_map/all_to_all | solution.py:507
  44.0 38.5 %copy-start.14 = (f32[768]{0:T(1024)S(1)}, f32[768]{0:T(1024)}, u32[]{:S(2)}) copy-start(f32[768]{0:T(1024)} %param.16) | copy-start | bytes 9220
  44.1 38.5 %copy-start.15 = (f32[768]{0:T(1024)S(1)}, f32[768]{0:T(1024)}, u32[]{:S(2)}) copy-start(f32[768]{0:T(1024)} %param.17) | copy-start | bytes 9220
  44.1 23.8 %collective-permute-start.6 = (bf16[768,384]{1,0:T(8,128)(2,1)S(1)}, bf16[768,384]{1,0:T(8,128)(2,1)}, u32[]{:S(2)}, u32[]{:S(2)}) collective-permute-start(bf16[768,384]{1,0:T(8,128)(2,1)S(1)} %bitcast.40), channel_id=1, source_target_pairs={{0,32},{32,64},{64,96},{96,0},{1,33},{33,65},{65,97},{97,1},{2,34}... | collective-permute-start | bytes 1769480 | tf_op jit(solution)/shard_map/ppermute | solution.py:521
  44.4 23.5 %collective-permute-start.7 = (bf16[768,384]{1,0:T(8,128)(2,1)S(1)}, bf16[768,384]{1,0:T(8,128)(2,1)}, u32[]{:S(2)}, u32[]{:S(2)}) collective-permute-start(bf16[768,384]{1,0:T(8,128)(2,1)S(1)} %bitcast.41), channel_id=1, source_target_pairs={{0,96},{32,0},{64,32},{96,64},{1,97},{33,1},{65,33},{97,65},{2,98}... | collective-permute-start | bytes 1769480 | tf_op jit(solution)/shard_map/ppermute | solution.py:521
  46.8 33.7 %collective-permute-start.8 = (bf16[48,2048]{1,0:T(8,128)(2,1)}, bf16[48,2048]{1,0:T(8,128)(2,1)}, u32[]{:S(2)}, u32[]{:S(2)}) collective-permute-start(bf16[48,2048]{1,0:T(8,128)(2,1)} %refs_0_), channel_id=1, source_target_pairs={{0,2},{1,3},{2,0},{3,1},{4,6},{5,7},{6,4},{7,5},{8,10},{9,11},{10,... | collective-permute-start | bytes 589832 | tf_op jit(solution)/shard_map/ppermute | solution.py:521
  49.1 35.7 %copy-start.4 = (s32[2]{0:T(128)}, s32[2]{0:T(128)S(1)}, u32[]{:S(2)}) copy-start(s32[2]{0:T(128)S(1)} %broadcast.308.info_ref) | copy-start | bytes 28
  55.3 1.6 copy-start.1
  62.9 21.9 %collective-permute-start.11 = (bf16[768,384]{1,0:T(8,128)(2,1)S(1)}, bf16[768,384]{1,0:T(8,128)(2,1)}, u32[]{:S(2)}, u32[]{:S(2)}) collective-permute-start(bf16[768,384]{1,0:T(8,128)(2,1)S(1)} %bitcast.42), channel_id=1, source_target_pairs={{0,16},{16,0},{1,17},{17,1},{2,18},{18,2},{3,19},{19,3},{4,20},{20... | collective-permute-start | bytes 1769480 | tf_op jit(solution)/shard_map/ppermute | solution.py:516
  68.9 13.2 %collective-permute-start.9 = (bf16[384,384]{1,0:T(8,128)(2,1)S(1)}, bf16[384,384]{1,0:T(8,128)(2,1)}, u32[]{:S(2)}, u32[]{:S(2)}) collective-permute-start(bf16[384,384]{1,0:T(8,128)(2,1)S(1)} %slice.27), channel_id=1, source_target_pairs={{0,32},{32,64},{64,96},{96,0},{1,33},{33,65},{65,97},{97,1},{2,34}... | collective-permute-start | bytes 884744 | tf_op jit(solution)/shard_map/ppermute | solution.py:521
  70.0 12.1 %collective-permute-start.10 = (bf16[384,384]{1,0:T(8,128)(2,1)S(1)}, bf16[384,384]{1,0:T(8,128)(2,1)}, u32[]{:S(2)}, u32[]{:S(2)}) collective-permute-start(bf16[384,384]{1,0:T(8,128)(2,1)S(1)} %slice.28), channel_id=1, source_target_pairs={{0,96},{32,0},{64,32},{96,64},{1,97},{33,1},{65,33},{97,65},{2,98}... | collective-permute-start | bytes 884744 | tf_op jit(solution)/shard_map/ppermute | solution.py:521
  72.9 12.0 %collective-permute-start.12 = (bf16[768,384]{1,0:T(8,128)(2,1)}, bf16[768,384]{1,0:T(8,128)(2,1)}, u32[]{:S(2)}, u32[]{:S(2)}) collective-permute-start(bf16[768,384]{1,0:T(8,128)(2,1)} %collective-permute-done.6.refs_1_), channel_id=1, source_target_pairs={{0,16},{16,0},{1,17},{17,1},{2,18},{18,2},{3,19},{19,3},{4,20},{20... | collective-permute-start | bytes 1769480 | tf_op jit(solution)/shard_map/ppermute | solution.py:516
  80.5 4.4 %collective-permute-start.15 = (bf16[768,384]{1,0:T(8,128)(2,1)}, bf16[768,384]{1,0:T(8,128)(2,1)}, u32[]{:S(2)}, u32[]{:S(2)}) collective-permute-start(bf16[768,384]{1,0:T(8,128)(2,1)} %collective-permute-done.7.refs_4_), channel_id=1, source_target_pairs={{0,16},{16,0},{1,17},{17,1},{2,18},{18,2},{3,19},{19,3},{4,20},{20... | collective-permute-start | bytes 1769480 | tf_op jit(solution)/shard_map/ppermute | solution.py:516
  82.0 2.8 %collective-permute-start.13 = (bf16[384,384]{1,0:T(8,128)(2,1)}, bf16[384,384]{1,0:T(8,128)(2,1)}, u32[]{:S(2)}, u32[]{:S(2)}) collective-permute-start(bf16[384,384]{1,0:T(8,128)(2,1)} %collective-permute-done.9.refs_2_), channel_id=1, source_target_pairs={{0,16},{16,0},{1,17},{17,1},{2,18},{18,2},{3,19},{19,3},{4,20},{20... | collective-permute-start | bytes 884744 | tf_op jit(solution)/shard_map/ppermute | solution.py:516
  82.0 2.8 %collective-permute-start.14 = (bf16[384,384]{1,0:T(8,128)(2,1)}, bf16[384,384]{1,0:T(8,128)(2,1)}, u32[]{:S(2)}, u32[]{:S(2)}) collective-permute-start(bf16[384,384]{1,0:T(8,128)(2,1)} %collective-permute-done.10.refs_3_), channel_id=1, source_target_pairs={{0,16},{16,0},{1,17},{17,1},{2,18},{18,2},{3,19},{19,3},{4,20},{20... | collective-permute-start | bytes 884744 | tf_op jit(solution)/shard_map/ppermute | solution.py:516
  84.9 23.8 %collective-permute-start.16 = (bf16[192,2048]{1,0:T(8,128)(2,1)}, bf16[192,2048]{1,0:T(8,128)(2,1)}, u32[]{:S(2)}, u32[]{:S(2)}) collective-permute-start(bf16[192,2048]{1,0:T(8,128)(2,1)} %shard_map.99.refs_0_), channel_id=1, source_target_pairs={{0,4},{4,8},{8,12},{12,0},{1,5},{5,9},{9,13},{13,1},{2,6},{6,10},{... | collective-permute-start | bytes 2359304 | tf_op jit(solution)/shard_map/ppermute | solution.py:521
  86.1 22.6 %collective-permute-start.17 = (bf16[192,2048]{1,0:T(8,128)(2,1)}, bf16[192,2048]{1,0:T(8,128)(2,1)}, u32[]{:S(2)}, u32[]{:S(2)}) collective-permute-start(bf16[192,2048]{1,0:T(8,128)(2,1)} %shard_map.99.refs_0_), channel_id=1, source_target_pairs={{0,12},{4,0},{8,4},{12,8},{1,13},{5,1},{9,5},{13,9},{2,14},{6,2},{... | collective-permute-start | bytes 2359304 | tf_op jit(solution)/shard_map/ppermute | solution.py:521
  92.0 22.8 %copy-start.2 = (bf16[768,2048]{1,0:T(8,128)(2,1)S(1)}, bf16[768,2048]{1,0:T(8,128)(2,1)}, u32[]{:S(2)}) copy-start(bf16[768,2048]{1,0:T(8,128)(2,1)} %copy-done.1) | copy-start | bytes 9437188
  108.6 9.9 %copy-start.5 = (bf16[1024,768]{1,0:T(8,128)(2,1)}, bf16[1024,768]{1,0:T(8,128)(2,1)S(1)}, u32[]{:S(2)}) copy-start(bf16[1024,768]{1,0:T(8,128)(2,1)S(1)} %shard_map.101.mine_ref) | copy-start | bytes 4718596
  108.7 6.1 %collective-permute-start.18 = (bf16[1024,768]{1,0:T(8,128)(2,1)S(1)}, bf16[1024,768]{1,0:T(8,128)(2,1)S(1)}, u32[]{:S(2)}, u32[]{:S(2)}) collective-permute-start(bf16[1024,768]{1,0:T(8,128)(2,1)S(1)} %shard_map.101.mine_ref), channel_id=1, source_target_pairs={{0,16},{16,0},{1,17},{17,1},{2,18},{18,2},{3,19},{19,3},{4,20},{20... | collective-permute-start | bytes 4718600 | tf_op jit(solution)/shard_map/ppermute | solution.py:516
  110.9 11.8 %collective-permute-start.19 = (bf16[96,2048]{1,0:T(8,128)(2,1)S(1)}, bf16[96,2048]{1,0:T(8,128)(2,1)S(1)}, u32[]{:S(2)}, u32[]{:S(2)}) collective-permute-start(bf16[96,2048]{1,0:T(8,128)(2,1)S(1)} %slice.30), channel_id=1, source_target_pairs={{0,4},{4,8},{8,12},{12,0},{1,5},{5,9},{9,13},{13,1},{2,6},{6,10},{... | collective-permute-start | bytes 1179656 | tf_op jit(solution)/shard_map/ppermute | solution.py:521
  112.1 10.7 %collective-permute-start.20 = (bf16[96,2048]{1,0:T(8,128)(2,1)S(1)}, bf16[96,2048]{1,0:T(8,128)(2,1)S(1)}, u32[]{:S(2)}, u32[]{:S(2)}) collective-permute-start(bf16[96,2048]{1,0:T(8,128)(2,1)S(1)} %slice.31), channel_id=1, source_target_pairs={{0,12},{4,0},{8,4},{12,8},{1,13},{5,1},{9,5},{13,9},{2,14},{6,2},{... | collective-permute-start | bytes 1179656 | tf_op jit(solution)/shard_map/ppermute | solution.py:521
  114.8 3.7 %copy-start.7 = (bf16[1024,768]{1,0:T(8,128)(2,1)}, bf16[1024,768]{1,0:T(8,128)(2,1)S(1)}, u32[]{:S(2)}) copy-start(bf16[1024,768]{1,0:T(8,128)(2,1)S(1)} %collective-permute-done.18.other_ref) | copy-start | bytes 4718596
  118.5 9.9 %copy-start = (bf16[192,2048]{1,0:T(8,128)(2,1)S(1)}, bf16[192,2048]{1,0:T(8,128)(2,1)}, u32[]{:S(2)}) copy-start(bf16[192,2048]{1,0:T(8,128)(2,1)} %shard_map.99.refs_0_) | copy-start | bytes 2359300
  122.8 31.0 %all-to-all-start.4 = ((bf16[16,40,768]{2,1,0:T(8,128)(2,1)}), bf16[16,40,768]{2,1,0:T(8,128)(2,1)S(1)}, u32[]{:S(2)}, u32[]{:S(2)}) async-start(bf16[16,40,768]{2,1,0:T(8,128)(2,1)} %shard_map.102), calls=%async_computation.4 | async-start | bytes 1966080 | tf_op jit(solution)/shard_map/all_to_all | solution.py:507
  153.7 0.9 copy-start.10
  159.3 15.9 %all-to-all-start.5 = ((f32[16,8,128]{2,1,0:T(8,128)}), f32[16,8,128]{2,1,0:T(8,128)S(1)}, u32[]{:S(2)}, u32[]{:S(2)}) async-start(f32[16,8,128]{2,1,0:T(8,128)} %get-tuple-element.171), calls=%async_computation.5 | async-start | bytes 131072 | tf_op jit(solution)/shard_map/all_to_all | solution.py:507
